TPU v7x, 512 devices: a whole 4x4x16 slice. The times are simulated.
512 devices in a mesh: grp: 16 (over z_lo, core), seq: 32 (over x, z_hi, y).
Axes of the slice: x: 4, y: 4, z: 16 (z_hi: 2, z_lo: 8; z = z_hi * 8 + z_lo), core: 2. Of those that a mesh axis runs over, the one named last changes fastest.
Arguments:
- queries: bfloat16 [65536, 3072], P(('grp', 'seq')), may hold values from -6 to 6, as said below
- key_states: bfloat16 [65536, 3072], P(('grp', 'seq')), may hold values from -6 to 6
- value_states: bfloat16 [65536, 3072], P(('grp', 'seq')), may hold values from -16 to 16
- key_keep: int32 [65536], P(('grp', 'seq')), may hold values 0 or 1
- summary_pos: int32 [16], replicated, may hold values from 0 to 31
Outputs:
- attended: bfloat16 [65536, 3072], P(('grp', 'seq'))
Inputs may be any that keep to these rules, and one draw needn't show every extreme that they name: queries and key_states entries lie within -6 to 6.
All inputs are finite; a program needn't handle non-finite values. No bound on the sum of `key_keep` on one device may be relied on, other than what follows from the above.
Results may differ from a plain program's by a relative error of at most 0.008.
Values may be sent and summed in bfloat16 or wider, within the bound.
No kernel may reach another device: no remote copies, remote signals or barrier semaphores. Data moves between devices by JAX's collectives and lax.ppermute only.
A program may use at most 64 MiB of HBM per device.

v0:
```python
import math

import jax
import jax.numpy as jnp
from jax import lax
from jax.sharding import PartitionSpec as P

HEADS = 24
HEAD_DIM = 128
FIXED_HEADS = 4
STRIDED_HEADS = 4
LOCAL_HEADS = 16
BLOCK = 128
LOOKBACK = 2


NEG = -1e30


def passed_along(block, axis, distance):
    devices = range(lax.axis_size(axis))
    route = [(i - distance, i) for i in devices if i - distance in devices]
    return lax.ppermute(block, axis, route)


def spread(value, axis, source):
    kept = jnp.where(lax.axis_index(axis) == source, value, 0).astype(value.dtype)
    return lax.psum(kept, axis)


def partial_softmax(query_heads, key_rows, value_rows, allowed):
    scores = jnp.einsum(
        "qhd,khd->hqk", query_heads, key_rows, preferred_element_type=jnp.float32
    ) / math.sqrt(HEAD_DIM)
    scores = jnp.where(allowed[None], scores, NEG)
    row_max = jnp.max(scores, axis=2)
    weights = jnp.where(allowed[None], jnp.exp(scores - row_max[:, :, None]), 0.0)
    row_sum = jnp.sum(weights, axis=2)
    weighted = jnp.einsum(
        "hqk,khd->hqd", weights.astype(jnp.bfloat16), value_rows, preferred_element_type=jnp.float32
    )
    return (row_max, row_sum, weighted)


def merge_state(left_part, right_part):
    row_max = jnp.maximum(left_part[0], right_part[0])
    left_scale = jnp.exp(left_part[0] - row_max)
    right_scale = jnp.exp(right_part[0] - row_max)
    row_sum = left_part[1] * left_scale + right_part[1] * right_scale
    weighted = left_part[2] * left_scale[:, :, None] + right_part[2] * right_scale[:, :, None]
    return (row_max, row_sum, weighted)


def blank_state(count):
    return (
        jnp.full((count, BLOCK), NEG, jnp.float32),
        jnp.zeros((count, BLOCK), jnp.float32),
        jnp.zeros((count, BLOCK, HEAD_DIM), jnp.float32),
    )


def head_range(state, head_lo, head_hi):
    return tuple((member[head_lo:head_hi] for member in state))


def on_device(queries, key_states, value_states, key_keep, summary_pos):
    stride = lax.axis_size("seq")
    groups = lax.axis_size("grp")
    column = lax.axis_index("seq")
    window = lax.axis_index("grp")
    block_id = window * stride + column
    lane_ids = jnp.arange(BLOCK, dtype=jnp.int32)
    group_ids = jnp.arange(groups, dtype=jnp.int32)
    query_heads = queries.reshape(BLOCK, HEADS, HEAD_DIM)
    keep_flag = key_keep.astype(jnp.bfloat16)
    own_block = (key_states, value_states, keep_flag)

    def all_heads(block_rows, allowed):
        return partial_softmax(
            query_heads,
            block_rows[0].reshape(BLOCK, HEADS, HEAD_DIM),
            block_rows[1].reshape(BLOCK, HEADS, HEAD_DIM),
            allowed,
        )

    diagonal = lane_ids[:, None] == lane_ids[None, :]
    causal = (lane_ids[None, :] <= lane_ids[:, None]) & ((key_keep[None, :] == 1) | diagonal)
    near_state = all_heads(own_block, causal)
    prior_one = passed_along((own_block[0], own_block[1], own_block[2]), ("grp", "seq"), 1)
    prior_two = passed_along((own_block[0], own_block[1], own_block[2]), ("grp", "seq"), 2)
    for earlier in (prior_one, prior_two):
        allowed = jnp.broadcast_to((earlier[2] > 0)[None, :], (BLOCK, BLOCK))
        near_state = merge_state(near_state, all_heads(earlier, allowed))
    fixed_lo = LOCAL_HEADS * HEAD_DIM
    fixed_hi = (LOCAL_HEADS + FIXED_HEADS) * HEAD_DIM
    root_dev = summary_pos[window]
    summary_own = (key_states[:, fixed_lo:fixed_hi], value_states[:, fixed_lo:fixed_hi], keep_flag)
    summary_here = (
        spread(summary_own[0], "seq", root_dev),
        spread(summary_own[1], "seq", root_dev),
        spread(summary_own[2], "seq", root_dev),
    )
    fixed_queries = query_heads[:, LOCAL_HEADS : LOCAL_HEADS + FIXED_HEADS]
    shard_rows = (
        lax.all_gather(summary_here[0], "grp", axis=0, tiled=True),
        lax.all_gather(summary_here[1], "grp", axis=0, tiled=True),
        lax.all_gather(summary_here[2], "grp", axis=0, tiled=True),
    )
    row_count = shard_rows[0].shape[0]
    row_window = jnp.arange(row_count, dtype=jnp.int32) // BLOCK
    hit_mask = row_window[:, None] == group_ids[None, :]
    row_summary = jnp.sum(jnp.where(hit_mask, summary_pos[None, :], 0), axis=1)
    usable = (row_window * stride + row_summary < block_id - LOOKBACK) & (shard_rows[2] > 0)
    allowed = jnp.broadcast_to(usable[None, :], (BLOCK, row_count))
    term = partial_softmax(
        fixed_queries,
        shard_rows[0].reshape(row_count, FIXED_HEADS, HEAD_DIM),
        shard_rows[1].reshape(row_count, FIXED_HEADS, HEAD_DIM),
        allowed,
    )
    fixed_state = merge_state(blank_state(FIXED_HEADS), term)
    column_own = (key_states[:, fixed_hi:], value_states[:, fixed_hi:], keep_flag)
    strided_queries = query_heads[:, LOCAL_HEADS + FIXED_HEADS :]
    shard_rows = (
        lax.all_gather(column_own[0], "grp", axis=0, tiled=True),
        lax.all_gather(column_own[1], "grp", axis=0, tiled=True),
        lax.all_gather(column_own[2], "grp", axis=0, tiled=True),
    )
    row_count = shard_rows[0].shape[0]
    row_window = jnp.arange(row_count, dtype=jnp.int32) // BLOCK
    usable = (row_window < window) & (shard_rows[2] > 0)
    allowed = jnp.broadcast_to(usable[None, :], (BLOCK, row_count))
    term = partial_softmax(
        strided_queries,
        shard_rows[0].reshape(row_count, STRIDED_HEADS, HEAD_DIM),
        shard_rows[1].reshape(row_count, STRIDED_HEADS, HEAD_DIM),
        allowed,
    )
    strided_state = merge_state(blank_state(STRIDED_HEADS), term)
    local_total = head_range(near_state, 0, LOCAL_HEADS)
    fixed_total = merge_state(
        head_range(near_state, LOCAL_HEADS, LOCAL_HEADS + FIXED_HEADS), fixed_state
    )
    strided_total = merge_state(
        head_range(near_state, LOCAL_HEADS + FIXED_HEADS, HEADS), strided_state
    )
    row_sum = jnp.concatenate([local_total[1], fixed_total[1], strided_total[1]], axis=0)
    weighted = jnp.concatenate([local_total[2], fixed_total[2], strided_total[2]], axis=0)
    result = weighted / row_sum[:, :, None]
    return jnp.transpose(result, (1, 0, 2)).reshape(BLOCK, HEADS * HEAD_DIM).astype(jnp.bfloat16)


def solution(mesh):
    return jax.shard_map(
        on_device,
        mesh=mesh,
        in_specs=(
            P(("grp", "seq"), None),
            P(("grp", "seq"), None),
            P(("grp", "seq"), None),
            P(("grp", "seq")),
            P(),
        ),
        out_specs=P(("grp", "seq"), None),
        check_vma=False,
    )
```

profile of v0, /device:TPU:1, one launch (start us, length us, event | category | flops | bytes accessed | tf_op | source)
XLA Modules:
  0.0 1218.3 jit_solution(5872520702400437514)
XLA Ops:
  7.4 2.3 copy.80
  12.6 1.8 slice_select_fusion.1
  17.4 559.2 %all-reduce.3.cloned.1.call-done = (bf16[128,512]{0,1:T(8,128)(2,1)}, bf16[128,512]{0,1:T(8,128)(2,1)}) async-done(((bf16[128,512]{0,1:T(8,128)(2,1)}, bf16[128,512]{0,1:T(8,128)(2,1)}), (bf16[128,512]{0,1:T(8,128)(2,1)}, bf16[128,512]{0,1:T(8,128)(2,1)})) %all-reduce.3.cloned.1.call-update) | async-done | bytes 262160 | tf_op jit(solution)/shard_map/psum | solution.py:28
  576.7 2.1 collective-permute-start.2
  578.8 1.9 collective-permute-start.1
  580.7 1.9 collective-permute-start.5
  582.6 1.9 collective-permute-start.4
  584.6 1.9 collective-permute-start
  586.9 282.3 %psum.21 = bf16[128]{0:T(256)(128)(2,1)S(1)} all-reduce(bf16[128]{0:T(256)(128)(2,1)S(1)} %broadcast_select_fusion), channel_id=1, replica_groups=mesh['grp'=16,'seq'=32] {'seq'}, use_global_device_ids=true, to_apply=%region_4.5 | all-reduce | flops 128 | bytes 512 | tf_op jit(solution)/shard_map/psum | solution.py:28
  869.2 219.4 %all-gather = bf16[16,1,128]{2,1,0:T(2,128)(2,1)S(1)} all-gather(bf16[1,1,128]{2,1,0:T(2,128)(2,1)S(1)} %bitcast.74), channel_id=1, replica_groups=mesh['grp'=16,'seq'=32] {'grp'}, dimensions={0}, use_global_device_ids=true | all-gather | bytes 4352 | tf_op jit(solution)/shard_map/all_gather | solution.py:107
  1088.7 25.1 %all-gather.1 = bf16[16,1,128]{2,1,0:T(2,128)(2,1)S(1)} all-gather(bf16[1,1,128]{2,1,0:T(2,128)(2,1)S(1)} %get-tuple-element.36), channel_id=1, replica_groups=mesh['grp'=16,'seq'=32] {'grp'}, dimensions={0}, use_global_device_ids=true | all-gather | bytes 4352 | tf_op jit(solution)/shard_map/all_gather | solution.py:127
  1115.1 2.1 collective-permute-start.3
  1117.3 16.0 %collective-permute-done.3 = bf16[128]{0:T(256)(128)(2,1)S(1)} collective-permute-done((bf16[128]{0:T(256)(128)(2,1)S(1)}, bf16[128]{0:T(256)(128)(2,1)S(1)}, u32[]{:S(2)}, u32[]{:S(2)}) %collective-permute-start.3) | collective-permute-done | bytes 288 | tf_op jit(solution)/shard_map/ppermute | solution.py:23
  1134.8 2.3 copy.88
  1137.1 1.6 fusion.96
  1139.0 1.6 fusion.94
  1144.0 3.9 copy.101
  1147.9 2.7 fusion.2
  1150.7 2.0 copy-done.3
  1153.8 2.9 bitcast_reduce_fusion
  1156.8 1.6 fusion.5
  1160.4 1.7 fusion.55
  1162.1 43.3 %all-gather.9.cloned.1.call-done = bf16[2048,512]{0,1:T(8,128)(2,1)} async-done(((bf16[128,512]{0,1:T(8,128)(2,1)}), bf16[2048,512]{0,1:T(8,128)(2,1)}) %all-gather.9.cloned.1.call-update) | async-done | bytes 2097168 | tf_op jit(solution)/shard_map/all_gather | solution.py:106
  1205.4 4.0 fusion.56
  (71 shorter events, 16.6 us)
Async XLA Ops:
  7.4 569.2 %all-reduce.3.cloned.1.call-start = ((), (), s32[]{:S(2)}) async-start(), calls=%async_computation.4 | async-start | bytes 524288 | tf_op jit(solution)/shard_map/psum | solution.py:28
  7.4 3.9 copy-start.9
  9.7 574.9 %copy-start.10 = (s32[128]{0:T(128)S(1)}, s32[128]{0:T(128)}, u32[]{:S(2)}) copy-start(s32[128]{0:T(128)} %param.8) | copy-start | bytes 1540
  9.7 576.9 %copy-start.7 = (bf16[128,3072]{1,0:T(8,128)(2,1)S(1)}, bf16[128,3072]{1,0:T(8,128)(2,1)}, u32[]{:S(2)}) copy-start(bf16[128,3072]{1,0:T(8,128)(2,1)} %param.5) | copy-start | bytes 2359300
  12.6 1101.4 %copy-start.8 = (bf16[128,3072]{1,0:T(8,128)(2,1)S(1)}, bf16[128,3072]{1,0:T(8,128)(2,1)}, u32[]{:S(2)}) copy-start(bf16[128,3072]{1,0:T(8,128)(2,1)} %param.6) | copy-start | bytes 2359300
  15.1 1128.9 %all-gather.13.cloned.1.call-start = ((), (), s32[]{:S(2)}) async-start(), calls=%async_computation.3 | async-start | bytes 2228224 | tf_op jit(solution)/shard_map/all_gather | solution.py:126
  16.7 1131.2 %all-gather.11.cloned.1.call-start = ((), (), s32[]{:S(2)}) async-start(), calls=%async_computation.2 | async-start | bytes 2228224 | tf_op jit(solution)/shard_map/all_gather | solution.py:125
  17.3 1136.5 %all-gather.7.cloned.1.call-start = ((), (), s32[]{:S(2)}) async-start(), calls=%async_computation | async-start | bytes 2228224 | tf_op jit(solution)/shard_map/all_gather | solution.py:105
  576.6 628.8 %all-gather.9.cloned.1.call-start = ((), (), s32[]{:S(2)}) async-start(), calls=%async_computation.1 | async-start | bytes 2228224 | tf_op jit(solution)/shard_map/all_gather | solution.py:106
  576.7 556.6 %collective-permute-start.2 = (bf16[128,3072]{1,0:T(8,128)(2,1)}, bf16[128,3072]{1,0:T(8,128)(2,1)}, u32[]{:S(2)}, u32[]{:S(2)}) collective-permute-start(bf16[128,3072]{1,0:T(8,128)(2,1)} %param.7), channel_id=1, source_target_pairs={{0,1},{1,2},{2,3},{3,4},{4,5},{5,6},{6,7},{7,8},{8,9},{9,10},{10,1... | collective-permute-start | bytes 2359304 | tf_op jit(solution)/shard_map/ppermute | solution.py:23
  578.8 560.2 %collective-permute-start.1 = (bf16[128,3072]{0,1:T(8,128)(2,1)}, bf16[128,3072]{0,1:T(8,128)(2,1)}, u32[]{:S(2)}, u32[]{:S(2)}) collective-permute-start(bf16[128,3072]{0,1:T(8,128)(2,1)} %copy.80), channel_id=1, source_target_pairs={{0,1},{1,2},{2,3},{3,4},{4,5},{5,6},{6,7},{7,8},{8,9},{9,10},{10,1... | collective-permute-start | bytes 2359304 | tf_op jit(solution)/shard_map/ppermute | solution.py:23
  580.7 554.1 %collective-permute-start.5 = (bf16[128,3072]{1,0:T(8,128)(2,1)}, bf16[128,3072]{1,0:T(8,128)(2,1)}, u32[]{:S(2)}, u32[]{:S(2)}) collective-permute-start(bf16[128,3072]{1,0:T(8,128)(2,1)} %param.7), channel_id=1, source_target_pairs={{0,2},{1,3},{2,4},{3,5},{4,6},{5,7},{6,8},{7,9},{8,10},{9,11},{10,... | collective-permute-start | bytes 2359304 | tf_op jit(solution)/shard_map/ppermute | solution.py:23
  582.6 554.4 %collective-permute-start.4 = (bf16[128,3072]{0,1:T(8,128)(2,1)}, bf16[128,3072]{0,1:T(8,128)(2,1)}, u32[]{:S(2)}, u32[]{:S(2)}) collective-permute-start(bf16[128,3072]{0,1:T(8,128)(2,1)} %copy.80), channel_id=1, source_target_pairs={{0,2},{1,3},{2,4},{3,5},{4,6},{5,7},{6,8},{7,9},{8,10},{9,11},{10,... | collective-permute-start | bytes 2359304 | tf_op jit(solution)/shard_map/ppermute | solution.py:23
  584.6 530.5 %collective-permute-start = (bf16[128]{0:T(256)(128)(2,1)S(1)}, bf16[128]{0:T(256)(128)(2,1)S(1)}, u32[]{:S(2)}, u32[]{:S(2)}) collective-permute-start(bf16[128]{0:T(256)(128)(2,1)S(1)} %get-tuple-element.37), channel_id=1, source_target_pairs={{0,1},{1,2},{2,3},{3,4},{4,5},{5,6},{6,7},{7,8},{8,9},{9,10},{10,1... | collective-permute-start | bytes 776 | tf_op jit(solution)/shard_map/ppermute | solution.py:23
  1115.1 18.1 %collective-permute-start.3 = (bf16[128]{0:T(256)(128)(2,1)S(1)}, bf16[128]{0:T(256)(128)(2,1)S(1)}, u32[]{:S(2)}, u32[]{:S(2)}) collective-permute-start(bf16[128]{0:T(256)(128)(2,1)S(1)} %get-tuple-element.37), channel_id=1, source_target_pairs={{0,2},{1,3},{2,4},{3,5},{4,6},{5,7},{6,8},{7,9},{8,10},{9,11},{10,... | collective-permute-start | bytes 776 | tf_op jit(solution)/shard_map/ppermute | solution.py:23
  1141.0 1.1 copy-start.5
  1142.8 1.2 copy-start.1
  1150.6 2.0 copy-start.3
  1153.8 5.1 copy-start.4
  1156.8 2.1 copy-start
  1156.8 2.6 copy-start.2
  1156.8 3.6 copy-start.6
  1205.4 4.0 slice-start
Sparse Core Ops, SparseCore 0:
  15.2 561.3 all-reduce.2
Sparse Core Ops, SparseCore 1:
  17.7 107.5 all-gather.12
  127.1 84.2 all-gather.10
  576.7 299.0 all-gather.6
  1133.3 72.0 all-gather.8
where the time goes:
time: 1220 us
  waiting for transfers between devices  619 us (51%)
  blocking collectives  527 us (43%)
  local copies, waits for them, and re-layouts  21.1 us (2%)
  matrix products  16.4 us (1%)
  between operations  16.2 us (1%)
    psum x1, waiting for transfers between devices, spread(): return lax.psum(kept, axis)  559 us
    psum x1, blocking collectives, spread(): return lax.psum(kept, axis)  282 us
    all_gather x1, blocking collectives, on_device(): lax.all_gather(summary_here[2], 'grp', axis=0, tiled=True)  219 us
    all_gather x1, waiting for transfers between devices, on_device(): lax.all_gather(summary_here[1], 'grp', axis=0, tiled=True)  43.3 us
    all_gather x1, blocking collectives, on_device(): lax.all_gather(column_own[2], 'grp', axis=0, tiled=True)  25.1 us
  transfers between devices with their start and end apart: 11, of which 3 were waited for; matrix products, arithmetic and copies ran while one was open for 2% of the time, Pallas kernels for 0%

commit v1 on v0

v1 whole, which is shorter than its diff:
```python
import math

import jax
import jax.numpy as jnp
from jax import lax
from jax.experimental import pallas as pl
from jax.experimental.pallas import tpu as pltpu
from jax.sharding import Mesh, PartitionSpec as P

HEADS = 24
DIM = 128
BLOCK = 128
LOCAL = 16
ZL, CORES, XS, ZH, YS = 8, 2, 4, 2, 4
AXES = ("zl", "core", "x", "zh", "y")
SIZES = dict(zip(AXES, (ZL, CORES, XS, ZH, YS)))
MINE = HEADS // YS
PER = LOCAL // YS
WIDE = MINE * DIM
FIX, STR = PER, PER + 1
FLAG_ROWS = 16
MARK = 128.0
NEG = -1e30
SCALE = 1.0 / (math.sqrt(DIM) * math.log(2.0))
f32, bf16 = jnp.float32, jnp.bfloat16


def index_of(place):
    at = 0
    for axis in AXES:
        at = at * SIZES[axis] + place[axis]
    return at


def route(move):
    pairs = []
    for zl in range(ZL):
        for core in range(CORES):
            for x in range(XS):
                for zh in range(ZH):
                    for y in range(YS):
                        place = dict(zl=zl, core=core, x=x, zh=zh, y=y)
                        to = move(place)
                        if to is not None:
                            pairs.append((index_of(place), index_of({**place, **to})))
    return pairs


def send(value, move):
    return lax.ppermute(value, AXES, route(move))


def next_group(p):
    if p["zh"] == 0:
        return dict(zh=1)
    if p["x"] < XS - 1:
        return dict(zh=0, x=p["x"] + 1)
    window = p["zl"] * CORES + p["core"] + 1
    if window == ZL * CORES:
        return None
    return dict(zh=0, x=0, zl=window // CORES, core=window % CORES)


def up(distance):
    return lambda p: dict(zl=p["zl"] + distance) if p["zl"] + distance < ZL else None


def other_core(p):
    return dict(core=1 - p["core"])


def head_parts(rows):
    fixed, strided = LOCAL * DIM, (LOCAL + YS) * DIM
    return jnp.stack(
        [
            jnp.concatenate(
                [
                    rows[:, y * PER * DIM : (y + 1) * PER * DIM],
                    rows[:, fixed + y * DIM : fixed + (y + 1) * DIM],
                    rows[:, strided + y * DIM : strided + (y + 1) * DIM],
                ],
                axis=1,
            )
            for y in range(YS)
        ]
    )


def qk(a, b):
    return lax.dot_general(a, b, (((1,), (1,)), ((), ())), preferred_element_type=f32)


def pv(p, v):
    return jnp.dot(p.astype(bf16), v, preferred_element_type=f32)


def attend(info, far_ok, q, kv, halo, fx, s1, s2, e1, e2, out, m_sc, l_sc, a_sc):
    has_prev = info[0]
    core = info[1]
    rows = lax.broadcasted_iota(jnp.int32, (BLOCK, BLOCK), 0)
    cols = lax.broadcasted_iota(jnp.int32, (BLOCK, BLOCK), 1)
    pick = jnp.where(lax.broadcasted_iota(jnp.int32, (16, DIM), 1) == 0, 1.0, 0.0).astype(bf16)

    def own_mask(j):
        keep = kv[j, 2 * BLOCK : 2 * BLOCK + 1, 0:BLOCK].astype(f32) > 0.5
        return keep

    keeps = [own_mask(j) for j in range(YS)]
    halo_keep = []
    for i in range(2):
        flag = qk(pick, halo[i, 0:BLOCK, 0:DIM])[0:1]
        halo_keep.append((flag < MARK / 2) & (has_prev > 0))

    for j in range(YS):
        own_ok = ((cols <= rows) & jnp.broadcast_to(keeps[j], (BLOCK, BLOCK))) | (cols == rows)
        oks = [own_ok]
        for back in (1, 2):
            flag = keeps[j - back] if j >= back else halo_keep[2 + j - back]
            oks.append(jnp.broadcast_to(flag, (BLOCK, BLOCK)))
        for h in range(MINE):
            lo, hi = h * DIM, (h + 1) * DIM
            query = q[j, :, lo:hi]
            scores, values = [], []
            for back in range(3):
                if j >= back:
                    key = kv[j - back, 0:BLOCK, lo:hi]
                    value = kv[j - back, BLOCK : 2 * BLOCK, lo:hi]
                else:
                    key = halo[2 + j - back, 0:BLOCK, lo:hi]
                    value = halo[2 + j - back, BLOCK : 2 * BLOCK, lo:hi]
                scores.append(jnp.where(oks[back], qk(query, key) * SCALE, NEG))
                values.append(value)
            top = jnp.maximum(jnp.maximum(scores[0], scores[1]), scores[2])
            top = jnp.max(top, axis=1, keepdims=True)
            weights = [jnp.exp2(s - top) for s in scores]
            total = jnp.sum(weights[0] + weights[1] + weights[2], axis=1, keepdims=True)
            acc = pv(weights[0], values[0]) + pv(weights[1], values[1]) + pv(weights[2], values[2])
            if h < PER:
                out[j, :, lo:hi] = (acc / total).astype(bf16)
            else:
                m_sc[h - PER, j] = top
                l_sc[h - PER, j] = total
                a_sc[h - PER, j] = acc

    def far(kind, j, parts):
        lo, hi = (PER + kind) * DIM, (PER + kind + 1) * DIM
        query = q[j, :, lo:hi]
        top = m_sc[kind, j]
        scores = []
        for rows_, ok in parts:
            key = rows_[:, 0:DIM]
            flag = qk(pick, key)[0:1]
            allowed = (flag < MARK / 2) & (ok > 0.5)
            s = jnp.where(jnp.broadcast_to(allowed, (BLOCK, key.shape[0])), qk(query, key) * SCALE, NEG)
            scores.append(s)
            top = jnp.maximum(top, jnp.max(s, axis=1, keepdims=True))
        shrink = jnp.exp2(m_sc[kind, j] - top)
        total = l_sc[kind, j] * shrink
        acc = a_sc[kind, j] * shrink
        for s, (rows_, ok) in zip(scores, parts):
            w = jnp.exp2(s - top)
            total = total + jnp.sum(w, axis=1, keepdims=True)
            acc = acc + pv(w, rows_[:, DIM : 2 * DIM])
        out[j, :, lo:hi] = (acc / total).astype(bf16)

    for j in range(YS):
        far(0, j, [(fx[...], far_ok[j : j + 1, :])])
    per = 2 * 4 * BLOCK
    for side, (near_items, far_items) in enumerate(((s1, s2), (e1, e2))):
        column_pair = core if side == 0 else 1 - core
        for jj in range(2):
            j = 2 * column_pair + jj
            parts = []
            for t, items in enumerate((near_items, far_items)):
                rows_ = items[:, :, jj].reshape(per, 2 * DIM)
                parts.append((rows_, far_ok[4 : 5, t * per : (t + 1) * per]))
            far(1, j, parts)


def on_device(queries, key_states, value_states, key_keep, summary_pos):
    zl, core, x, zh, y = (lax.axis_index(a) for a in AXES)
    window = zl * CORES + core
    group = window * (XS * ZH) + x * ZH + zh

    flags = jnp.broadcast_to(key_keep.astype(bf16)[None, None, :], (YS, FLAG_ROWS, BLOCK))
    flags = jnp.pad(flags, ((0, 0), (0, 0), (0, WIDE - BLOCK)))
    packed = jnp.concatenate([head_parts(key_states), head_parts(value_states), flags], axis=1)
    kv = lax.all_to_all(packed, "y", 0, 0)
    q = lax.all_to_all(head_parts(queries), "y", 0, 0)

    keep = kv[:, 2 * BLOCK, :BLOCK] > 0.5
    keys = jnp.where(keep[:, :, None], kv[:, :BLOCK], MARK).astype(bf16)
    vals = kv[:, BLOCK : 2 * BLOCK]
    halo = send(jnp.concatenate([keys[2:], vals[2:]], axis=1), next_group)

    cut = slice(STR * DIM, (STR + 1) * DIM)
    strided = jnp.concatenate([keys[:, :, cut], vals[:, :, cut]], axis=2)
    stay = jnp.where(core == 0, strided[:2], strided[2:])
    leave = jnp.where(core == 0, strided[2:], strided[:2])
    come = send(leave, other_core)
    first = jnp.where(core == 0, jnp.stack([stay, come]), jnp.stack([come, stay]))[None]
    r1 = send(first, up(4))
    two = jnp.concatenate([first, r1])
    r2 = send(two, up(2))
    s1 = jnp.concatenate([two, r2])
    s2 = send(s1, up(1))
    e1 = send(s1, other_core)
    e2 = send(s2, other_core)

    cut = slice(FIX * DIM, (FIX + 1) * DIM)
    fixed = jnp.concatenate([keys[:, :, cut], vals[:, :, cut]], axis=2)
    root = summary_pos[window]
    root_x, root_zh, root_y = root // (ZH * YS), (root // YS) % ZH, root % YS
    block = lax.dynamic_index_in_dim(fixed, root_y, 0, keepdims=False)
    quarters = lax.all_to_all(block.reshape(XS, BLOCK // XS, 2 * DIM), "x", 0, 0)
    piece = lax.dynamic_index_in_dim(quarters, root_x, 0, keepdims=False)
    twin = send(piece, lambda p: dict(zh=1 - p["zh"]))
    piece = jnp.where(zh == root_zh, piece, twin)
    pieces = jnp.broadcast_to(piece[None], (ZL * CORES,) + piece.shape)
    pieces = lax.all_to_all(pieces, ("zl", "core"), 0, 0)
    pieces = jnp.broadcast_to(pieces[None], (XS,) + pieces.shape)
    pieces = lax.all_to_all(pieces, "x", 0, 0)
    fx = pieces.reshape(-1, 2 * DIM)

    windows = jnp.arange(ZL * CORES, dtype=jnp.int32)
    block_ids = group * YS + jnp.arange(YS, dtype=jnp.int32)
    fixed_ok = (windows * (XS * ZH * YS) + summary_pos)[None, :] < block_ids[:, None] - 2
    fixed_ok = jnp.broadcast_to(fixed_ok[:, None, :, None], (YS, XS, ZL * CORES, BLOCK // XS)).reshape(YS, -1)
    chips = zl - jnp.array([0, 4, 2, 6, 1, 5, 3, 7], jnp.int32)
    their = chips[:, None] * CORES + jnp.arange(CORES, dtype=jnp.int32)[None, :]
    strided_ok = (chips[:, None] >= 0) & (their < window)
    strided_ok = jnp.broadcast_to(strided_ok[:, :, None], (ZL, CORES, BLOCK)).reshape(1, -1)
    far_ok = jnp.concatenate([fixed_ok, strided_ok, strided_ok, strided_ok, strided_ok]).astype(f32)
    info = jnp.stack([(group > 0).astype(jnp.int32), core.astype(jnp.int32)])

    vmem = pl.BlockSpec(memory_space=pltpu.VMEM)
    out = pl.pallas_call(
        attend,
        out_shape=jax.ShapeDtypeStruct((YS, BLOCK, WIDE), bf16),
        in_specs=[pl.BlockSpec(memory_space=pltpu.SMEM)] + [vmem] * 9,
        out_specs=vmem,
        scratch_shapes=[
            pltpu.VMEM((2, YS, BLOCK, 1), f32),
            pltpu.VMEM((2, YS, BLOCK, 1), f32),
            pltpu.VMEM((2, YS, BLOCK, DIM), f32),
        ],
        compiler_params=pltpu.CompilerParams(vmem_limit_bytes=48 << 20),
        name="attend",
    )(info, far_ok, q, kv, halo, fx, s1, s2, e1, e2)
    back = lax.all_to_all(out, "y", 0, 0)
    near = [back[i, :, : PER * DIM] for i in range(YS)]
    fixed = [back[i, :, FIX * DIM : STR * DIM] for i in range(YS)]
    strided = [back[i, :, STR * DIM :] for i in range(YS)]
    return jnp.concatenate(near + fixed + strided, axis=1)


def solution(mesh):
    fine = Mesh(mesh.devices.reshape(ZL, CORES, XS, ZH, YS), AXES)
    return jax.shard_map(
        on_device,
        mesh=fine,
        in_specs=(P(AXES, None), P(AXES, None), P(AXES, None), P(AXES), P()),
        out_specs=P(AXES, None),
        check_vma=False,
    )
```

time: 1220 us -> 292 us (0.24)
  the two profiles are of different devices: /device:TPU:1 before, /device:TPU:32 now
where the time goes in v1:
time: 292 us; the launch traced here: 291 us
  waiting for transfers between devices  139 us (48%)
  starting transfers between devices  98.6 us (34%)
  Pallas kernels  15.5 us (5%)
  blocking collectives  13.8 us (5%)
  local copies, waits for them, and re-layouts  11 us (4%)
  other arithmetic  10.2 us (3%)
  between operations  3.11 us (1%)
    ppermute x8, waiting for transfers between devices, send(): return lax.ppermute(value, AXES, route(move))  110 us
    ppermute x8, starting transfers between devices, send(): return lax.ppermute(value, AXES, route(move))  59.5 us
    all_to_all x1, starting transfers between devices, on_device(): pieces = lax.all_to_all(pieces, ('zl', 'core'), 0, 0)  23.2 us
    all_to_all x1, waiting for transfers between devices, on_device(): kv = lax.all_to_all(packed, 'y', 0, 0)  21.8 us
    pallas_call x1, Pallas kernels, on_device(): pl.pallas_call(attend, out_shape=jax.ShapeDtypeStruct((YS, BLOCK, WIDE),...  15.5 us
    all_to_all x1, blocking collectives, on_device(): back = lax.all_to_all(out, 'y', 0, 0)  13.8 us
  transfers between devices with their start and end apart: 13, of which 7 were waited for; matrix products, arithmetic and copies ran while one was open for 4% of the time, Pallas kernels for 0%

profile of v1, /device:TPU:32, one launch (start us, length us, event | category | flops | bytes accessed | tf_op | source)
XLA Modules:
  0.0 291.2 jit_solution(6589318248997560303)
XLA Ops:
  2.5 1.3 pad_maximum_fusion
  3.8 4.5 %all-to-all-start.1 = ((bf16[4,272,768]{2,1,0:T(8,128)(2,1)}), bf16[4,272,768]{2,1,0:T(8,128)(2,1)S(1)}, u32[]{:S(2)}, u32[]{:S(2)}) async-start(bf16[4,272,768]{2,1,0:T(8,128)(2,1)} %pad_maximum_fusion), calls=%async_computation.1 | async-start | bytes 3342336 | tf_op jit(solution)/shard_map/all_to_all | solution.py:188
  8.2 21.8 %all-to-all-done.1.kv = bf16[4,272,768]{2,1,0:T(8,128)(2,1)S(1)} async-done(((bf16[4,272,768]{2,1,0:T(8,128)(2,1)}), bf16[4,272,768]{2,1,0:T(8,128)(2,1)S(1)}, u32[]{:S(2)}, u32[]{:S(2)}) %all-to-all-start.1) | async-done | bytes 1671200 | tf_op jit(solution)/shard_map/all_to_all | solution.py:188
  31.0 2.1 collective-permute-start.2
  34.5 9.1 %collective-permute-start.3 = (bf16[1,2,2,128,256]{4,3,2,1,0:T(8,128)(2,1)S(1)}, bf16[1,2,2,128,256]{4,3,2,1,0:T(8,128)(2,1)S(1)}, u32[]{:S(2)}, u32[]{:S(2)}) collective-permute-start(bf16[1,2,2,128,256]{4,3,2,1,0:T(8,128)(2,1)S(1)} %maximum_select_fusion), channel_id=1, source_target_pairs={{0,256},{1,257},{2,258},{3,259},{4,260},{5,261},{6,262},{7,263},{8... | collective-permute-start | bytes 786440 | tf_op jit(solution)/shard_map/ppermute | solution.py:50
  44.4 10.3 %collective-permute-done.3 = bf16[1,2,2,128,256]{4,3,2,1,0:T(8,128)(2,1)S(1)} collective-permute-done((bf16[1,2,2,128,256]{4,3,2,1,0:T(8,128)(2,1)S(1)}, bf16[1,2,2,128,256]{4,3,2,1,0:T(8,128)(2,1)S(1)}, u32[]{:S(2)}, u32[]{:S(2)}) %collective-permute-start.3) | collective-permute-done | bytes 262176 | tf_op jit(solution)/shard_map/ppermute | solution.py:50
  55.6 27.4 %collective-permute-start.4 = (bf16[2,2,2,128,256]{4,3,2,1,0:T(8,128)(2,1)}, bf16[2,2,2,128,256]{4,3,2,1,0:T(8,128)(2,1)}, u32[]{:S(2)}, u32[]{:S(2)}) collective-permute-start(bf16[2,2,2,128,256]{4,3,2,1,0:T(8,128)(2,1)} %pad_maximum_fusion.4), channel_id=1, source_target_pairs={{0,128},{1,129},{2,130},{3,131},{4,132},{5,133},{6,134},{7,135},{8... | collective-permute-start | bytes 1572872 | tf_op jit(solution)/shard_map/ppermute | solution.py:50
  87.6 1.4 fusion.5
  89.0 4.3 %all-to-all-start.2 = ((bf16[4,32,256]{2,1,0:T(8,128)(2,1)}), bf16[4,32,256]{2,1,0:T(8,128)(2,1)S(1)}, u32[]{:S(2)}, u32[]{:S(2)}) async-start(bf16[4,32,256]{2,1,0:T(8,128)(2,1)} %bitcast.15), calls=%async_computation.2 | async-start | bytes 131072 | tf_op jit(solution)/shard_map/all_to_all | solution.py:215
  94.3 4.6 %all-to-all-done.2 = bf16[4,32,256]{2,1,0:T(8,128)(2,1)S(1)} async-done(((bf16[4,32,256]{2,1,0:T(8,128)(2,1)}), bf16[4,32,256]{2,1,0:T(8,128)(2,1)S(1)}, u32[]{:S(2)}, u32[]{:S(2)}) %all-to-all-start.2) | async-done | bytes 65568 | tf_op jit(solution)/shard_map/all_to_all | solution.py:215
  98.9 3.5 %all-to-all-start = ((bf16[4,128,768]{2,1,0:T(8,128)(2,1)}), bf16[4,128,768]{2,1,0:T(8,128)(2,1)S(1)}, u32[]{:S(2)}, u32[]{:S(2)}) async-start(bf16[4,128,768]{2,1,0:T(8,128)(2,1)} %pad_maximum_fusion.2), calls=%async_computation | async-start | bytes 1572864 | tf_op jit(solution)/shard_map/all_to_all | solution.py:189
  103.8 1.9 collective-permute-start.5
  107.1 9.6 %collective-permute-start.1 = (bf16[32,256]{1,0:T(8,128)(2,1)S(1)}, bf16[32,256]{1,0:T(8,128)(2,1)S(1)}, u32[]{:S(2)}, u32[]{:S(2)}) collective-permute-start(bf16[32,256]{1,0:T(8,128)(2,1)S(1)} %dynamic-slice_bitcast_fusion), channel_id=1, source_target_pairs={{0,4},{1,5},{2,6},{3,7},{4,0},{5,1},{6,2},{7,3},{8,12},{9,13},{10,... | collective-permute-start | bytes 49160 | tf_op jit(solution)/shard_map/ppermute | solution.py:50
  116.7 4.7 %collective-permute-done.1 = bf16[32,256]{1,0:T(8,128)(2,1)S(1)} collective-permute-done((bf16[32,256]{1,0:T(8,128)(2,1)S(1)}, bf16[32,256]{1,0:T(8,128)(2,1)S(1)}, u32[]{:S(2)}, u32[]{:S(2)}) %collective-permute-start.1) | collective-permute-done | bytes 16416 | tf_op jit(solution)/shard_map/ppermute | solution.py:50
  122.9 23.2 %all-to-all-start.3 = ((bf16[16,32,256]{2,1,0:T(8,128)(2,1)}), bf16[16,32,256]{2,1,0:T(8,128)(2,1)}, u32[]{:S(2)}, u32[]{:S(2)}) async-start(bf16[16,32,256]{2,1,0:T(8,128)(2,1)} %broadcast_in_dim.24), calls=%async_computation.3 | async-start | bytes 524288 | tf_op jit(solution)/shard_map/all_to_all | solution.py:220
  146.1 2.1 collective-permute-start.6
  148.1 2.3 collective-permute-start.7
  152.4 5.0 %collective-permute-start = (bf16[2,256,768]{2,1,0:T(8,128)(2,1)}, bf16[2,256,768]{2,1,0:T(8,128)(2,1)}, u32[]{:S(2)}, u32[]{:S(2)}) collective-permute-start(bf16[2,256,768]{2,1,0:T(8,128)(2,1)} %pad_maximum_fusion.3), channel_id=1, source_target_pairs={{0,4},{1,5},{2,6},{3,7},{4,8},{5,9},{6,10},{7,11},{8,12},{9,13},{1... | collective-permute-start | bytes 2359304 | tf_op jit(solution)/shard_map/ppermute | solution.py:50
  157.4 3.0 %all-to-all-done.3 = bf16[16,32,256]{2,1,0:T(8,128)(2,1)} async-done(((bf16[16,32,256]{2,1,0:T(8,128)(2,1)}), bf16[16,32,256]{2,1,0:T(8,128)(2,1)}, u32[]{:S(2)}, u32[]{:S(2)}) %all-to-all-start.3) | async-done | bytes 262176 | tf_op jit(solution)/shard_map/all_to_all | solution.py:220
  160.4 2.1 broadcast_in_dim.25
  162.5 3.7 %all-to-all-start.4 = ((bf16[4,16,32,256]{3,2,1,0:T(8,128)(2,1)}), bf16[4,16,32,256]{3,2,1,0:T(8,128)(2,1)S(1)}, u32[]{:S(2)}, u32[]{:S(2)}) async-start(bf16[4,16,32,256]{3,2,1,0:T(8,128)(2,1)} %broadcast_in_dim.25), calls=%async_computation.4 | async-start | bytes 2097152 | tf_op jit(solution)/shard_map/all_to_all | solution.py:222
  166.9 93.3 %collective-permute-done.halo = bf16[2,256,768]{2,1,0:T(8,128)(2,1)} collective-permute-done((bf16[2,256,768]{2,1,0:T(8,128)(2,1)}, bf16[2,256,768]{2,1,0:T(8,128)(2,1)}, u32[]{:S(2)}, u32[]{:S(2)}) %collective-permute-start) | collective-permute-done | bytes 786464 | tf_op jit(solution)/shard_map/ppermute | solution.py:50
  260.2 15.5 %attend.1 = bf16[4,128,768]{2,1,0:T(8,128)(2,1)S(1)} custom-call(s32[2]{0:T(128)S(1)} %pad_add_fusion.info, f32[8,2048]{1,0:T(8,128)S(1)} %convert_element_type.11.far_ok, bf16[4,128,768]{2,1,0:T(8,128)(2,1)S(1)} %all-to-all-done.q, bf16[4,272,768]{2,1,0:T(8,128)(2,1)} %copy-done, bf16[2,256,768]{2,1,0:T(8,128)(2,1)} %collective-permute-done.halo, ...), custom_call_target="tpu_custom_call" | custom-call | tf_op jit(solution)/shard_map/attend/pallas_call | solution.py:237
  275.7 13.8 %all_to_all.30 = bf16[4,128,768]{2,1,0:T(8,128)(2,1)S(1)} all-to-all(bf16[4,128,768]{2,1,0:T(8,128)(2,1)S(1)} %attend.1), channel_id=1, replica_groups=mesh['zl'=8,'core'=2,'x'=4,'zh'=2,'y'=4] {'y'}, dimensions={0} | all-to-all | bytes 1572864 | tf_op jit(solution)/shard_map/all_to_all | solution.py:250
  (87 shorter events, 17.7 us)
Async XLA Ops:
  0.0 2.1 copy-start.4
  0.0 2.2 copy-start.8
  3.8 26.2 %all-to-all-start.1 = ((bf16[4,272,768]{2,1,0:T(8,128)(2,1)}), bf16[4,272,768]{2,1,0:T(8,128)(2,1)S(1)}, u32[]{:S(2)}, u32[]{:S(2)}) async-start(bf16[4,272,768]{2,1,0:T(8,128)(2,1)} %pad_maximum_fusion), calls=%async_computation.1 | async-start | bytes 3342336 | tf_op jit(solution)/shard_map/all_to_all | solution.py:188
  30.0 120.5 %copy-start = (bf16[4,272,768]{2,1,0:T(8,128)(2,1)}, bf16[4,272,768]{2,1,0:T(8,128)(2,1)S(1)}, u32[]{:S(2)}) copy-start(bf16[4,272,768]{2,1,0:T(8,128)(2,1)S(1)} %all-to-all-done.1.kv) | copy-start | bytes 5013508
  30.0 13.5 %copy-start.5 = (bf16[128,3072]{1,0:T(8,128)(2,1)S(1)}, bf16[128,3072]{1,0:T(8,128)(2,1)}, u32[]{:S(2)}) copy-start(bf16[128,3072]{1,0:T(8,128)(2,1)} %param.6) | copy-start | bytes 2359300
  30.2 25.4 %copy-start.1 = (bf16[4,128,768]{2,1,0:T(8,128)(2,1)}, bf16[4,128,768]{2,1,0:T(8,128)(2,1)S(1)}, u32[]{:S(2)}) copy-start(bf16[4,128,768]{2,1,0:T(8,128)(2,1)S(1)} %slice_select_fusion) | copy-start | bytes 2359300
  31.0 52.0 %copy-start.9 = (s32[16]{0:T(128)S(1)}, s32[16]{0:T(128)}, u32[]{:S(2)}) copy-start(s32[16]{0:T(128)} %param.10) | copy-start | bytes 196
  31.0 3.4 %collective-permute-start.2 = (bf16[2,128,256]{2,1,0:T(8,128)(2,1)S(1)}, bf16[2,128,256]{2,1,0:T(8,128)(2,1)S(1)}, u32[]{:S(2)}, u32[]{:S(2)}) collective-permute-start(bf16[2,128,256]{2,1,0:T(8,128)(2,1)S(1)} %get-tuple-element.46), channel_id=1, source_target_pairs={{0,32},{1,33},{2,34},{3,35},{4,36},{5,37},{6,38},{7,39},{8,40},{9,... | collective-permute-start | bytes 393224 | tf_op jit(solution)/shard_map/ppermute | solution.py:50
  34.4 52.2 %copy-start.2 = (bf16[1,2,2,128,256]{4,3,2,1,0:T(8,128)(2,1)}, bf16[1,2,2,128,256]{4,3,2,1,0:T(8,128)(2,1)S(1)}, u32[]{:S(2)}) copy-start(bf16[1,2,2,128,256]{4,3,2,1,0:T(8,128)(2,1)S(1)} %maximum_select_fusion) | copy-start | bytes 786436
  34.5 20.2 %collective-permute-start.3 = (bf16[1,2,2,128,256]{4,3,2,1,0:T(8,128)(2,1)S(1)}, bf16[1,2,2,128,256]{4,3,2,1,0:T(8,128)(2,1)S(1)}, u32[]{:S(2)}, u32[]{:S(2)}) collective-permute-start(bf16[1,2,2,128,256]{4,3,2,1,0:T(8,128)(2,1)S(1)} %maximum_select_fusion), channel_id=1, source_target_pairs={{0,256},{1,257},{2,258},{3,259},{4,260},{5,261},{6,262},{7,263},{8... | collective-permute-start | bytes 786440 | tf_op jit(solution)/shard_map/ppermute | solution.py:50
  54.7 34.3 %copy-start.3 = (bf16[1,2,2,128,256]{4,3,2,1,0:T(8,128)(2,1)}, bf16[1,2,2,128,256]{4,3,2,1,0:T(8,128)(2,1)S(1)}, u32[]{:S(2)}) copy-start(bf16[1,2,2,128,256]{4,3,2,1,0:T(8,128)(2,1)S(1)} %collective-permute-done.3) | copy-start | bytes 786436
  55.6 46.9 %collective-permute-start.4 = (bf16[2,2,2,128,256]{4,3,2,1,0:T(8,128)(2,1)}, bf16[2,2,2,128,256]{4,3,2,1,0:T(8,128)(2,1)}, u32[]{:S(2)}, u32[]{:S(2)}) collective-permute-start(bf16[2,2,2,128,256]{4,3,2,1,0:T(8,128)(2,1)} %pad_maximum_fusion.4), channel_id=1, source_target_pairs={{0,128},{1,129},{2,130},{3,131},{4,132},{5,133},{6,134},{7,135},{8... | collective-permute-start | bytes 1572872 | tf_op jit(solution)/shard_map/ppermute | solution.py:50
  89.0 9.9 %all-to-all-start.2 = ((bf16[4,32,256]{2,1,0:T(8,128)(2,1)}), bf16[4,32,256]{2,1,0:T(8,128)(2,1)S(1)}, u32[]{:S(2)}, u32[]{:S(2)}) async-start(bf16[4,32,256]{2,1,0:T(8,128)(2,1)} %bitcast.15), calls=%async_computation.2 | async-start | bytes 131072 | tf_op jit(solution)/shard_map/all_to_all | solution.py:215
  98.9 3.5 %copy-start.6 = (bf16[4,32,256]{2,1,0:T(8,128)(2,1)}, bf16[4,32,256]{2,1,0:T(8,128)(2,1)S(1)}, u32[]{:S(2)}) copy-start(bf16[4,32,256]{2,1,0:T(8,128)(2,1)S(1)} %all-to-all-done.2) | copy-start | bytes 196612
  98.9 23.2 %all-to-all-start = ((bf16[4,128,768]{2,1,0:T(8,128)(2,1)}), bf16[4,128,768]{2,1,0:T(8,128)(2,1)S(1)}, u32[]{:S(2)}, u32[]{:S(2)}) async-start(bf16[4,128,768]{2,1,0:T(8,128)(2,1)} %pad_maximum_fusion.2), calls=%async_computation | async-start | bytes 1572864 | tf_op jit(solution)/shard_map/all_to_all | solution.py:189
  102.5 43.6 %copy-start.10 = (s32[8]{0:T(128)S(1)}, s32[8]{0:T(128)}, u32[]{:S(2)}) copy-start(s32[8]{0:T(128)} %constant.98) | copy-start | bytes 100
  103.8 44.3 %collective-permute-start.5 = (bf16[4,2,2,128,256]{4,3,2,1,0:T(8,128)(2,1)S(1)}, bf16[4,2,2,128,256]{4,3,2,1,0:T(8,128)(2,1)}, u32[]{:S(2)}, u32[]{:S(2)}) collective-permute-start(bf16[4,2,2,128,256]{4,3,2,1,0:T(8,128)(2,1)S(1)} %pad_maximum_fusion.1.s1), channel_id=1, source_target_pairs={{0,64},{1,65},{2,66},{3,67},{4,68},{5,69},{6,70},{7,71},{8,72},{9,... | collective-permute-start | bytes 3145736 | tf_op jit(solution)/shard_map/ppermute | solution.py:50
  107.1 14.3 %collective-permute-start.1 = (bf16[32,256]{1,0:T(8,128)(2,1)S(1)}, bf16[32,256]{1,0:T(8,128)(2,1)S(1)}, u32[]{:S(2)}, u32[]{:S(2)}) collective-permute-start(bf16[32,256]{1,0:T(8,128)(2,1)S(1)} %dynamic-slice_bitcast_fusion), channel_id=1, source_target_pairs={{0,4},{1,5},{2,6},{3,7},{4,0},{5,1},{6,2},{7,3},{8,12},{9,13},{10,... | collective-permute-start | bytes 49160 | tf_op jit(solution)/shard_map/ppermute | solution.py:50
  122.9 37.6 %all-to-all-start.3 = ((bf16[16,32,256]{2,1,0:T(8,128)(2,1)}), bf16[16,32,256]{2,1,0:T(8,128)(2,1)}, u32[]{:S(2)}, u32[]{:S(2)}) async-start(bf16[16,32,256]{2,1,0:T(8,128)(2,1)} %broadcast_in_dim.24), calls=%async_computation.3 | async-start | bytes 524288 | tf_op jit(solution)/shard_map/all_to_all | solution.py:220
  146.1 114.1 %collective-permute-start.6 = (bf16[4,2,2,128,256]{4,3,2,1,0:T(8,128)(2,1)S(1)}, bf16[4,2,2,128,256]{4,3,2,1,0:T(8,128)(2,1)}, u32[]{:S(2)}, u32[]{:S(2)}) collective-permute-start(bf16[4,2,2,128,256]{4,3,2,1,0:T(8,128)(2,1)S(1)} %pad_maximum_fusion.1.s1), channel_id=1, source_target_pairs={{0,32},{1,33},{2,34},{3,35},{4,36},{5,37},{6,38},{7,39},{8,40},{9,... | collective-permute-start | bytes 3145736 | tf_op jit(solution)/shard_map/ppermute | solution.py:50
  148.1 112.0 %collective-permute-start.7 = (bf16[4,2,2,128,256]{4,3,2,1,0:T(8,128)(2,1)}, bf16[4,2,2,128,256]{4,3,2,1,0:T(8,128)(2,1)}, u32[]{:S(2)}, u32[]{:S(2)}) collective-permute-start(bf16[4,2,2,128,256]{4,3,2,1,0:T(8,128)(2,1)} %collective-permute-done.5.s2), channel_id=1, source_target_pairs={{0,32},{1,33},{2,34},{3,35},{4,36},{5,37},{6,38},{7,39},{8,40},{9,... | collective-permute-start | bytes 3145736 | tf_op jit(solution)/shard_map/ppermute | solution.py:50
  150.4 1.0 slice-start
  152.4 107.8 %collective-permute-start = (bf16[2,256,768]{2,1,0:T(8,128)(2,1)}, bf16[2,256,768]{2,1,0:T(8,128)(2,1)}, u32[]{:S(2)}, u32[]{:S(2)}) collective-permute-start(bf16[2,256,768]{2,1,0:T(8,128)(2,1)} %pad_maximum_fusion.3), channel_id=1, source_target_pairs={{0,4},{1,5},{2,6},{3,7},{4,8},{5,9},{6,10},{7,11},{8,12},{9,13},{1... | collective-permute-start | bytes 2359304 | tf_op jit(solution)/shard_map/ppermute | solution.py:50
  162.5 97.7 %all-to-all-start.4 = ((bf16[4,16,32,256]{3,2,1,0:T(8,128)(2,1)}), bf16[4,16,32,256]{3,2,1,0:T(8,128)(2,1)S(1)}, u32[]{:S(2)}, u32[]{:S(2)}) async-start(bf16[4,16,32,256]{3,2,1,0:T(8,128)(2,1)} %broadcast_in_dim.25), calls=%async_computation.4 | async-start | bytes 2097152 | tf_op jit(solution)/shard_map/all_to_all | solution.py:222
  (1 other events, 0.9 us)

commit v2 on v1

v2 whole, which is shorter than its diff:
```python
import itertools
import math

import jax
import jax.numpy as jnp
from jax import lax
from jax.experimental import pallas as pl
from jax.experimental.pallas import tpu as pltpu
from jax.sharding import Mesh, PartitionSpec as P

HEADS = 24
DIM = 128
BLOCK = 128
LOCAL = 16
ZP, ZQ, CORES, XS, ZH, YS = 4, 2, 2, 4, 2, 4
AXES = ("zp", "zq", "core", "x", "zh", "y")
SIZES = dict(zip(AXES, (ZP, ZQ, CORES, XS, ZH, YS)))
GRP = ("zp", "zq", "core")
WINDOWS = ZP * ZQ * CORES
PART = BLOCK // YS
PER = LOCAL // YS
MINE = PER + 2
WIDE = MINE * DIM
ROWS = 2 * BLOCK + 16
MARK = 128.0
NEG = -1e30
LEGS = (4, 4)
LEAST = -1e4
SCALE = 1.0 / (math.sqrt(DIM) * math.log(2.0))
f32, bf16 = jnp.float32, jnp.bfloat16


def index_of(place):
    at = 0
    for axis in AXES:
        at = at * SIZES[axis] + place[axis]
    return at


def route(move):
    pairs = []
    for spot in itertools.product(*(range(SIZES[a]) for a in AXES)):
        place = dict(zip(AXES, spot))
        to = move(place)
        if to is not None:
            pairs.append((index_of(place), index_of({**place, **to})))
    return pairs


def send(value, move):
    return lax.ppermute(value, AXES, route(move))


def next_group(p):
    if p["zh"] == 0:
        return dict(p, zh=1)
    if p["x"] < XS - 1:
        return dict(p, zh=0, x=p["x"] + 1)
    window = (p["zp"] * ZQ + p["zq"]) * CORES + p["core"] + 1
    if window == WINDOWS:
        return None
    return dict(p, zh=0, x=0, zp=window // (ZQ * CORES), zq=window // CORES % ZQ, core=window % CORES)


def along_z(p, steps):
    z = (p["zh"] * ZP + p["zp"]) * ZQ + p["zq"]
    z = (z + (steps if p["core"] == 0 else -steps)) % (ZH * ZP * ZQ)
    return dict(p, zh=z // (ZP * ZQ), zp=z // ZQ % ZP, zq=z % ZQ)


def leg(n):
    pairs = []
    for spot in itertools.product(*(range(SIZES[a]) for a in AXES)):
        place = dict(zip(AXES, spot))
        end = next_group(place)
        if end is not None:
            to = along_z(place, sum(LEGS[: n + 1])) if n < len(LEGS) - 1 else end
            pairs.append((index_of(along_z(place, sum(LEGS[:n]))), index_of(to)))
    return pairs


def flip(axis, bits):
    return lambda p: {axis: p[axis] ^ bits}


def heads_of(y):
    return [PER * y + i for i in range(PER)] + [LOCAL + y, LOCAL + YS + y]


def qk(a, b):
    return lax.dot_general(a, b, (((1,), (1,)), ((), ())), preferred_element_type=f32)


def pv(p, v):
    return jnp.dot(p.astype(bf16), v, preferred_element_type=f32)


def unmarked(keys):
    rows = 16
    pick = jnp.where(lax.broadcasted_iota(jnp.int32, (rows, DIM), 1) == 0, 1.0, 0.0).astype(bf16)
    return qk(pick, keys)[0:1] < MARK / 2


def column(head):
    return slice(head * DIM, (head + 1) * DIM)


def pack_kernel(info, keep_row, keep_col, q, k, v, s1, f1, *outs):
    pieces, queries = outs[:YS], outs[YS:]
    keep = jnp.broadcast_to(keep_col[...] > 0, (BLOCK, DIM))
    for h in range(YS):
        c = column(LOCAL + YS + h)
        key = jnp.where(keep, k[:, c], jnp.array(MARK, bf16))
        for s in range(BLOCK // PART):
            r = slice(s * PART, (s + 1) * PART)
            s1[h * YS + s, :, 0:DIM] = key[r]
            s1[h * YS + s, :, DIM : 2 * DIM] = v[r, c]
            s1[h * YS + s, :, 2 * DIM : 3 * DIM] = q[r, c]
        c = column(LOCAL + h)
        key = jnp.where(keep, k[:, c], jnp.array(MARK, bf16))
        for s in range(XS):
            r = slice(s * PART, (s + 1) * PART)
            f1[s * YS + h, :, 0:DIM] = key[r]
            f1[s * YS + h, :, DIM : 2 * DIM] = v[r, c]
    row = jnp.broadcast_to(keep_row[...].astype(f32), (16, BLOCK)).astype(bf16)
    for here in range(YS):

        @pl.when(info[1] == here)
        def _():
            for d in range(YS):
                for i, h in enumerate(heads_of(here ^ d)):
                    to = column(i)
                    pieces[d][0:BLOCK, to] = k[:, column(h)]
                    pieces[d][BLOCK : 2 * BLOCK, to] = v[:, column(h)]
                    pieces[d][2 * BLOCK : ROWS, to] = row
                    queries[d][:, to] = q[:, column(h)]


def halo_kernel(info, *refs):
    out = refs[-1]
    for here in range(YS):

        @pl.when(info[1] == here)
        def _():
            for i in range(2):
                ref = refs[here ^ (2 + i)]
                row = ref[2 * BLOCK : 2 * BLOCK + 1, 0:BLOCK].astype(f32)
                keep = jnp.transpose(jnp.broadcast_to(row, (BLOCK, BLOCK))) > 0.5
                for h in range(MINE):
                    c = column(h)
                    out[i, 0:BLOCK, c] = jnp.where(keep, ref[0:BLOCK, c], jnp.array(MARK, bf16))
                out[i, BLOCK : 2 * BLOCK] = ref[BLOCK : 2 * BLOCK]


def stats_of(top, total, shape):
    rough = total.astype(bf16).astype(f32)
    lanes = lax.broadcasted_iota(jnp.int32, shape, 1)
    return jnp.where(lanes == 0, top, jnp.where(lanes == 1, rough, total - rough)).astype(bf16)


def far_kernel(part, keys_values, out):
    count = WINDOWS * BLOCK
    kv = keys_values[...].reshape(count, 2 * DIM)
    flags = unmarked(kv[:, :DIM])
    step = 128
    for t in range(WINDOWS * PART // step):
        windows = step // PART
        query = part[t * windows : (t + 1) * windows, :, 2 * DIM : 3 * DIM].reshape(step, DIM)
        row_window = t * windows + lax.broadcasted_iota(jnp.int32, (step, count), 0) // PART
        key_window = lax.broadcasted_iota(jnp.int32, (step, count), 1) // PART % WINDOWS
        ok = (key_window < row_window) & jnp.broadcast_to(flags, (step, count))
        scores = jnp.where(ok, qk(query, kv[:, :DIM]) * SCALE, NEG)
        top = jnp.maximum(jnp.max(scores, axis=1, keepdims=True), LEAST)
        top = top.astype(bf16).astype(f32)
        weights = jnp.exp2(scores - top)
        total = jnp.sum(weights, axis=1, keepdims=True)
        acc = pv(weights, kv[:, DIM:])
        both = jnp.concatenate([acc.astype(bf16), stats_of(top, total, (step, DIM))], axis=1)
        out[t * windows : (t + 1) * windows] = both.reshape(windows, PART, 2 * DIM)


def attend_kernel(info, fixed_ok, p0, p1, p2, p3, q0, q1, q2, q3, halo, f0, f1, f2, f3, out, kv, q):
    for d, (piece, query) in enumerate(zip((p0, p1, p2, p3), (q0, q1, q2, q3))):
        kv[info[1] ^ d] = piece[...]
        q[info[1] ^ d] = query[...]
    summary = (f0, f1, f2, f3)
    rows = lax.broadcasted_iota(jnp.int32, (BLOCK, BLOCK), 0)
    cols = lax.broadcasted_iota(jnp.int32, (BLOCK, BLOCK), 1)
    keeps = [kv[j, 2 * BLOCK : 2 * BLOCK + 1, 0:BLOCK].astype(f32) > 0.5 for j in range(YS)]
    halo_keeps = [unmarked(halo[i, 0:BLOCK, 0:DIM]) & (info[0] > 0) for i in range(2)]
    far_flags = [unmarked(f[:, 0:DIM]) for f in summary]
    for j in range(YS):
        masks = [((cols <= rows) & jnp.broadcast_to(keeps[j], (BLOCK, BLOCK))) | (cols == rows)]
        for back in (1, 2):
            flag = keeps[j - back] if j >= back else halo_keeps[2 + j - back]
            masks.append(jnp.broadcast_to(flag, (BLOCK, BLOCK)))
        for h in range(MINE):
            c = column(h)
            query = q[j, :, c]
            scores, values = [], []
            for back in range(3):
                ref, at = (kv, j - back) if j >= back else (halo, 2 + j - back)
                scores.append(jnp.where(masks[back], qk(query, ref[at, 0:BLOCK, c]) * SCALE, NEG))
                values.append(ref[at, BLOCK : 2 * BLOCK, c])
            if h == PER:
                for f, flag in zip(summary, far_flags):
                    ok = flag & (fixed_ok[j : j + 1, :] > 0.5)
                    s = qk(query, f[:, 0:DIM]) * SCALE
                    scores.append(jnp.where(jnp.broadcast_to(ok, s.shape), s, NEG))
                    values.append(f[:, DIM : 2 * DIM])
            top = jnp.max(jnp.maximum(jnp.maximum(scores[0], scores[1]), scores[2]), axis=1, keepdims=True)
            for s in scores[3:]:
                top = jnp.maximum(top, jnp.max(s, axis=1, keepdims=True))
            if h == PER + 1:
                top = top.astype(bf16).astype(f32)
            weights = [jnp.exp2(s - top) for s in scores]
            total = jnp.sum(weights[0] + weights[1] + weights[2], axis=1, keepdims=True)
            acc = pv(weights[0], values[0]) + pv(weights[1], values[1]) + pv(weights[2], values[2])
            for w, v in zip(weights[3:], values[3:]):
                total = total + jnp.sum(w, axis=1, keepdims=True)
                acc = acc + pv(w, v)
            if h == PER + 1:
                out[j, :, c] = acc.astype(bf16)
                out[j, :, column(h + 1)] = stats_of(top, total, (BLOCK, DIM))
            else:
                out[j, :, c] = (acc / total).astype(bf16)


def merge_kernel(back, far, out):
    for y in range(YS):
        for i, h in enumerate(heads_of(y)[:-1]):
            out[:, column(h)] = back[y, :, column(i)]
        near = back[y, :, column(MINE)].astype(f32)
        there = far[y, :, column(1)].astype(f32)
        near_top, near_total = near[:, 0:1], near[:, 1:2] + near[:, 2:3]
        far_top, far_total = there[:, 0:1], there[:, 1:2] + there[:, 2:3]
        top = jnp.maximum(near_top, far_top)
        near_scale, far_scale = jnp.exp2(near_top - top), jnp.exp2(far_top - top)
        acc = back[y, :, column(MINE - 1)].astype(f32) * near_scale
        acc = acc + far[y, :, column(0)].astype(f32) * far_scale
        total = near_total * near_scale + far_total * far_scale
        out[:, column(heads_of(y)[-1])] = (acc / total).astype(bf16)


VMEM = pl.BlockSpec(memory_space=pltpu.VMEM)
SMEM = pl.BlockSpec(memory_space=pltpu.SMEM)


def call(kernel, shapes, flops, operands, scratch=()):
    many = isinstance(shapes, list)
    moved = sum(o.size * o.dtype.itemsize for o in operands)
    outs = [jax.ShapeDtypeStruct(s, bf16) for s in shapes] if many else jax.ShapeDtypeStruct(shapes, bf16)
    return pl.pallas_call(
        kernel,
        out_shape=outs,
        in_specs=[SMEM if o.ndim == 1 else VMEM for o in operands],
        out_specs=[VMEM] * len(shapes) if many else VMEM,
        scratch_shapes=scratch,
        compiler_params=pltpu.CompilerParams(vmem_limit_bytes=40 << 20),
        cost_estimate=pl.CostEstimate(flops=flops, bytes_accessed=moved, transcendentals=0),
        name=kernel.__name__,
    )(*operands)


tie = lax.optimization_barrier
DOUBLING = (("zp", 2, 8), ("zp", 1, 4), ("zq", 1, 2), ("core", 1, 1))


def on_device(queries, key_states, value_states, key_keep, summary_pos):
    zp, zq, core, x, zh, y = (lax.axis_index(a) for a in AXES)
    window = (zp * ZQ + zq) * CORES + core
    group = window * (XS * ZH) + x * ZH + zh
    info = jnp.stack([(group > 0).astype(jnp.int32), y.astype(jnp.int32)])

    windows = jnp.arange(WINDOWS, dtype=jnp.int32)
    masks = [0]
    for _, bit, mask in DOUBLING:
        masks += [m ^ mask for m in masks]
    order = window ^ jnp.array(masks, jnp.int32)
    where = jnp.sum(jnp.where(order[:, None] == windows[None, :], summary_pos[None, :], 0), axis=1)
    block_ids = group * YS + jnp.arange(YS, dtype=jnp.int32)
    fixed_ok = (order * (XS * ZH * YS) + where)[None, :] < block_ids[:, None] - 2
    fixed_ok = jnp.repeat(fixed_ok.astype(f32), PART, axis=1)

    shapes = [(WINDOWS, PART, 3 * DIM), (XS * YS, PART, 2 * DIM)] + [(ROWS, WIDE)] * YS + [(BLOCK, WIDE)] * YS
    keep_row, keep_col = key_keep.reshape(1, BLOCK), key_keep.reshape(BLOCK, 1)
    packed = call(pack_kernel, shapes, 10**6, [info, keep_row, keep_col, queries, key_states, value_states])
    s1, f1, pieces, asked = packed[0], packed[1], packed[2 : 2 + YS], packed[2 + YS :]

    root = summary_pos[window]
    at = root // (ZH * YS) * YS + root % YS
    here = zh == root // YS % ZH
    got = [pieces[0]] + [send(pieces[d], flip("y", d)) for d in range(1, YS)]
    parts = lax.all_to_all(f1, ("x", "y"), 0, 0)
    parts, s1 = tie((parts, s1))
    part = lax.all_to_all(s1, GRP, 0, 0)
    piece = lax.dynamic_index_in_dim(parts, at, 0, keepdims=False)
    twin = send(piece, flip("zh", 1))
    spread = jnp.where(here, piece, twin)
    got1, got2, got3, part, spread, asked = tie((got[1], got[2], got[3], part, spread, asked))
    got = [got[0], got1, got2, got3]
    halo = call(halo_kernel, (2, 2 * BLOCK, WIDE), 10**6, [info] + got)
    for n in range(len(LEGS) // 2):
        halo = lax.ppermute(halo, AXES, leg(n))

    for axis, bit, _ in DOUBLING:
        spread = jnp.concatenate([spread, send(spread, flip(axis, bit))])
    quarter = jnp.broadcast_to(part[None, :, :, : 2 * DIM], (YS, WINDOWS, PART, 2 * DIM))
    quarters = lax.all_to_all(quarter, ("zq", "core"), 0, 0)
    asked = [asked[0]] + [send(asked[d], flip("y", d)) for d in range(1, YS)]
    halo, quarters, spread, asked = tie((halo, quarters, spread, asked))

    for n in range(len(LEGS) // 2, len(LEGS)):
        halo = lax.ppermute(halo, AXES, leg(n))
    far = call(far_kernel, (WINDOWS, PART, 2 * DIM), 10**9, [part, quarters])
    far = lax.all_to_all(far, GRP, 0, 0).reshape(YS, BLOCK, 2 * DIM)
    summary = [spread] + [send(spread, flip("x", d)) for d in range(1, XS)]
    halo, far, summary = tie((halo, far, summary))

    out = call(
        attend_kernel,
        (YS, BLOCK, WIDE + DIM),
        2 * 10**9,
        [info, fixed_ok] + got + asked + [halo] + summary,
        [pltpu.VMEM((YS, ROWS, WIDE), bf16), pltpu.VMEM((YS, BLOCK, WIDE), bf16)],
    )
    back = lax.all_to_all(out, "y", 0, 0)
    return call(merge_kernel, queries.shape, 10**6, [back, far])


def solution(mesh):
    fine = Mesh(mesh.devices.reshape(tuple(SIZES.values())), AXES)
    return jax.shard_map(
        on_device,
        mesh=fine,
        in_specs=(P(AXES, None), P(AXES, None), P(AXES, None), P(AXES), P()),
        out_specs=P(AXES, None),
        check_vma=False,
    )
```

time: 292 us -> 229 us (0.78)
  the two profiles are of different devices: /device:TPU:32 before, /device:TPU:67 now
where the time goes in v2:
time: 229 us; the launch traced here: 227 us
  starting transfers between devices  92.3 us (40%)
  waiting for transfers between devices  71.9 us (31%)
  blocking collectives  27.5 us (12%)
  Pallas kernels  16.9 us (7%)
  local copies, waits for them, and re-layouts  14.6 us (6%)
  between operations  3.11 us (1%)
    ppermute x14, starting transfers between devices, send(): return lax.ppermute(value, AXES, route(move))  52.2 us
    ppermute x14, waiting for transfers between devices, send(): return lax.ppermute(value, AXES, route(move))  47.3 us
    ppermute x2, waiting for transfers between devices, on_device(): halo = lax.ppermute(halo, AXES, leg(n))  24.6 us
    pallas_call x5, Pallas kernels, call(): pl.pallas_call(kernel, out_shape=outs, in_specs=[SMEM if o.ndim == 1 else...  16.9 us
    all_to_all x1, blocking collectives, on_device(): back = lax.all_to_all(out, 'y', 0, 0)  14.7 us
    all_to_all x1, starting transfers between devices, on_device(): part = lax.all_to_all(s1, GRP, 0, 0)  13.8 us
    all_to_all x1, blocking collectives, on_device(): parts = lax.all_to_all(f1, ('x', 'y'), 0, 0)  12.9 us
    ppermute x2, starting transfers between devices, on_device(): halo = lax.ppermute(halo, AXES, leg(n))  12.7 us
  transfers between devices with their start and end apart: 19, of which 8 were waited for; matrix products, arithmetic and copies ran while one was open for 1% of the time, Pallas kernels for 0%

profile of v2, /device:TPU:67, one launch (start us, length us, event | category | flops | bytes accessed | tf_op | source)
XLA Modules:
  0.0 227.5 jit_solution(16665792219671086611)
XLA Ops:
  7.3 12.9 %all_to_all.25 = bf16[16,32,256]{2,1,0:T(8,128)(2,1)} all-to-all(bf16[16,32,256]{2,1,0:T(8,128)(2,1)S(1)} %get-tuple-element.43), channel_id=1, replica_groups=mesh['zp'=4,'zq'=2,'core'=2,'x'=4,'zh'=2,'y'=4] {'x','y'}, dimensions={0} | all-to-all | bytes 524288 | tf_op jit(solution)/shard_map/all_to_all | solution.py:294
  20.2 13.8 %all-to-all-start.1 = ((bf16[16,32,384]{2,1,0:T(8,128)(2,1)}), bf16[16,32,384]{2,1,0:T(8,128)(2,1)S(1)}, u32[]{:S(2)}, u32[]{:S(2)}) async-start(bf16[16,32,384]{2,1,0:T(8,128)(2,1)} %get-tuple-element.45), calls=%async_computation.1 | async-start | bytes 786432 | tf_op jit(solution)/shard_map/all_to_all | solution.py:296
  36.1 3.6 %collective-permute-start.1 = (bf16[272,768]{1,0:T(8,128)(2,1)S(1)}, bf16[272,768]{1,0:T(8,128)(2,1)S(1)}, u32[]{:S(2)}, u32[]{:S(2)}) collective-permute-start(bf16[272,768]{1,0:T(8,128)(2,1)S(1)} %get-tuple-element.41), channel_id=1, source_target_pairs={{0,2},{1,3},{2,0},{3,1},{4,6},{5,7},{6,4},{7,5},{8,10},{9,11},{10,... | collective-permute-start | bytes 1253384 | tf_op jit(solution)/shard_map/ppermute | solution.py:51
  39.8 3.8 %collective-permute-start.2 = (bf16[272,768]{1,0:T(8,128)(2,1)S(1)}, bf16[272,768]{1,0:T(8,128)(2,1)S(1)}, u32[]{:S(2)}, u32[]{:S(2)}) collective-permute-start(bf16[272,768]{1,0:T(8,128)(2,1)S(1)} %get-tuple-element.42), channel_id=1, source_target_pairs={{0,3},{1,2},{2,1},{3,0},{4,7},{5,6},{6,5},{7,4},{8,11},{9,10},{10,... | collective-permute-start | bytes 1253384 | tf_op jit(solution)/shard_map/ppermute | solution.py:51
  48.3 7.9 %collective-permute-start.3 = (bf16[32,256]{1,0:T(8,128)(2,1)S(1)}, bf16[32,256]{1,0:T(8,128)(2,1)S(1)}, u32[]{:S(2)}, u32[]{:S(2)}) collective-permute-start(bf16[32,256]{1,0:T(8,128)(2,1)S(1)} %dynamic-slice_bitcast_fusion), channel_id=1, source_target_pairs={{0,4},{1,5},{2,6},{3,7},{4,0},{5,1},{6,2},{7,3},{8,12},{9,13},{10,... | collective-permute-start | bytes 49160 | tf_op jit(solution)/shard_map/ppermute | solution.py:51
  56.3 5.2 %collective-permute-done.3 = bf16[32,256]{1,0:T(8,128)(2,1)S(1)} collective-permute-done((bf16[32,256]{1,0:T(8,128)(2,1)S(1)}, bf16[32,256]{1,0:T(8,128)(2,1)S(1)}, u32[]{:S(2)}, u32[]{:S(2)}) %collective-permute-start.3) | collective-permute-done | bytes 16416 | tf_op jit(solution)/shard_map/ppermute | solution.py:51
  63.5 5.8 %all-to-all-start.2 = ((bf16[4,16,32,256]{3,2,1,0:T(8,128)(2,1)}), bf16[4,16,32,256]{3,2,1,0:T(8,128)(2,1)S(1)}, u32[]{:S(2)}, u32[]{:S(2)}) async-start(bf16[4,16,32,256]{3,2,1,0:T(8,128)(2,1)} %broadcast_in_dim.29), calls=%async_computation.2 | async-start | bytes 2097152 | tf_op jit(solution)/shard_map/all_to_all | solution.py:309
  69.3 7.3 %collective-permute-start.5 = (bf16[32,256]{1,0:T(8,128)(2,1)S(1)}, bf16[32,256]{1,0:T(8,128)(2,1)S(1)}, u32[]{:S(2)}, u32[]{:S(2)}) collective-permute-start(bf16[32,256]{1,0:T(8,128)(2,1)S(1)} %broadcast_select_fusion), channel_id=1, source_target_pairs={{0,256},{1,257},{2,258},{3,259},{4,260},{5,261},{6,262},{7,263},{8... | collective-permute-start | bytes 49160 | tf_op jit(solution)/shard_map/ppermute | solution.py:51
  77.4 2.9 %collective-permute-start.4 = (bf16[2,256,768]{2,1,0:T(8,128)(2,1)S(1)}, bf16[2,256,768]{2,1,0:T(8,128)(2,1)}, u32[]{:S(2)}, u32[]{:S(2)}) collective-permute-start(bf16[2,256,768]{2,1,0:T(8,128)(2,1)S(1)} %halo_kernel.1), channel_id=1, source_target_pairs={{0,256},{1,257},{2,258},{3,259},{4,260},{5,261},{6,262},{7,263},{8... | collective-permute-start | bytes 2359304 | tf_op jit(solution)/shard_map/ppermute | solution.py:304
  80.2 19.0 %collective-permute-done.5 = bf16[32,256]{1,0:T(8,128)(2,1)S(1)} collective-permute-done((bf16[32,256]{1,0:T(8,128)(2,1)S(1)}, bf16[32,256]{1,0:T(8,128)(2,1)S(1)}, u32[]{:S(2)}, u32[]{:S(2)}) %collective-permute-start.5) | collective-permute-done | bytes 16416 | tf_op jit(solution)/shard_map/ppermute | solution.py:51
  103.1 4.8 %collective-permute-start.10 = (bf16[128,768]{1,0:T(8,128)(2,1)S(1)}, bf16[128,768]{1,0:T(8,128)(2,1)S(1)}, u32[]{:S(2)}, u32[]{:S(2)}) collective-permute-start(bf16[128,768]{1,0:T(8,128)(2,1)S(1)} %copy-done.9), channel_id=1, source_target_pairs={{0,2},{1,3},{2,0},{3,1},{4,6},{5,7},{6,4},{7,5},{8,10},{9,11},{10,... | collective-permute-start | bytes 589832 | tf_op jit(solution)/shard_map/ppermute | solution.py:51
  108.0 2.8 %collective-permute-start.11 = (bf16[128,768]{1,0:T(8,128)(2,1)S(1)}, bf16[128,768]{1,0:T(8,128)(2,1)S(1)}, u32[]{:S(2)}, u32[]{:S(2)}) collective-permute-start(bf16[128,768]{1,0:T(8,128)(2,1)S(1)} %copy-done.7), channel_id=1, source_target_pairs={{0,3},{1,2},{2,1},{3,0},{4,7},{5,6},{6,5},{7,4},{8,11},{9,10},{10,... | collective-permute-start | bytes 589832 | tf_op jit(solution)/shard_map/ppermute | solution.py:51
  110.8 9.8 %collective-permute-done.6 = bf16[64,256]{1,0:T(8,128)(2,1)S(1)} collective-permute-done((bf16[64,256]{1,0:T(8,128)(2,1)S(1)}, bf16[64,256]{1,0:T(8,128)(2,1)S(1)}, u32[]{:S(2)}, u32[]{:S(2)}) %collective-permute-start.6) | collective-permute-done | bytes 32800 | tf_op jit(solution)/shard_map/ppermute | solution.py:51
  120.6 3.7 %collective-permute-start.7 = (bf16[128,256]{1,0:T(8,128)(2,1)S(1)}, bf16[128,256]{1,0:T(8,128)(2,1)S(1)}, u32[]{:S(2)}, u32[]{:S(2)}) collective-permute-start(bf16[128,256]{1,0:T(8,128)(2,1)S(1)} %pad_maximum_fusion.1), channel_id=1, source_target_pairs={{0,64},{1,65},{2,66},{3,67},{4,68},{5,69},{6,70},{7,71},{8,72},{9,... | collective-permute-start | bytes 196616 | tf_op jit(solution)/shard_map/ppermute | solution.py:51
  126.4 2.9 %collective-permute-start.8 = (bf16[256,256]{1,0:T(8,128)(2,1)S(1)}, bf16[256,256]{1,0:T(8,128)(2,1)S(1)}, u32[]{:S(2)}, u32[]{:S(2)}) collective-permute-start(bf16[256,256]{1,0:T(8,128)(2,1)S(1)} %pad_maximum_fusion), channel_id=1, source_target_pairs={{0,32},{1,33},{2,34},{3,35},{4,36},{5,37},{6,38},{7,39},{8,40},{9,... | collective-permute-start | bytes 393224 | tf_op jit(solution)/shard_map/ppermute | solution.py:51
  132.4 3.1 %far_kernel.1 = bf16[16,32,256]{2,1,0:T(8,128)(2,1)} custom-call(bf16[16,32,384]{2,1,0:T(8,128)(2,1)S(1)} %all-to-all-done.1.part, bf16[4,16,32,256]{3,2,1,0:T(8,128)(2,1)S(1)} %all-to-all-done.2.keys_values), custom_call_target="tpu_custom_call" | custom-call | flops 1000000000 | bytes 1441792 | tf_op jit(solution)/shard_map/far_kernel/pallas_call | solution.py:253
  135.5 7.8 %all-to-all-start.3 = ((bf16[16,32,256]{2,1,0:T(8,128)(2,1)}), bf16[16,32,256]{2,1,0:T(8,128)(2,1)S(1)}, u32[]{:S(2)}, u32[]{:S(2)}) async-start(bf16[16,32,256]{2,1,0:T(8,128)(2,1)} %far_kernel.1), calls=%async_computation.3 | async-start | bytes 524288 | tf_op jit(solution)/shard_map/all_to_all | solution.py:316
  143.3 9.9 %collective-permute-start.12 = (bf16[2,256,768]{2,1,0:T(8,128)(2,1)}, bf16[2,256,768]{2,1,0:T(8,128)(2,1)S(1)}, u32[]{:S(2)}, u32[]{:S(2)}) collective-permute-start(bf16[2,256,768]{2,1,0:T(8,128)(2,1)} %collective-permute-done.4), channel_id=1, source_target_pairs={{256,4},{257,5},{258,6},{259,7},{260,8},{261,9},{262,10},{263,11},... | collective-permute-start | bytes 2359304 | tf_op jit(solution)/shard_map/ppermute | solution.py:314
  156.0 4.5 %collective-permute-start.14 = (bf16[512,256]{1,0:T(8,128)(2,1)S(1)}, bf16[512,256]{1,0:T(8,128)(2,1)}, u32[]{:S(2)}, u32[]{:S(2)}) collective-permute-start(bf16[512,256]{1,0:T(8,128)(2,1)S(1)} %constant_dynamic-update-slice_fusion.f0), channel_id=1, source_target_pairs={{0,16},{1,17},{2,18},{3,19},{4,20},{5,21},{6,22},{7,23},{8,24},{9,... | collective-permute-start | bytes 786440 | tf_op jit(solution)/shard_map/ppermute | solution.py:51
  162.9 5.9 %collective-permute-done.15.f3 = bf16[512,256]{1,0:T(8,128)(2,1)S(1)} collective-permute-done((bf16[512,256]{1,0:T(8,128)(2,1)S(1)}, bf16[512,256]{1,0:T(8,128)(2,1)S(1)}, u32[]{:S(2)}, u32[]{:S(2)}) %collective-permute-start.15) | collective-permute-done | bytes 262176 | tf_op jit(solution)/shard_map/ppermute | solution.py:51
  168.8 4.4 %collective-permute-done.13.f1 = bf16[512,256]{1,0:T(8,128)(2,1)} collective-permute-done((bf16[512,256]{1,0:T(8,128)(2,1)S(1)}, bf16[512,256]{1,0:T(8,128)(2,1)}, u32[]{:S(2)}, u32[]{:S(2)}) %collective-permute-start.13) | collective-permute-done | bytes 262176 | tf_op jit(solution)/shard_map/ppermute | solution.py:51
  173.2 24.6 %collective-permute-done.12.halo = bf16[2,256,768]{2,1,0:T(8,128)(2,1)S(1)} collective-permute-done((bf16[2,256,768]{2,1,0:T(8,128)(2,1)}, bf16[2,256,768]{2,1,0:T(8,128)(2,1)S(1)}, u32[]{:S(2)}, u32[]{:S(2)}) %collective-permute-start.12) | collective-permute-done | bytes 786464 | tf_op jit(solution)/shard_map/ppermute | solution.py:314
  201.5 9.6 %attend_kernel.1 = bf16[4,128,896]{2,1,0:T(8,128)(2,1)S(1)} custom-call(s32[2]{0:T(128)S(1)} %pad_add_fusion.info, f32[4,512]{1,0:T(4,128)S(1)} %reshape.22.fixed_ok, bf16[272,768]{1,0:T(8,128)(2,1)S(1)} %get-tuple-element.39.refs_0_.p0, bf16[272,768]{1,0:T(8,128)(2,1)S(1)} %collective-permute-done.refs_1_.p1, ...), custom_call_target="tpu_custom_call" | custom-call | flops 2000000000 | bytes 4300808 | tf_op jit(solution)/shard_map/attend_kernel/pallas_call | solution.py:253
  211.1 14.7 %all_to_all.26.back = bf16[4,128,896]{2,1,0:T(8,128)(2,1)S(1)} all-to-all(bf16[4,128,896]{2,1,0:T(8,128)(2,1)S(1)} %attend_kernel.1), channel_id=1, replica_groups=mesh['zp'=4,'zq'=2,'core'=2,'x'=4,'zh'=2,'y'=4] {'y'}, dimensions={0} | all-to-all | bytes 1835008 | tf_op jit(solution)/shard_map/all_to_all | solution.py:327
  (83 shorter events, 33.6 us)
Async XLA Ops:
  7.3 12.9 %copy-start.4 = (bf16[128,768]{1,0:T(8,128)(2,1)}, bf16[128,768]{1,0:T(8,128)(2,1)S(1)}, u32[]{:S(2)}) copy-start(bf16[128,768]{1,0:T(8,128)(2,1)S(1)} %get-tuple-element.60.q0) | copy-start | bytes 589828
  7.3 12.9 %copy-start.6 = (bf16[128,768]{1,0:T(8,128)(2,1)}, bf16[128,768]{1,0:T(8,128)(2,1)S(1)}, u32[]{:S(2)}) copy-start(bf16[128,768]{1,0:T(8,128)(2,1)S(1)} %get-tuple-element.59) | copy-start | bytes 589828
  20.2 42.1 %all-to-all-start.1 = ((bf16[16,32,384]{2,1,0:T(8,128)(2,1)}), bf16[16,32,384]{2,1,0:T(8,128)(2,1)S(1)}, u32[]{:S(2)}, u32[]{:S(2)}) async-start(bf16[16,32,384]{2,1,0:T(8,128)(2,1)} %get-tuple-element.45), calls=%async_computation.1 | async-start | bytes 786432 | tf_op jit(solution)/shard_map/all_to_all | solution.py:296
  34.0 28.3 %collective-permute-start = (bf16[272,768]{1,0:T(8,128)(2,1)S(1)}, bf16[272,768]{1,0:T(8,128)(2,1)S(1)}, u32[]{:S(2)}, u32[]{:S(2)}) collective-permute-start(bf16[272,768]{1,0:T(8,128)(2,1)S(1)} %get-tuple-element.40), channel_id=1, source_target_pairs={{0,1},{1,0},{2,3},{3,2},{4,5},{5,4},{6,7},{7,6},{8,9},{9,8},{10,11... | collective-permute-start | bytes 1253384 | tf_op jit(solution)/shard_map/ppermute | solution.py:51
  36.1 26.2 %collective-permute-start.1 = (bf16[272,768]{1,0:T(8,128)(2,1)S(1)}, bf16[272,768]{1,0:T(8,128)(2,1)S(1)}, u32[]{:S(2)}, u32[]{:S(2)}) collective-permute-start(bf16[272,768]{1,0:T(8,128)(2,1)S(1)} %get-tuple-element.41), channel_id=1, source_target_pairs={{0,2},{1,3},{2,0},{3,1},{4,6},{5,7},{6,4},{7,5},{8,10},{9,11},{10,... | collective-permute-start | bytes 1253384 | tf_op jit(solution)/shard_map/ppermute | solution.py:51
  39.8 22.6 %collective-permute-start.2 = (bf16[272,768]{1,0:T(8,128)(2,1)S(1)}, bf16[272,768]{1,0:T(8,128)(2,1)S(1)}, u32[]{:S(2)}, u32[]{:S(2)}) collective-permute-start(bf16[272,768]{1,0:T(8,128)(2,1)S(1)} %get-tuple-element.42), channel_id=1, source_target_pairs={{0,3},{1,2},{2,1},{3,0},{4,7},{5,6},{6,5},{7,4},{8,11},{9,10},{10,... | collective-permute-start | bytes 1253384 | tf_op jit(solution)/shard_map/ppermute | solution.py:51
  48.3 13.2 %collective-permute-start.3 = (bf16[32,256]{1,0:T(8,128)(2,1)S(1)}, bf16[32,256]{1,0:T(8,128)(2,1)S(1)}, u32[]{:S(2)}, u32[]{:S(2)}) collective-permute-start(bf16[32,256]{1,0:T(8,128)(2,1)S(1)} %dynamic-slice_bitcast_fusion), channel_id=1, source_target_pairs={{0,4},{1,5},{2,6},{3,7},{4,0},{5,1},{6,2},{7,3},{8,12},{9,13},{10,... | collective-permute-start | bytes 49160 | tf_op jit(solution)/shard_map/ppermute | solution.py:51
  63.5 68.9 %all-to-all-start.2 = ((bf16[4,16,32,256]{3,2,1,0:T(8,128)(2,1)}), bf16[4,16,32,256]{3,2,1,0:T(8,128)(2,1)S(1)}, u32[]{:S(2)}, u32[]{:S(2)}) async-start(bf16[4,16,32,256]{3,2,1,0:T(8,128)(2,1)} %broadcast_in_dim.29), calls=%async_computation.2 | async-start | bytes 2097152 | tf_op jit(solution)/shard_map/all_to_all | solution.py:309
  69.3 29.9 %collective-permute-start.5 = (bf16[32,256]{1,0:T(8,128)(2,1)S(1)}, bf16[32,256]{1,0:T(8,128)(2,1)S(1)}, u32[]{:S(2)}, u32[]{:S(2)}) collective-permute-start(bf16[32,256]{1,0:T(8,128)(2,1)S(1)} %broadcast_select_fusion), channel_id=1, source_target_pairs={{0,256},{1,257},{2,258},{3,259},{4,260},{5,261},{6,262},{7,263},{8... | collective-permute-start | bytes 49160 | tf_op jit(solution)/shard_map/ppermute | solution.py:51
  76.6 24.6 %copy-start.11 = (bf16[128,768]{1,0:T(8,128)(2,1)S(1)}, bf16[128,768]{1,0:T(8,128)(2,1)}, u32[]{:S(2)}) copy-start(bf16[128,768]{1,0:T(8,128)(2,1)} %copy-done.10) | copy-start | bytes 589828
  76.6 26.5 %copy-start.9 = (bf16[128,768]{1,0:T(8,128)(2,1)S(1)}, bf16[128,768]{1,0:T(8,128)(2,1)}, u32[]{:S(2)}) copy-start(bf16[128,768]{1,0:T(8,128)(2,1)} %copy-done.8) | copy-start | bytes 589828
  76.6 31.3 %copy-start.7 = (bf16[128,768]{1,0:T(8,128)(2,1)S(1)}, bf16[128,768]{1,0:T(8,128)(2,1)}, u32[]{:S(2)}) copy-start(bf16[128,768]{1,0:T(8,128)(2,1)} %copy-done.6) | copy-start | bytes 589828
  77.4 55.0 %collective-permute-start.4 = (bf16[2,256,768]{2,1,0:T(8,128)(2,1)S(1)}, bf16[2,256,768]{2,1,0:T(8,128)(2,1)}, u32[]{:S(2)}, u32[]{:S(2)}) collective-permute-start(bf16[2,256,768]{2,1,0:T(8,128)(2,1)S(1)} %halo_kernel.1), channel_id=1, source_target_pairs={{0,256},{1,257},{2,258},{3,259},{4,260},{5,261},{6,262},{7,263},{8... | collective-permute-start | bytes 2359304 | tf_op jit(solution)/shard_map/ppermute | solution.py:304
  99.2 21.4 %collective-permute-start.6 = (bf16[64,256]{1,0:T(8,128)(2,1)S(1)}, bf16[64,256]{1,0:T(8,128)(2,1)S(1)}, u32[]{:S(2)}, u32[]{:S(2)}) collective-permute-start(bf16[64,256]{1,0:T(8,128)(2,1)S(1)} %pad_maximum_fusion.2), channel_id=1, source_target_pairs={{0,128},{1,129},{2,130},{3,131},{4,132},{5,133},{6,134},{7,135},{8... | collective-permute-start | bytes 98312 | tf_op jit(solution)/shard_map/ppermute | solution.py:51
  101.2 29.1 %collective-permute-start.9 = (bf16[128,768]{1,0:T(8,128)(2,1)S(1)}, bf16[128,768]{1,0:T(8,128)(2,1)S(1)}, u32[]{:S(2)}, u32[]{:S(2)}) collective-permute-start(bf16[128,768]{1,0:T(8,128)(2,1)S(1)} %copy-done.11), channel_id=1, source_target_pairs={{0,1},{1,0},{2,3},{3,2},{4,5},{5,4},{6,7},{7,6},{8,9},{9,8},{10,11... | collective-permute-start | bytes 589832 | tf_op jit(solution)/shard_map/ppermute | solution.py:51
  103.1 27.9 %collective-permute-start.10 = (bf16[128,768]{1,0:T(8,128)(2,1)S(1)}, bf16[128,768]{1,0:T(8,128)(2,1)S(1)}, u32[]{:S(2)}, u32[]{:S(2)}) collective-permute-start(bf16[128,768]{1,0:T(8,128)(2,1)S(1)} %copy-done.9), channel_id=1, source_target_pairs={{0,2},{1,3},{2,0},{3,1},{4,6},{5,7},{6,4},{7,5},{8,10},{9,11},{10,... | collective-permute-start | bytes 589832 | tf_op jit(solution)/shard_map/ppermute | solution.py:51
  108.0 23.7 %collective-permute-start.11 = (bf16[128,768]{1,0:T(8,128)(2,1)S(1)}, bf16[128,768]{1,0:T(8,128)(2,1)S(1)}, u32[]{:S(2)}, u32[]{:S(2)}) collective-permute-start(bf16[128,768]{1,0:T(8,128)(2,1)S(1)} %copy-done.7), channel_id=1, source_target_pairs={{0,3},{1,2},{2,1},{3,0},{4,7},{5,6},{6,5},{7,4},{8,11},{9,10},{10,... | collective-permute-start | bytes 589832 | tf_op jit(solution)/shard_map/ppermute | solution.py:51
  120.6 5.8 %collective-permute-start.7 = (bf16[128,256]{1,0:T(8,128)(2,1)S(1)}, bf16[128,256]{1,0:T(8,128)(2,1)S(1)}, u32[]{:S(2)}, u32[]{:S(2)}) collective-permute-start(bf16[128,256]{1,0:T(8,128)(2,1)S(1)} %pad_maximum_fusion.1), channel_id=1, source_target_pairs={{0,64},{1,65},{2,66},{3,67},{4,68},{5,69},{6,70},{7,71},{8,72},{9,... | collective-permute-start | bytes 196616 | tf_op jit(solution)/shard_map/ppermute | solution.py:51
  126.4 3.9 %collective-permute-start.8 = (bf16[256,256]{1,0:T(8,128)(2,1)S(1)}, bf16[256,256]{1,0:T(8,128)(2,1)S(1)}, u32[]{:S(2)}, u32[]{:S(2)}) collective-permute-start(bf16[256,256]{1,0:T(8,128)(2,1)S(1)} %pad_maximum_fusion), channel_id=1, source_target_pairs={{0,32},{1,33},{2,34},{3,35},{4,36},{5,37},{6,38},{7,39},{8,40},{9,... | collective-permute-start | bytes 393224 | tf_op jit(solution)/shard_map/ppermute | solution.py:51
  135.5 62.3 %all-to-all-start.3 = ((bf16[16,32,256]{2,1,0:T(8,128)(2,1)}), bf16[16,32,256]{2,1,0:T(8,128)(2,1)S(1)}, u32[]{:S(2)}, u32[]{:S(2)}) async-start(bf16[16,32,256]{2,1,0:T(8,128)(2,1)} %far_kernel.1), calls=%async_computation.3 | async-start | bytes 524288 | tf_op jit(solution)/shard_map/all_to_all | solution.py:316
  143.3 54.5 %collective-permute-start.12 = (bf16[2,256,768]{2,1,0:T(8,128)(2,1)}, bf16[2,256,768]{2,1,0:T(8,128)(2,1)S(1)}, u32[]{:S(2)}, u32[]{:S(2)}) collective-permute-start(bf16[2,256,768]{2,1,0:T(8,128)(2,1)} %collective-permute-done.4), channel_id=1, source_target_pairs={{256,4},{257,5},{258,6},{259,7},{260,8},{261,9},{262,10},{263,11},... | collective-permute-start | bytes 2359304 | tf_op jit(solution)/shard_map/ppermute | solution.py:314
  153.4 15.4 %collective-permute-start.15 = (bf16[512,256]{1,0:T(8,128)(2,1)S(1)}, bf16[512,256]{1,0:T(8,128)(2,1)S(1)}, u32[]{:S(2)}, u32[]{:S(2)}) collective-permute-start(bf16[512,256]{1,0:T(8,128)(2,1)S(1)} %constant_dynamic-update-slice_fusion.f0), channel_id=1, source_target_pairs={{0,24},{1,25},{2,26},{3,27},{4,28},{5,29},{6,30},{7,31},{8,16},{9,... | collective-permute-start | bytes 786440 | tf_op jit(solution)/shard_map/ppermute | solution.py:51
  156.0 12.8 %collective-permute-start.14 = (bf16[512,256]{1,0:T(8,128)(2,1)S(1)}, bf16[512,256]{1,0:T(8,128)(2,1)}, u32[]{:S(2)}, u32[]{:S(2)}) collective-permute-start(bf16[512,256]{1,0:T(8,128)(2,1)S(1)} %constant_dynamic-update-slice_fusion.f0), channel_id=1, source_target_pairs={{0,16},{1,17},{2,18},{3,19},{4,20},{5,21},{6,22},{7,23},{8,24},{9,... | collective-permute-start | bytes 786440 | tf_op jit(solution)/shard_map/ppermute | solution.py:51
  160.5 12.7 %collective-permute-start.13 = (bf16[512,256]{1,0:T(8,128)(2,1)S(1)}, bf16[512,256]{1,0:T(8,128)(2,1)}, u32[]{:S(2)}, u32[]{:S(2)}) collective-permute-start(bf16[512,256]{1,0:T(8,128)(2,1)S(1)} %constant_dynamic-update-slice_fusion.f0), channel_id=1, source_target_pairs={{0,8},{1,9},{2,10},{3,11},{4,12},{5,13},{6,14},{7,15},{8,0},{9,1},... | collective-permute-start | bytes 786440 | tf_op jit(solution)/shard_map/ppermute | solution.py:51
  (15 other events, 21.7 us)

commit v3 on v2

--- a/solution.py
+++ b/solution.py
@@ -24,7 +24,7 @@
 ROWS = 2 * BLOCK + 16
 MARK = 128.0
 NEG = -1e30
-LEGS = (4, 4)
+LEGS = (2, 2, 4)
 LEAST = -1e4
 SCALE = 1.0 / (math.sqrt(DIM) * math.log(2.0))
 f32, bf16 = jnp.float32, jnp.bfloat16
@@ -105,9 +105,22 @@
     return slice(head * DIM, (head + 1) * DIM)
 
 
-def pack_kernel(info, keep_row, keep_col, q, k, v, s1, f1, *outs):
-    pieces, queries = outs[:YS], outs[YS:]
-    keep = jnp.broadcast_to(keep_col[...] > 0, (BLOCK, DIM))
+def fetch(pairs, sems):
+    copies = [pltpu.make_async_copy(a, b, sems.at[n]) for n, (a, b) in enumerate(pairs)]
+    for copy in copies:
+        copy.start()
+    for copy in copies:
+        copy.wait()
+
+
+def keep_of(row):
+    return jnp.transpose(jnp.broadcast_to(row.astype(f32), (BLOCK, DIM))) > 0.5
+
+
+def pack_kernel(info, keep_row, q_in, k_in, v_in, s1, f1, *outs):
+    pieces, queries, (q, k, v, sems) = outs[:YS], outs[YS : 2 * YS], outs[2 * YS :]
+    fetch([(q_in, q), (k_in, k), (v_in, v)], sems)
+    keep = keep_of(keep_row[...])
     for h in range(YS):
         c = column(LOCAL + YS + h)
         key = jnp.where(keep, k[:, c], jnp.array(MARK, bf16))
@@ -136,16 +149,15 @@
                     queries[d][:, to] = q[:, column(h)]
 
 
-def halo_kernel(info, *refs):
-    out = refs[-1]
+def halo_kernel(info, r0, r1, r2, r3, out):
+    refs = (r0, r1, r2, r3)
     for here in range(YS):
 
         @pl.when(info[1] == here)
         def _():
             for i in range(2):
                 ref = refs[here ^ (2 + i)]
-                row = ref[2 * BLOCK : 2 * BLOCK + 1, 0:BLOCK].astype(f32)
-                keep = jnp.transpose(jnp.broadcast_to(row, (BLOCK, BLOCK))) > 0.5
+                keep = keep_of(ref[2 * BLOCK : 2 * BLOCK + 1, 0:BLOCK])
                 for h in range(MINE):
                     c = column(h)
                     out[i, 0:BLOCK, c] = jnp.where(keep, ref[0:BLOCK, c], jnp.array(MARK, bf16))
@@ -179,22 +191,23 @@
         out[t * windows : (t + 1) * windows] = both.reshape(windows, PART, 2 * DIM)
 
 
-def attend_kernel(info, fixed_ok, p0, p1, p2, p3, q0, q1, q2, q3, halo, f0, f1, f2, f3, out, kv, q):
-    for d, (piece, query) in enumerate(zip((p0, p1, p2, p3), (q0, q1, q2, q3))):
-        kv[info[1] ^ d] = piece[...]
-        q[info[1] ^ d] = query[...]
-    summary = (f0, f1, f2, f3)
+def attend(info, work, kv, q, halo, summary, fixed_ok, out, first=0):
     rows = lax.broadcasted_iota(jnp.int32, (BLOCK, BLOCK), 0)
     cols = lax.broadcasted_iota(jnp.int32, (BLOCK, BLOCK), 1)
     keeps = [kv[j, 2 * BLOCK : 2 * BLOCK + 1, 0:BLOCK].astype(f32) > 0.5 for j in range(YS)]
-    halo_keeps = [unmarked(halo[i, 0:BLOCK, 0:DIM]) & (info[0] > 0) for i in range(2)]
     far_flags = [unmarked(f[:, 0:DIM]) for f in summary]
+    if halo is not None:
+        halo_keeps = [unmarked(halo[i, 0:BLOCK, 0:DIM]) & (info[0] > 0) for i in range(2)]
     for j in range(YS):
+        heads = [h for jj, h in work if jj == j]
+        if not heads:
+            continue
         masks = [((cols <= rows) & jnp.broadcast_to(keeps[j], (BLOCK, BLOCK))) | (cols == rows)]
         for back in (1, 2):
             flag = keeps[j - back] if j >= back else halo_keeps[2 + j - back]
             masks.append(jnp.broadcast_to(flag, (BLOCK, BLOCK)))
-        for h in range(MINE):
+        all_scores, all_values = [], []
+        for h in heads:
             c = column(h)
             query = q[j, :, c]
             scores, values = [], []
@@ -208,22 +221,57 @@
                     s = qk(query, f[:, 0:DIM]) * SCALE
                     scores.append(jnp.where(jnp.broadcast_to(ok, s.shape), s, NEG))
                     values.append(f[:, DIM : 2 * DIM])
+            all_scores.append(scores)
+            all_values.append(values)
+        tops = []
+        for h, scores in zip(heads, all_scores):
             top = jnp.max(jnp.maximum(jnp.maximum(scores[0], scores[1]), scores[2]), axis=1, keepdims=True)
             for s in scores[3:]:
                 top = jnp.maximum(top, jnp.max(s, axis=1, keepdims=True))
-            if h == PER + 1:
-                top = top.astype(bf16).astype(f32)
-            weights = [jnp.exp2(s - top) for s in scores]
+            tops.append(top.astype(bf16).astype(f32) if h == PER + 1 else top)
+        all_weights = [[jnp.exp2(s - top) for s in scores] for scores, top in zip(all_scores, tops)]
+        totals, accs = [], []
+        for weights, values in zip(all_weights, all_values):
             total = jnp.sum(weights[0] + weights[1] + weights[2], axis=1, keepdims=True)
             acc = pv(weights[0], values[0]) + pv(weights[1], values[1]) + pv(weights[2], values[2])
             for w, v in zip(weights[3:], values[3:]):
                 total = total + jnp.sum(w, axis=1, keepdims=True)
                 acc = acc + pv(w, v)
+            totals.append(total)
+            accs.append(acc)
+        for h, top, total, acc in zip(heads, tops, totals, accs):
+            c = column(h)
             if h == PER + 1:
-                out[j, :, c] = acc.astype(bf16)
-                out[j, :, column(h + 1)] = stats_of(top, total, (BLOCK, DIM))
+                out[j - first, :, c] = acc.astype(bf16)
+                out[j - first, :, column(h + 1)] = stats_of(top, total, (BLOCK, DIM))
             else:
-                out[j, :, c] = (acc / total).astype(bf16)
+                out[j - first, :, c] = (acc / total).astype(bf16)
+
+
+def by_block(info, pieces, queries, kv, q):
+    here = info[1]
+    return [(a, kv.at[here ^ d]) for d, a in enumerate(pieces)] + [(a, q.at[here ^ d]) for d, a in enumerate(queries)]
+
+
+EARLY = [(j, h) for j in (2, 3) for h in range(MINE)]
+LATE = [(j, h) for j in (0, 1) for h in range(MINE)]
+
+
+def gather(info, p, q_in, f_in, kv, q, f, sems):
+    pairs = by_block(info, p, q_in, kv, q) + [(a, f.at[d]) for d, a in enumerate(f_in)]
+    fetch(pairs, sems)
+    return [f.at[d] for d in range(XS)]
+
+
+def early_kernel(info, fixed_ok, p0, p1, p2, p3, q0, q1, q2, q3, f0, f1, f2, f3, out, kv, q, f, sems):
+    summary = gather(info, (p0, p1, p2, p3), (q0, q1, q2, q3), (f0, f1, f2, f3), kv, q, f, sems)
+    attend(info, EARLY, kv, q, None, summary, fixed_ok, out, first=2)
+
+
+def late_kernel(info, fixed_ok, halo, early, p0, p1, p2, p3, q0, q1, q2, q3, f0, f1, f2, f3, out, kv, q, f, sems):
+    summary = gather(info, (p0, p1, p2, p3), (q0, q1, q2, q3), (f0, f1, f2, f3), kv, q, f, sems)
+    attend(info, LATE, kv, q, halo, summary, fixed_ok, out)
+    out[2:YS] = early[...]
 
 
 def merge_kernel(back, far, out):
@@ -246,24 +294,26 @@
 SMEM = pl.BlockSpec(memory_space=pltpu.SMEM)
 
 
-def call(kernel, shapes, flops, operands, scratch=()):
+ANY = pl.BlockSpec(memory_space=pl.ANY)
+
+
+def call(kernel, shapes, flops, operands, scratch=(), left=0):
     many = isinstance(shapes, list)
     moved = sum(o.size * o.dtype.itemsize for o in operands)
     outs = [jax.ShapeDtypeStruct(s, bf16) for s in shapes] if many else jax.ShapeDtypeStruct(shapes, bf16)
     return pl.pallas_call(
         kernel,
         out_shape=outs,
-        in_specs=[SMEM if o.ndim == 1 else VMEM for o in operands],
+        in_specs=[SMEM if o.ndim == 1 else VMEM for o in operands[: len(operands) - left]] + [ANY] * left,
         out_specs=[VMEM] * len(shapes) if many else VMEM,
         scratch_shapes=scratch,
-        compiler_params=pltpu.CompilerParams(vmem_limit_bytes=40 << 20),
+        compiler_params=pltpu.CompilerParams(vmem_limit_bytes=(58 if left else 40) << 20),
         cost_estimate=pl.CostEstimate(flops=flops, bytes_accessed=moved, transcendentals=0),
         name=kernel.__name__,
     )(*operands)
 
 
 tie = lax.optimization_barrier
-DOUBLING = (("zp", 2, 8), ("zp", 1, 4), ("zq", 1, 2), ("core", 1, 1))
 
 
 def on_device(queries, key_states, value_states, key_keep, summary_pos):
@@ -273,57 +323,58 @@
     info = jnp.stack([(group > 0).astype(jnp.int32), y.astype(jnp.int32)])
 
     windows = jnp.arange(WINDOWS, dtype=jnp.int32)
-    masks = [0]
-    for _, bit, mask in DOUBLING:
-        masks += [m ^ mask for m in masks]
-    order = window ^ jnp.array(masks, jnp.int32)
-    where = jnp.sum(jnp.where(order[:, None] == windows[None, :], summary_pos[None, :], 0), axis=1)
     block_ids = group * YS + jnp.arange(YS, dtype=jnp.int32)
-    fixed_ok = (order * (XS * ZH * YS) + where)[None, :] < block_ids[:, None] - 2
+    fixed_ok = (windows * (XS * ZH * YS) + summary_pos)[None, :] < block_ids[:, None] - 2
     fixed_ok = jnp.repeat(fixed_ok.astype(f32), PART, axis=1)
 
     shapes = [(WINDOWS, PART, 3 * DIM), (XS * YS, PART, 2 * DIM)] + [(ROWS, WIDE)] * YS + [(BLOCK, WIDE)] * YS
-    keep_row, keep_col = key_keep.reshape(1, BLOCK), key_keep.reshape(BLOCK, 1)
-    packed = call(pack_kernel, shapes, 10**6, [info, keep_row, keep_col, queries, key_states, value_states])
+    wide = pltpu.VMEM((BLOCK, HEADS * DIM), bf16)
+    scratch = [wide, wide, wide, pltpu.SemaphoreType.DMA((3,))]
+    rows = [info, key_keep.reshape(1, BLOCK), queries, key_states, value_states]
+    packed = call(pack_kernel, shapes, 10**6, rows, scratch, left=3)
     s1, f1, pieces, asked = packed[0], packed[1], packed[2 : 2 + YS], packed[2 + YS :]
-
-    root = summary_pos[window]
-    at = root // (ZH * YS) * YS + root % YS
+    root = jnp.sum(jnp.where(windows == window, summary_pos, 0))
+    slot = jnp.arange(XS * YS, dtype=jnp.int32) == root // (ZH * YS) * YS + root % YS
     here = zh == root // YS % ZH
+
     got = [pieces[0]] + [send(pieces[d], flip("y", d)) for d in range(1, YS)]
     parts = lax.all_to_all(f1, ("x", "y"), 0, 0)
     parts, s1 = tie((parts, s1))
     part = lax.all_to_all(s1, GRP, 0, 0)
-    piece = lax.dynamic_index_in_dim(parts, at, 0, keepdims=False)
+    piece = jnp.sum(jnp.where(slot[:, None, None], parts, 0).astype(f32), axis=0).astype(bf16)
     twin = send(piece, flip("zh", 1))
     spread = jnp.where(here, piece, twin)
-    got1, got2, got3, part, spread, asked = tie((got[1], got[2], got[3], part, spread, asked))
+    got1, got2, got3, part, spread = tie((got[1], got[2], got[3], part, spread))
     got = [got[0], got1, got2, got3]
-    halo = call(halo_kernel, (2, 2 * BLOCK, WIDE), 10**6, [info] + got)
-    for n in range(len(LEGS) // 2):
-        halo = lax.ppermute(halo, AXES, leg(n))
-
-    for axis, bit, _ in DOUBLING:
-        spread = jnp.concatenate([spread, send(spread, flip(axis, bit))])
+
     quarter = jnp.broadcast_to(part[None, :, :, : 2 * DIM], (YS, WINDOWS, PART, 2 * DIM))
     quarters = lax.all_to_all(quarter, ("zq", "core"), 0, 0)
+    halo = call(halo_kernel, (2, 2 * BLOCK, WIDE), 10**6, [info] + got)
+    halo = lax.ppermute(halo, AXES, leg(0))
+    halo, quarters, spread = tie((halo, quarters, spread))
+    halo = lax.ppermute(halo, AXES, leg(1))
+    spread = jnp.broadcast_to(spread[None], (WINDOWS,) + spread.shape)
+    spread = lax.all_to_all(spread, GRP, 0, 0).reshape(-1, 2 * DIM)
+    part, halo = tie((part, halo))
+    far = call(far_kernel, (WINDOWS, PART, 2 * DIM), 10**10, [part, quarters])
+    halo, far, spread, asked = tie((halo, far, spread, asked))
+
+    halo = lax.ppermute(halo, AXES, leg(2))
     asked = [asked[0]] + [send(asked[d], flip("y", d)) for d in range(1, YS)]
-    halo, quarters, spread, asked = tie((halo, quarters, spread, asked))
-
-    for n in range(len(LEGS) // 2, len(LEGS)):
-        halo = lax.ppermute(halo, AXES, leg(n))
-    far = call(far_kernel, (WINDOWS, PART, 2 * DIM), 10**9, [part, quarters])
+    scratch = [
+        pltpu.VMEM((YS, ROWS, WIDE), bf16),
+        pltpu.VMEM((YS, BLOCK, WIDE), bf16),
+        pltpu.VMEM((XS, WINDOWS * PART, 2 * DIM), bf16),
+        pltpu.SemaphoreType.DMA((2 * YS + XS,)),
+    ]
+    shape = (YS, BLOCK, WIDE + DIM)
     far = lax.all_to_all(far, GRP, 0, 0).reshape(YS, BLOCK, 2 * DIM)
     summary = [spread] + [send(spread, flip("x", d)) for d in range(1, XS)]
-    halo, far, summary = tie((halo, far, summary))
-
-    out = call(
-        attend_kernel,
-        (YS, BLOCK, WIDE + DIM),
-        2 * 10**9,
-        [info, fixed_ok] + got + asked + [halo] + summary,
-        [pltpu.VMEM((YS, ROWS, WIDE), bf16), pltpu.VMEM((YS, BLOCK, WIDE), bf16)],
-    )
+    rest = got + asked + summary
+    early = call(early_kernel, (2,) + shape[1:], 3 * 10**8, [info, fixed_ok] + rest, scratch, left=len(rest))
+    halo, early = tie((halo, early))
+    out = call(late_kernel, shape, 10**10, [info, fixed_ok, halo, early] + rest, scratch, left=len(rest))
+    out, far = tie((out, far))
     back = lax.all_to_all(out, "y", 0, 0)
     return call(merge_kernel, queries.shape, 10**6, [back, far])
 

time: 229 us -> 215 us (0.939)
  the two profiles are of different devices: /device:TPU:67 before, /device:TPU:1 now
where the time goes in v3:
time: 215 us; the launch traced here: 213 us
  starting transfers between devices  106 us (49%)
  waiting for transfers between devices  41.3 us (19%)
  blocking collectives  32.1 us (15%)
  Pallas kernels  22.6 us (11%)
  local copies, waits for them, and re-layouts  5.68 us (3%)
  between operations  3.07 us (1%)
    ppermute x10, starting transfers between devices, send(): return lax.ppermute(value, AXES, route(move))  36.1 us
    pallas_call x6, Pallas kernels, call(): pl.pallas_call(kernel, out_shape=outs, in_specs=[SMEM if o.ndim == 1 else...  22.6 us
    all_to_all x1, starting transfers between devices, on_device(): spread = lax.all_to_all(spread, GRP, 0, 0).reshape(-1, 2 * DIM)  21.7 us
    all_to_all x1, blocking collectives, on_device(): back = lax.all_to_all(out, 'y', 0, 0)  17 us
    all_to_all x1, blocking collectives, on_device(): parts = lax.all_to_all(f1, ('x', 'y'), 0, 0)  15.1 us
    all_to_all x1, starting transfers between devices, on_device(): part = lax.all_to_all(s1, GRP, 0, 0)  14.7 us
    all_to_all x1, waiting for transfers between devices, on_device(): spread = lax.all_to_all(spread, GRP, 0, 0).reshape(-1, 2 * DIM)  13.8 us
    ppermute x10, waiting for transfers between devices, send(): return lax.ppermute(value, AXES, route(move))  13.4 us
  transfers between devices with their start and end apart: 17, of which 7 were waited for; matrix products, arithmetic and copies ran while one was open for 1% of the time, Pallas kernels for 8%

profile of v3, /device:TPU:1, one launch (start us, length us, event | category | flops | bytes accessed | tf_op | source)
XLA Modules:
  0.0 212.7 jit_solution(2514631609086810676)
XLA Ops:
  0.6 4.4 %pack_kernel.1 = (bf16[16,32,384]{2,1,0:T(8,128)(2,1)}, bf16[16,32,256]{2,1,0:T(8,128)(2,1)}, bf16[272,768]{1,0:T(8,128)(2,1)}, bf16[272,768]{1,0:T(8,128)(2,1)}...) custom-call(s32[2]{0:T(128)} %pad_add_fusion.info, ...), custom_call_target="tpu_custom_call" | custom-call | flops 1000000 | bytes 2359816 | tf_op jit(solution)/shard_map/pack_kernel/pallas_call | solution.py:304
  5.0 15.1 %all_to_all.30 = bf16[16,32,256]{2,1,0:T(8,128)(2,1)S(1)} all-to-all(bf16[16,32,256]{2,1,0:T(8,128)(2,1)} %get-tuple-element.41), channel_id=1, replica_groups=mesh['zp'=4,'zq'=2,'core'=2,'x'=4,'zh'=2,'y'=4] {'x','y'}, dimensions={0} | all-to-all | bytes 524288 | tf_op jit(solution)/shard_map/all_to_all | solution.py:341
  20.1 14.7 %all-to-all-start.1 = ((bf16[16,32,384]{2,1,0:T(8,128)(2,1)}), bf16[16,32,384]{2,1,0:T(8,128)(2,1)S(1)}, u32[]{:S(2)}, u32[]{:S(2)}) async-start(bf16[16,32,384]{2,1,0:T(8,128)(2,1)} %get-tuple-element.43), calls=%async_computation.1 | async-start | bytes 786432 | tf_op jit(solution)/shard_map/all_to_all | solution.py:343
  37.1 3.5 %collective-permute-start.1 = (bf16[272,768]{1,0:T(8,128)(2,1)S(1)}, bf16[272,768]{1,0:T(8,128)(2,1)S(1)}, u32[]{:S(2)}, u32[]{:S(2)}) collective-permute-start(bf16[272,768]{1,0:T(8,128)(2,1)S(1)} %copy-done.15), channel_id=1, source_target_pairs={{0,2},{1,3},{2,0},{3,1},{4,6},{5,7},{6,4},{7,5},{8,10},{9,11},{10,... | collective-permute-start | bytes 1253384 | tf_op jit(solution)/shard_map/ppermute | solution.py:51
  40.6 3.9 %collective-permute-start.2 = (bf16[272,768]{1,0:T(8,128)(2,1)S(1)}, bf16[272,768]{1,0:T(8,128)(2,1)S(1)}, u32[]{:S(2)}, u32[]{:S(2)}) collective-permute-start(bf16[272,768]{1,0:T(8,128)(2,1)S(1)} %copy-done.14), channel_id=1, source_target_pairs={{0,3},{1,2},{2,1},{3,0},{4,7},{5,6},{6,5},{7,4},{8,11},{9,10},{10,... | collective-permute-start | bytes 1253384 | tf_op jit(solution)/shard_map/ppermute | solution.py:51
  47.9 7.9 %collective-permute-start.3 = (bf16[32,256]{1,0:T(8,128)(2,1)S(1)}, bf16[32,256]{1,0:T(8,128)(2,1)S(1)}, u32[]{:S(2)}, u32[]{:S(2)}) collective-permute-start(bf16[32,256]{1,0:T(8,128)(2,1)S(1)} %select_reduce_fusion), channel_id=1, source_target_pairs={{0,4},{1,5},{2,6},{3,7},{4,0},{5,1},{6,2},{7,3},{8,12},{9,13},{10,... | collective-permute-start | bytes 49160 | tf_op jit(solution)/shard_map/ppermute | solution.py:51
  55.9 5.2 %collective-permute-done.3 = bf16[32,256]{1,0:T(8,128)(2,1)S(1)} collective-permute-done((bf16[32,256]{1,0:T(8,128)(2,1)S(1)}, bf16[32,256]{1,0:T(8,128)(2,1)S(1)}, u32[]{:S(2)}, u32[]{:S(2)}) %collective-permute-start.3) | collective-permute-done | bytes 16416 | tf_op jit(solution)/shard_map/ppermute | solution.py:51
  64.4 5.1 %all-to-all-start.2 = ((bf16[4,16,32,256]{3,2,1,0:T(8,128)(2,1)}), bf16[4,16,32,256]{3,2,1,0:T(8,128)(2,1)S(1)}, u32[]{:S(2)}, u32[]{:S(2)}) async-start(bf16[4,16,32,256]{3,2,1,0:T(8,128)(2,1)} %broadcast_in_dim.38), calls=%async_computation.2 | async-start | bytes 2097152 | tf_op jit(solution)/shard_map/all_to_all | solution.py:351
  70.8 8.1 %collective-permute-start.4 = (bf16[2,256,768]{2,1,0:T(8,128)(2,1)S(1)}, bf16[2,256,768]{2,1,0:T(8,128)(2,1)}, u32[]{:S(2)}, u32[]{:S(2)}) collective-permute-start(bf16[2,256,768]{2,1,0:T(8,128)(2,1)S(1)} %halo_kernel.1), channel_id=1, source_target_pairs={{0,128},{1,129},{2,130},{3,131},{4,132},{5,133},{6,134},{7,135},{8... | collective-permute-start | bytes 2359304 | tf_op jit(solution)/shard_map/ppermute | solution.py:353
  78.9 9.0 %collective-permute-done.4 = bf16[2,256,768]{2,1,0:T(8,128)(2,1)} collective-permute-done((bf16[2,256,768]{2,1,0:T(8,128)(2,1)S(1)}, bf16[2,256,768]{2,1,0:T(8,128)(2,1)}, u32[]{:S(2)}, u32[]{:S(2)}) %collective-permute-start.4) | collective-permute-done | bytes 786464 | tf_op jit(solution)/shard_map/ppermute | solution.py:353
  87.9 3.6 %all-to-all-done.2.keys_values = bf16[4,16,32,256]{3,2,1,0:T(8,128)(2,1)S(1)} async-done(((bf16[4,16,32,256]{3,2,1,0:T(8,128)(2,1)}), bf16[4,16,32,256]{3,2,1,0:T(8,128)(2,1)S(1)}, u32[]{:S(2)}, u32[]{:S(2)}) %all-to-all-start.2) | async-done | bytes 1048608 | tf_op jit(solution)/shard_map/all_to_all | solution.py:351
  91.5 8.2 %collective-permute-start.5 = (bf16[2,256,768]{2,1,0:T(8,128)(2,1)}, bf16[2,256,768]{2,1,0:T(8,128)(2,1)}, u32[]{:S(2)}, u32[]{:S(2)}) collective-permute-start(bf16[2,256,768]{2,1,0:T(8,128)(2,1)} %collective-permute-done.4), channel_id=1, source_target_pairs={{128,256},{129,257},{130,258},{131,259},{132,260},{133,261},{134,2... | collective-permute-start | bytes 2359304 | tf_op jit(solution)/shard_map/ppermute | solution.py:355
  100.5 21.7 %all-to-all-start.3 = ((bf16[16,32,256]{2,1,0:T(8,128)(2,1)}), bf16[16,32,256]{2,1,0:T(8,128)(2,1)S(1)}, u32[]{:S(2)}, u32[]{:S(2)}) async-start(bf16[16,32,256]{2,1,0:T(8,128)(2,1)} %broadcast_in_dim.39), calls=%async_computation.3 | async-start | bytes 524288 | tf_op jit(solution)/shard_map/all_to_all | solution.py:357
  122.2 3.2 %far_kernel.1 = bf16[16,32,256]{2,1,0:T(8,128)(2,1)} custom-call(bf16[16,32,384]{2,1,0:T(8,128)(2,1)S(1)} %all-to-all-done.1.part, bf16[4,16,32,256]{3,2,1,0:T(8,128)(2,1)S(1)} %all-to-all-done.2.keys_values), custom_call_target="tpu_custom_call" | custom-call | flops 10000000000 | bytes 1441792 | tf_op jit(solution)/shard_map/far_kernel/pallas_call | solution.py:304
  125.3 13.8 %all-to-all-done.3 = bf16[16,32,256]{2,1,0:T(8,128)(2,1)S(1)} async-done(((bf16[16,32,256]{2,1,0:T(8,128)(2,1)}), bf16[16,32,256]{2,1,0:T(8,128)(2,1)S(1)}, u32[]{:S(2)}, u32[]{:S(2)}) %all-to-all-start.3) | async-done | bytes 262176 | tf_op jit(solution)/shard_map/all_to_all | solution.py:357
  139.2 4.3 %collective-permute-start.6 = (bf16[2,256,768]{2,1,0:T(8,128)(2,1)}, bf16[2,256,768]{2,1,0:T(8,128)(2,1)S(1)}, u32[]{:S(2)}, u32[]{:S(2)}) collective-permute-start(bf16[2,256,768]{2,1,0:T(8,128)(2,1)} %collective-permute-done.5), channel_id=1, source_target_pairs={{256,4},{257,5},{258,6},{259,7},{260,8},{261,9},{262,10},{263,11},... | collective-permute-start | bytes 2359304 | tf_op jit(solution)/shard_map/ppermute | solution.py:362
  145.4 5.1 %collective-permute-start.8 = (bf16[128,768]{1,0:T(8,128)(2,1)S(1)}, bf16[128,768]{1,0:T(8,128)(2,1)S(1)}, u32[]{:S(2)}, u32[]{:S(2)}) collective-permute-start(bf16[128,768]{1,0:T(8,128)(2,1)S(1)} %copy-done.18), channel_id=1, source_target_pairs={{0,2},{1,3},{2,0},{3,1},{4,6},{5,7},{6,4},{7,5},{8,10},{9,11},{10,... | collective-permute-start | bytes 589832 | tf_op jit(solution)/shard_map/ppermute | solution.py:51
  152.6 3.5 %collective-permute-start.11 = (bf16[512,256]{1,0:T(8,128)(2,1)S(1)}, bf16[512,256]{1,0:T(8,128)(2,1)S(1)}, u32[]{:S(2)}, u32[]{:S(2)}) collective-permute-start(bf16[512,256]{1,0:T(8,128)(2,1)S(1)} %bitcast.7), channel_id=1, source_target_pairs={{0,16},{1,17},{2,18},{3,19},{4,20},{5,21},{6,22},{7,23},{8,24},{9,... | collective-permute-start | bytes 786440 | tf_op jit(solution)/shard_map/ppermute | solution.py:51
  156.1 3.4 %collective-permute-start.10 = (bf16[512,256]{1,0:T(8,128)(2,1)S(1)}, bf16[512,256]{1,0:T(8,128)(2,1)S(1)}, u32[]{:S(2)}, u32[]{:S(2)}) collective-permute-start(bf16[512,256]{1,0:T(8,128)(2,1)S(1)} %bitcast.8), channel_id=1, source_target_pairs={{0,8},{1,9},{2,10},{3,11},{4,12},{5,13},{6,14},{7,15},{8,0},{9,1},... | collective-permute-start | bytes 786440 | tf_op jit(solution)/shard_map/ppermute | solution.py:51
  159.6 8.1 %all-to-all-start.4 = ((bf16[16,32,256]{2,1,0:T(8,128)(2,1)}), bf16[16,32,256]{2,1,0:T(8,128)(2,1)S(1)}, u32[]{:S(2)}, u32[]{:S(2)}) async-start(bf16[16,32,256]{2,1,0:T(8,128)(2,1)} %far_kernel.1), calls=%async_computation.4 | async-start | bytes 524288 | tf_op jit(solution)/shard_map/all_to_all | solution.py:371
  171.2 6.1 %collective-permute-done.9.q3 = bf16[128,768]{1,0:T(8,128)(2,1)S(1)} collective-permute-done((bf16[128,768]{1,0:T(8,128)(2,1)S(1)}, bf16[128,768]{1,0:T(8,128)(2,1)S(1)}, u32[]{:S(2)}, u32[]{:S(2)}) %collective-permute-start.9) | collective-permute-done | bytes 196640 | tf_op jit(solution)/shard_map/ppermute | solution.py:51
  178.9 5.9 %early_kernel.1.early = bf16[2,128,896]{2,1,0:T(8,128)(2,1)} custom-call(s32[2]{0:T(128)} %pad_add_fusion.info, f32[4,512]{1,0:T(4,128)} %reshape.25.fixed_ok, bf16[272,768]{1,0:T(8,128)(2,1)} %get-tuple-element.46.r0.p0, bf16[272,768]{1,0:T(8,128)(2,1)} %copy-done.1, bf16[272,768]{1,0:T(8,128)(2,1)} %copy-done.2, bf16[272,768]{1,0:T(8,128)(2,1)} %copy-done.3, ...), custom_call_target="tpu_custom_call" | custom-call | flops 300000000 | bytes 3514376 | tf_op jit(solution)/shard_map/early_kernel/pallas_call | solution.py:304
  187.2 6.7 %late_kernel.1 = bf16[4,128,896]{2,1,0:T(8,128)(2,1)} custom-call(s32[2]{0:T(128)} %pad_add_fusion.info, f32[4,512]{1,0:T(4,128)} %reshape.25.fixed_ok, bf16[2,256,768]{2,1,0:T(8,128)(2,1)} %copy-done.13, bf16[2,128,896]{2,1,0:T(8,128)(2,1)} %early_kernel.1.early, bf16[272,768]{1,0:T(8,128)(2,1)} %get-tuple-element.46.r0.p0, bf16[272,768]{1,0:T(8,128)(2,1)} %copy-done.1, ...), custom_call_target="tpu_custom_call" | custom-call | flops 10000000000 | bytes 4759560 | tf_op jit(solution)/shard_map/late_kernel/pallas_call | solution.py:304
  193.9 17.0 %all_to_all.31.back = bf16[4,128,896]{2,1,0:T(8,128)(2,1)S(1)} all-to-all(bf16[4,128,896]{2,1,0:T(8,128)(2,1)} %late_kernel.1), channel_id=1, replica_groups=mesh['zp'=4,'zq'=2,'core'=2,'x'=4,'zh'=2,'y'=4] {'y'}, dimensions={0} | all-to-all | bytes 1835008 | tf_op jit(solution)/shard_map/all_to_all | solution.py:378
  (70 shorter events, 21.9 us)
Async XLA Ops:
  5.0 29.9 %copy-start.16 = (bf16[272,768]{1,0:T(8,128)(2,1)S(1)}, bf16[272,768]{1,0:T(8,128)(2,1)}, u32[]{:S(2)}) copy-start(bf16[272,768]{1,0:T(8,128)(2,1)} %get-tuple-element.38) | copy-start | bytes 1253380
  5.0 32.0 %copy-start.15 = (bf16[272,768]{1,0:T(8,128)(2,1)S(1)}, bf16[272,768]{1,0:T(8,128)(2,1)}, u32[]{:S(2)}) copy-start(bf16[272,768]{1,0:T(8,128)(2,1)} %get-tuple-element.39) | copy-start | bytes 1253380
  20.1 20.5 %copy-start.14 = (bf16[272,768]{1,0:T(8,128)(2,1)S(1)}, bf16[272,768]{1,0:T(8,128)(2,1)}, u32[]{:S(2)}) copy-start(bf16[272,768]{1,0:T(8,128)(2,1)} %get-tuple-element.40) | copy-start | bytes 1253380
  20.1 43.1 %all-to-all-start.1 = ((bf16[16,32,384]{2,1,0:T(8,128)(2,1)}), bf16[16,32,384]{2,1,0:T(8,128)(2,1)S(1)}, u32[]{:S(2)}, u32[]{:S(2)}) async-start(bf16[16,32,384]{2,1,0:T(8,128)(2,1)} %get-tuple-element.43), calls=%async_computation.1 | async-start | bytes 786432 | tf_op jit(solution)/shard_map/all_to_all | solution.py:343
  34.9 26.2 %collective-permute-start = (bf16[272,768]{1,0:T(8,128)(2,1)S(1)}, bf16[272,768]{1,0:T(8,128)(2,1)S(1)}, u32[]{:S(2)}, u32[]{:S(2)}) collective-permute-start(bf16[272,768]{1,0:T(8,128)(2,1)S(1)} %copy-done.16), channel_id=1, source_target_pairs={{0,1},{1,0},{2,3},{3,2},{4,5},{5,4},{6,7},{7,6},{8,9},{9,8},{10,11... | collective-permute-start | bytes 1253384 | tf_op jit(solution)/shard_map/ppermute | solution.py:51
  37.1 24.1 %collective-permute-start.1 = (bf16[272,768]{1,0:T(8,128)(2,1)S(1)}, bf16[272,768]{1,0:T(8,128)(2,1)S(1)}, u32[]{:S(2)}, u32[]{:S(2)}) collective-permute-start(bf16[272,768]{1,0:T(8,128)(2,1)S(1)} %copy-done.15), channel_id=1, source_target_pairs={{0,2},{1,3},{2,0},{3,1},{4,6},{5,7},{6,4},{7,5},{8,10},{9,11},{10,... | collective-permute-start | bytes 1253384 | tf_op jit(solution)/shard_map/ppermute | solution.py:51
  40.6 22.6 %collective-permute-start.2 = (bf16[272,768]{1,0:T(8,128)(2,1)S(1)}, bf16[272,768]{1,0:T(8,128)(2,1)S(1)}, u32[]{:S(2)}, u32[]{:S(2)}) collective-permute-start(bf16[272,768]{1,0:T(8,128)(2,1)S(1)} %copy-done.14), channel_id=1, source_target_pairs={{0,3},{1,2},{2,1},{3,0},{4,7},{5,6},{6,5},{7,4},{8,11},{9,10},{10,... | collective-permute-start | bytes 1253384 | tf_op jit(solution)/shard_map/ppermute | solution.py:51
  47.9 13.2 %collective-permute-start.3 = (bf16[32,256]{1,0:T(8,128)(2,1)S(1)}, bf16[32,256]{1,0:T(8,128)(2,1)S(1)}, u32[]{:S(2)}, u32[]{:S(2)}) collective-permute-start(bf16[32,256]{1,0:T(8,128)(2,1)S(1)} %select_reduce_fusion), channel_id=1, source_target_pairs={{0,4},{1,5},{2,6},{3,7},{4,0},{5,1},{6,2},{7,3},{8,12},{9,13},{10,... | collective-permute-start | bytes 49160 | tf_op jit(solution)/shard_map/ppermute | solution.py:51
  64.4 27.1 %all-to-all-start.2 = ((bf16[4,16,32,256]{3,2,1,0:T(8,128)(2,1)}), bf16[4,16,32,256]{3,2,1,0:T(8,128)(2,1)S(1)}, u32[]{:S(2)}, u32[]{:S(2)}) async-start(bf16[4,16,32,256]{3,2,1,0:T(8,128)(2,1)} %broadcast_in_dim.38), calls=%async_computation.2 | async-start | bytes 2097152 | tf_op jit(solution)/shard_map/all_to_all | solution.py:351
  70.8 17.1 %collective-permute-start.4 = (bf16[2,256,768]{2,1,0:T(8,128)(2,1)S(1)}, bf16[2,256,768]{2,1,0:T(8,128)(2,1)}, u32[]{:S(2)}, u32[]{:S(2)}) collective-permute-start(bf16[2,256,768]{2,1,0:T(8,128)(2,1)S(1)} %halo_kernel.1), channel_id=1, source_target_pairs={{0,128},{1,129},{2,130},{3,131},{4,132},{5,133},{6,134},{7,135},{8... | collective-permute-start | bytes 2359304 | tf_op jit(solution)/shard_map/ppermute | solution.py:353
  91.5 30.7 %collective-permute-start.5 = (bf16[2,256,768]{2,1,0:T(8,128)(2,1)}, bf16[2,256,768]{2,1,0:T(8,128)(2,1)}, u32[]{:S(2)}, u32[]{:S(2)}) collective-permute-start(bf16[2,256,768]{2,1,0:T(8,128)(2,1)} %collective-permute-done.4), channel_id=1, source_target_pairs={{128,256},{129,257},{130,258},{131,259},{132,260},{133,261},{134,2... | collective-permute-start | bytes 2359304 | tf_op jit(solution)/shard_map/ppermute | solution.py:355
  100.5 38.7 %all-to-all-start.3 = ((bf16[16,32,256]{2,1,0:T(8,128)(2,1)}), bf16[16,32,256]{2,1,0:T(8,128)(2,1)S(1)}, u32[]{:S(2)}, u32[]{:S(2)}) async-start(bf16[16,32,256]{2,1,0:T(8,128)(2,1)} %broadcast_in_dim.39), calls=%async_computation.3 | async-start | bytes 524288 | tf_op jit(solution)/shard_map/all_to_all | solution.py:357
  122.2 21.3 %copy-start.19 = (bf16[128,768]{1,0:T(8,128)(2,1)S(1)}, bf16[128,768]{1,0:T(8,128)(2,1)}, u32[]{:S(2)}) copy-start(bf16[128,768]{1,0:T(8,128)(2,1)} %get-tuple-element.62) | copy-start | bytes 589828
  122.2 23.3 %copy-start.18 = (bf16[128,768]{1,0:T(8,128)(2,1)S(1)}, bf16[128,768]{1,0:T(8,128)(2,1)}, u32[]{:S(2)}) copy-start(bf16[128,768]{1,0:T(8,128)(2,1)} %get-tuple-element.63) | copy-start | bytes 589828
  139.2 20.4 %copy-start.5 = (bf16[16,32,256]{2,1,0:T(8,128)(2,1)}, bf16[16,32,256]{2,1,0:T(8,128)(2,1)S(1)}, u32[]{:S(2)}) copy-start(bf16[16,32,256]{2,1,0:T(8,128)(2,1)S(1)} %all-to-all-done.3) | copy-start | bytes 786436
  139.2 47.2 %collective-permute-start.6 = (bf16[2,256,768]{2,1,0:T(8,128)(2,1)}, bf16[2,256,768]{2,1,0:T(8,128)(2,1)S(1)}, u32[]{:S(2)}, u32[]{:S(2)}) collective-permute-start(bf16[2,256,768]{2,1,0:T(8,128)(2,1)} %collective-permute-done.5), channel_id=1, source_target_pairs={{256,4},{257,5},{258,6},{259,7},{260,8},{261,9},{262,10},{263,11},... | collective-permute-start | bytes 2359304 | tf_op jit(solution)/shard_map/ppermute | solution.py:362
  143.5 12.6 %collective-permute-start.7 = (bf16[128,768]{1,0:T(8,128)(2,1)S(1)}, bf16[128,768]{1,0:T(8,128)(2,1)S(1)}, u32[]{:S(2)}, u32[]{:S(2)}) collective-permute-start(bf16[128,768]{1,0:T(8,128)(2,1)S(1)} %copy-done.19), channel_id=1, source_target_pairs={{0,1},{1,0},{2,3},{3,2},{4,5},{5,4},{6,7},{7,6},{8,9},{9,8},{10,11... | collective-permute-start | bytes 589832 | tf_op jit(solution)/shard_map/ppermute | solution.py:51
  145.4 22.3 %collective-permute-start.8 = (bf16[128,768]{1,0:T(8,128)(2,1)S(1)}, bf16[128,768]{1,0:T(8,128)(2,1)S(1)}, u32[]{:S(2)}, u32[]{:S(2)}) collective-permute-start(bf16[128,768]{1,0:T(8,128)(2,1)S(1)} %copy-done.18), channel_id=1, source_target_pairs={{0,2},{1,3},{2,0},{3,1},{4,6},{5,7},{6,4},{7,5},{8,10},{9,11},{10,... | collective-permute-start | bytes 589832 | tf_op jit(solution)/shard_map/ppermute | solution.py:51
  150.5 26.8 %collective-permute-start.12 = (bf16[512,256]{1,0:T(8,128)(2,1)S(1)}, bf16[512,256]{1,0:T(8,128)(2,1)S(1)}, u32[]{:S(2)}, u32[]{:S(2)}) collective-permute-start(bf16[512,256]{1,0:T(8,128)(2,1)S(1)} %bitcast.6), channel_id=1, source_target_pairs={{0,24},{1,25},{2,26},{3,27},{4,28},{5,29},{6,30},{7,31},{8,16},{9,... | collective-permute-start | bytes 786440 | tf_op jit(solution)/shard_map/ppermute | solution.py:51
  152.6 24.7 %collective-permute-start.11 = (bf16[512,256]{1,0:T(8,128)(2,1)S(1)}, bf16[512,256]{1,0:T(8,128)(2,1)S(1)}, u32[]{:S(2)}, u32[]{:S(2)}) collective-permute-start(bf16[512,256]{1,0:T(8,128)(2,1)S(1)} %bitcast.7), channel_id=1, source_target_pairs={{0,16},{1,17},{2,18},{3,19},{4,20},{5,21},{6,22},{7,23},{8,24},{9,... | collective-permute-start | bytes 786440 | tf_op jit(solution)/shard_map/ppermute | solution.py:51
  156.1 21.2 %collective-permute-start.10 = (bf16[512,256]{1,0:T(8,128)(2,1)S(1)}, bf16[512,256]{1,0:T(8,128)(2,1)S(1)}, u32[]{:S(2)}, u32[]{:S(2)}) collective-permute-start(bf16[512,256]{1,0:T(8,128)(2,1)S(1)} %bitcast.8), channel_id=1, source_target_pairs={{0,8},{1,9},{2,10},{3,11},{4,12},{5,13},{6,14},{7,15},{8,0},{9,1},... | collective-permute-start | bytes 786440 | tf_op jit(solution)/shard_map/ppermute | solution.py:51
  159.6 34.3 %all-to-all-start.4 = ((bf16[16,32,256]{2,1,0:T(8,128)(2,1)}), bf16[16,32,256]{2,1,0:T(8,128)(2,1)S(1)}, u32[]{:S(2)}, u32[]{:S(2)}) async-start(bf16[16,32,256]{2,1,0:T(8,128)(2,1)} %far_kernel.1), calls=%async_computation.4 | async-start | bytes 524288 | tf_op jit(solution)/shard_map/all_to_all | solution.py:371
  167.7 9.6 %copy-start.10 = (bf16[128,768]{1,0:T(8,128)(2,1)}, bf16[128,768]{1,0:T(8,128)(2,1)S(1)}, u32[]{:S(2)}) copy-start(bf16[128,768]{1,0:T(8,128)(2,1)S(1)} %collective-permute-done.8.q2) | copy-start | bytes 589828
  167.7 9.6 %collective-permute-start.9 = (bf16[128,768]{1,0:T(8,128)(2,1)S(1)}, bf16[128,768]{1,0:T(8,128)(2,1)S(1)}, u32[]{:S(2)}, u32[]{:S(2)}) collective-permute-start(bf16[128,768]{1,0:T(8,128)(2,1)S(1)} %copy-done.17), channel_id=1, source_target_pairs={{0,3},{1,2},{2,1},{3,0},{4,7},{5,6},{6,5},{7,4},{8,11},{9,10},{10,... | collective-permute-start | bytes 589832 | tf_op jit(solution)/shard_map/ppermute | solution.py:51
  (13 other events, 51.8 us)

commit v4 on v3

--- a/solution.py
+++ b/solution.py
@@ -24,7 +24,7 @@
 ROWS = 2 * BLOCK + 16
 MARK = 128.0
 NEG = -1e30
-LEGS = (2, 2, 4)
+LEGS = (2, 3, 3)
 LEAST = -1e4
 SCALE = 1.0 / (math.sqrt(DIM) * math.log(2.0))
 f32, bf16 = jnp.float32, jnp.bfloat16
@@ -357,10 +357,10 @@
     spread = lax.all_to_all(spread, GRP, 0, 0).reshape(-1, 2 * DIM)
     part, halo = tie((part, halo))
     far = call(far_kernel, (WINDOWS, PART, 2 * DIM), 10**10, [part, quarters])
+    asked = [asked[0]] + [send(asked[d], flip("y", d)) for d in range(1, YS)]
     halo, far, spread, asked = tie((halo, far, spread, asked))
 
     halo = lax.ppermute(halo, AXES, leg(2))
-    asked = [asked[0]] + [send(asked[d], flip("y", d)) for d in range(1, YS)]
     scratch = [
         pltpu.VMEM((YS, ROWS, WIDE), bf16),
         pltpu.VMEM((YS, BLOCK, WIDE), bf16),

time: 215 us -> 216 us (level)
  the two profiles are of different devices: /device:TPU:1 before, /device:TPU:70 now
where the time goes in v4:
time: 216 us; the launch traced here: 215 us
  starting transfers between devices  89.2 us (41%)
  waiting for transfers between devices  62.4 us (29%)
  blocking collectives  31.6 us (15%)
  Pallas kernels  22.7 us (11%)
  local copies, waits for them, and re-layouts  4.8 us (2%)
  between operations  3.06 us (1%)
    ppermute x10, starting transfers between devices, send(): return lax.ppermute(value, AXES, route(move))  38.9 us
    ppermute x10, waiting for transfers between devices, send(): return lax.ppermute(value, AXES, route(move))  24.4 us
    ppermute x1, waiting for transfers between devices, on_device(): halo = lax.ppermute(halo, AXES, leg(0))  23.3 us
    pallas_call x6, Pallas kernels, call(): pl.pallas_call(kernel, out_shape=outs, in_specs=[SMEM if o.ndim == 1 else...  22.7 us
    all_to_all x1, blocking collectives, on_device(): back = lax.all_to_all(out, 'y', 0, 0)  17.7 us
    all_to_all x1, blocking collectives, on_device(): parts = lax.all_to_all(f1, ('x', 'y'), 0, 0)  14 us
    all_to_all x1, starting transfers between devices, on_device(): spread = lax.all_to_all(spread, GRP, 0, 0).reshape(-1, 2 * DIM)  12.9 us
    all_to_all x1, starting transfers between devices, on_device(): part = lax.all_to_all(s1, GRP, 0, 0)  12.3 us
  transfers between devices with their start and end apart: 17, of which 8 were waited for; matrix products, arithmetic and copies ran while one was open for 1% of the time, Pallas kernels for 8%

profile of v4, /device:TPU:70, one launch (start us, length us, event | category | flops | bytes accessed | tf_op | source)
XLA Modules:
  0.0 215.1 jit_solution(12612012077684940366)
XLA Ops:
  0.6 4.4 %pack_kernel.1 = (bf16[16,32,384]{2,1,0:T(8,128)(2,1)}, bf16[16,32,256]{2,1,0:T(8,128)(2,1)}, bf16[272,768]{1,0:T(8,128)(2,1)}, bf16[272,768]{1,0:T(8,128)(2,1)}...) custom-call(s32[2]{0:T(128)} %pad_add_fusion.info, ...), custom_call_target="tpu_custom_call" | custom-call | flops 1000000 | bytes 2359816 | tf_op jit(solution)/shard_map/pack_kernel/pallas_call | solution.py:304
  5.0 14.0 %all_to_all.30 = bf16[16,32,256]{2,1,0:T(8,128)(2,1)S(1)} all-to-all(bf16[16,32,256]{2,1,0:T(8,128)(2,1)} %get-tuple-element.41), channel_id=1, replica_groups=mesh['zp'=4,'zq'=2,'core'=2,'x'=4,'zh'=2,'y'=4] {'x','y'}, dimensions={0} | all-to-all | bytes 524288 | tf_op jit(solution)/shard_map/all_to_all | solution.py:341
  19.0 12.3 %all-to-all-start.1 = ((bf16[16,32,384]{2,1,0:T(8,128)(2,1)}), bf16[16,32,384]{2,1,0:T(8,128)(2,1)S(1)}, u32[]{:S(2)}, u32[]{:S(2)}) async-start(bf16[16,32,384]{2,1,0:T(8,128)(2,1)} %get-tuple-element.43), calls=%async_computation.1 | async-start | bytes 786432 | tf_op jit(solution)/shard_map/all_to_all | solution.py:343
  33.8 3.7 %collective-permute-start.1 = (bf16[272,768]{1,0:T(8,128)(2,1)S(1)}, bf16[272,768]{1,0:T(8,128)(2,1)S(1)}, u32[]{:S(2)}, u32[]{:S(2)}) collective-permute-start(bf16[272,768]{1,0:T(8,128)(2,1)S(1)} %copy-done.15), channel_id=1, source_target_pairs={{0,2},{1,3},{2,0},{3,1},{4,6},{5,7},{6,4},{7,5},{8,10},{9,11},{10,... | collective-permute-start | bytes 1253384 | tf_op jit(solution)/shard_map/ppermute | solution.py:51
  37.5 4.3 %collective-permute-start.2 = (bf16[272,768]{1,0:T(8,128)(2,1)S(1)}, bf16[272,768]{1,0:T(8,128)(2,1)S(1)}, u32[]{:S(2)}, u32[]{:S(2)}) collective-permute-start(bf16[272,768]{1,0:T(8,128)(2,1)S(1)} %copy-done.14), channel_id=1, source_target_pairs={{0,3},{1,2},{2,1},{3,0},{4,7},{5,6},{6,5},{7,4},{8,11},{9,10},{10,... | collective-permute-start | bytes 1253384 | tf_op jit(solution)/shard_map/ppermute | solution.py:51
  45.2 8.2 %collective-permute-start.3 = (bf16[32,256]{1,0:T(8,128)(2,1)S(1)}, bf16[32,256]{1,0:T(8,128)(2,1)S(1)}, u32[]{:S(2)}, u32[]{:S(2)}) collective-permute-start(bf16[32,256]{1,0:T(8,128)(2,1)S(1)} %select_reduce_fusion), channel_id=1, source_target_pairs={{0,4},{1,5},{2,6},{3,7},{4,0},{5,1},{6,2},{7,3},{8,12},{9,13},{10,... | collective-permute-start | bytes 49160 | tf_op jit(solution)/shard_map/ppermute | solution.py:51
  53.4 6.1 %collective-permute-done.3 = bf16[32,256]{1,0:T(8,128)(2,1)S(1)} collective-permute-done((bf16[32,256]{1,0:T(8,128)(2,1)S(1)}, bf16[32,256]{1,0:T(8,128)(2,1)S(1)}, u32[]{:S(2)}, u32[]{:S(2)}) %collective-permute-start.3) | collective-permute-done | bytes 16416 | tf_op jit(solution)/shard_map/ppermute | solution.py:51
  61.9 3.6 %all-to-all-start.2 = ((bf16[4,16,32,256]{3,2,1,0:T(8,128)(2,1)}), bf16[4,16,32,256]{3,2,1,0:T(8,128)(2,1)S(1)}, u32[]{:S(2)}, u32[]{:S(2)}) async-start(bf16[4,16,32,256]{3,2,1,0:T(8,128)(2,1)} %broadcast_in_dim.38), calls=%async_computation.2 | async-start | bytes 2097152 | tf_op jit(solution)/shard_map/all_to_all | solution.py:351
  66.8 5.5 %collective-permute-start.4 = (bf16[2,256,768]{2,1,0:T(8,128)(2,1)S(1)}, bf16[2,256,768]{2,1,0:T(8,128)(2,1)}, u32[]{:S(2)}, u32[]{:S(2)}) collective-permute-start(bf16[2,256,768]{2,1,0:T(8,128)(2,1)S(1)} %halo_kernel.1), channel_id=1, source_target_pairs={{0,128},{1,129},{2,130},{3,131},{4,132},{5,133},{6,134},{7,135},{8... | collective-permute-start | bytes 2359304 | tf_op jit(solution)/shard_map/ppermute | solution.py:353
  72.3 23.3 %collective-permute-done.4 = bf16[2,256,768]{2,1,0:T(8,128)(2,1)} collective-permute-done((bf16[2,256,768]{2,1,0:T(8,128)(2,1)S(1)}, bf16[2,256,768]{2,1,0:T(8,128)(2,1)}, u32[]{:S(2)}, u32[]{:S(2)}) %collective-permute-start.4) | collective-permute-done | bytes 786464 | tf_op jit(solution)/shard_map/ppermute | solution.py:353
  98.3 12.9 %all-to-all-start.3 = ((bf16[16,32,256]{2,1,0:T(8,128)(2,1)}), bf16[16,32,256]{2,1,0:T(8,128)(2,1)S(1)}, u32[]{:S(2)}, u32[]{:S(2)}) async-start(bf16[16,32,256]{2,1,0:T(8,128)(2,1)} %broadcast_in_dim.39), calls=%async_computation.3 | async-start | bytes 524288 | tf_op jit(solution)/shard_map/all_to_all | solution.py:357
  113.1 5.7 %collective-permute-start.7 = (bf16[128,768]{1,0:T(8,128)(2,1)S(1)}, bf16[128,768]{1,0:T(8,128)(2,1)S(1)}, u32[]{:S(2)}, u32[]{:S(2)}) collective-permute-start(bf16[128,768]{1,0:T(8,128)(2,1)S(1)} %copy-done.18), channel_id=1, source_target_pairs={{0,2},{1,3},{2,0},{3,1},{4,6},{5,7},{6,4},{7,5},{8,10},{9,11},{10,... | collective-permute-start | bytes 589832 | tf_op jit(solution)/shard_map/ppermute | solution.py:51
  121.7 4.1 %collective-permute-done.5 = bf16[2,256,768]{2,1,0:T(8,128)(2,1)} collective-permute-done((bf16[2,256,768]{2,1,0:T(8,128)(2,1)}, bf16[2,256,768]{2,1,0:T(8,128)(2,1)}, u32[]{:S(2)}, u32[]{:S(2)}) %collective-permute-start.5) | collective-permute-done | bytes 786464 | tf_op jit(solution)/shard_map/ppermute | solution.py:355
  125.8 3.2 %far_kernel.1 = bf16[16,32,256]{2,1,0:T(8,128)(2,1)} custom-call(bf16[16,32,384]{2,1,0:T(8,128)(2,1)S(1)} %all-to-all-done.1.part, bf16[4,16,32,256]{3,2,1,0:T(8,128)(2,1)S(1)} %all-to-all-done.2.keys_values), custom_call_target="tpu_custom_call" | custom-call | flops 10000000000 | bytes 1441792 | tf_op jit(solution)/shard_map/far_kernel/pallas_call | solution.py:304
  130.3 10.6 %all-to-all-done.3 = bf16[16,32,256]{2,1,0:T(8,128)(2,1)S(1)} async-done(((bf16[16,32,256]{2,1,0:T(8,128)(2,1)}), bf16[16,32,256]{2,1,0:T(8,128)(2,1)S(1)}, u32[]{:S(2)}, u32[]{:S(2)}) %all-to-all-start.3) | async-done | bytes 262176 | tf_op jit(solution)/shard_map/all_to_all | solution.py:357
  140.8 4.2 %collective-permute-start.9 = (bf16[2,256,768]{2,1,0:T(8,128)(2,1)}, bf16[2,256,768]{2,1,0:T(8,128)(2,1)S(1)}, u32[]{:S(2)}, u32[]{:S(2)}) collective-permute-start(bf16[2,256,768]{2,1,0:T(8,128)(2,1)} %collective-permute-done.5), channel_id=1, source_target_pairs={{320,4},{321,5},{322,6},{323,7},{324,8},{325,9},{326,10},{327,11},... | collective-permute-start | bytes 2359304 | tf_op jit(solution)/shard_map/ppermute | solution.py:363
  145.1 4.3 %collective-permute-start.12 = (bf16[512,256]{1,0:T(8,128)(2,1)S(1)}, bf16[512,256]{1,0:T(8,128)(2,1)S(1)}, u32[]{:S(2)}, u32[]{:S(2)}) collective-permute-start(bf16[512,256]{1,0:T(8,128)(2,1)S(1)} %bitcast.6), channel_id=1, source_target_pairs={{0,24},{1,25},{2,26},{3,27},{4,28},{5,29},{6,30},{7,31},{8,16},{9,... | collective-permute-start | bytes 786440 | tf_op jit(solution)/shard_map/ppermute | solution.py:51
  149.3 3.4 %collective-permute-start.11 = (bf16[512,256]{1,0:T(8,128)(2,1)S(1)}, bf16[512,256]{1,0:T(8,128)(2,1)S(1)}, u32[]{:S(2)}, u32[]{:S(2)}) collective-permute-start(bf16[512,256]{1,0:T(8,128)(2,1)S(1)} %bitcast.7), channel_id=1, source_target_pairs={{0,16},{1,17},{2,18},{3,19},{4,20},{5,21},{6,22},{7,23},{8,24},{9,... | collective-permute-start | bytes 786440 | tf_op jit(solution)/shard_map/ppermute | solution.py:51
  154.9 9.8 %all-to-all-start.4 = ((bf16[16,32,256]{2,1,0:T(8,128)(2,1)}), bf16[16,32,256]{2,1,0:T(8,128)(2,1)S(1)}, u32[]{:S(2)}, u32[]{:S(2)}) async-start(bf16[16,32,256]{2,1,0:T(8,128)(2,1)} %far_kernel.1), calls=%async_computation.4 | async-start | bytes 524288 | tf_op jit(solution)/shard_map/all_to_all | solution.py:371
  165.6 11.3 %collective-permute-done.12.f3 = bf16[512,256]{1,0:T(8,128)(2,1)S(1)} collective-permute-done((bf16[512,256]{1,0:T(8,128)(2,1)S(1)}, bf16[512,256]{1,0:T(8,128)(2,1)S(1)}, u32[]{:S(2)}, u32[]{:S(2)}) %collective-permute-start.12) | collective-permute-done | bytes 262176 | tf_op jit(solution)/shard_map/ppermute | solution.py:51
  176.9 4.6 %collective-permute-done.10.f1 = bf16[512,256]{1,0:T(8,128)(2,1)S(1)} collective-permute-done((bf16[512,256]{1,0:T(8,128)(2,1)S(1)}, bf16[512,256]{1,0:T(8,128)(2,1)S(1)}, u32[]{:S(2)}, u32[]{:S(2)}) %collective-permute-start.10) | collective-permute-done | bytes 262176 | tf_op jit(solution)/shard_map/ppermute | solution.py:51
  182.2 5.9 %early_kernel.1.early = bf16[2,128,896]{2,1,0:T(8,128)(2,1)} custom-call(s32[2]{0:T(128)} %pad_add_fusion.info, f32[4,512]{1,0:T(4,128)} %reshape.25.fixed_ok, bf16[272,768]{1,0:T(8,128)(2,1)} %get-tuple-element.46.r0.p0, bf16[272,768]{1,0:T(8,128)(2,1)} %copy-done.1, bf16[272,768]{1,0:T(8,128)(2,1)} %copy-done.2, bf16[272,768]{1,0:T(8,128)(2,1)} %copy-done.3, ...), custom_call_target="tpu_custom_call" | custom-call | flops 300000000 | bytes 3514376 | tf_op jit(solution)/shard_map/early_kernel/pallas_call | solution.py:304
  189.0 6.7 %late_kernel.1 = bf16[4,128,896]{2,1,0:T(8,128)(2,1)} custom-call(s32[2]{0:T(128)} %pad_add_fusion.info, f32[4,512]{1,0:T(4,128)} %reshape.25.fixed_ok, bf16[2,256,768]{2,1,0:T(8,128)(2,1)} %copy-done.13, bf16[2,128,896]{2,1,0:T(8,128)(2,1)} %early_kernel.1.early, bf16[272,768]{1,0:T(8,128)(2,1)} %get-tuple-element.46.r0.p0, bf16[272,768]{1,0:T(8,128)(2,1)} %copy-done.1, ...), custom_call_target="tpu_custom_call" | custom-call | flops 10000000000 | bytes 4759560 | tf_op jit(solution)/shard_map/late_kernel/pallas_call | solution.py:304
  195.7 17.7 %all_to_all.31.back = bf16[4,128,896]{2,1,0:T(8,128)(2,1)S(1)} all-to-all(bf16[4,128,896]{2,1,0:T(8,128)(2,1)} %late_kernel.1), channel_id=1, replica_groups=mesh['zp'=4,'zq'=2,'core'=2,'x'=4,'zh'=2,'y'=4] {'y'}, dimensions={0} | all-to-all | bytes 1835008 | tf_op jit(solution)/shard_map/all_to_all | solution.py:378
  (70 shorter events, 22.3 us)
Async XLA Ops:
  5.0 26.3 %copy-start.16 = (bf16[272,768]{1,0:T(8,128)(2,1)S(1)}, bf16[272,768]{1,0:T(8,128)(2,1)}, u32[]{:S(2)}) copy-start(bf16[272,768]{1,0:T(8,128)(2,1)} %get-tuple-element.38) | copy-start | bytes 1253380
  5.0 28.8 %copy-start.15 = (bf16[272,768]{1,0:T(8,128)(2,1)S(1)}, bf16[272,768]{1,0:T(8,128)(2,1)}, u32[]{:S(2)}) copy-start(bf16[272,768]{1,0:T(8,128)(2,1)} %get-tuple-element.39) | copy-start | bytes 1253380
  19.0 18.5 %copy-start.14 = (bf16[272,768]{1,0:T(8,128)(2,1)S(1)}, bf16[272,768]{1,0:T(8,128)(2,1)}, u32[]{:S(2)}) copy-start(bf16[272,768]{1,0:T(8,128)(2,1)} %get-tuple-element.40) | copy-start | bytes 1253380
  19.0 41.7 %all-to-all-start.1 = ((bf16[16,32,384]{2,1,0:T(8,128)(2,1)}), bf16[16,32,384]{2,1,0:T(8,128)(2,1)S(1)}, u32[]{:S(2)}, u32[]{:S(2)}) async-start(bf16[16,32,384]{2,1,0:T(8,128)(2,1)} %get-tuple-element.43), calls=%async_computation.1 | async-start | bytes 786432 | tf_op jit(solution)/shard_map/all_to_all | solution.py:343
  31.3 28.2 %collective-permute-start = (bf16[272,768]{1,0:T(8,128)(2,1)S(1)}, bf16[272,768]{1,0:T(8,128)(2,1)S(1)}, u32[]{:S(2)}, u32[]{:S(2)}) collective-permute-start(bf16[272,768]{1,0:T(8,128)(2,1)S(1)} %copy-done.16), channel_id=1, source_target_pairs={{0,1},{1,0},{2,3},{3,2},{4,5},{5,4},{6,7},{7,6},{8,9},{9,8},{10,11... | collective-permute-start | bytes 1253384 | tf_op jit(solution)/shard_map/ppermute | solution.py:51
  33.8 25.8 %collective-permute-start.1 = (bf16[272,768]{1,0:T(8,128)(2,1)S(1)}, bf16[272,768]{1,0:T(8,128)(2,1)S(1)}, u32[]{:S(2)}, u32[]{:S(2)}) collective-permute-start(bf16[272,768]{1,0:T(8,128)(2,1)S(1)} %copy-done.15), channel_id=1, source_target_pairs={{0,2},{1,3},{2,0},{3,1},{4,6},{5,7},{6,4},{7,5},{8,10},{9,11},{10,... | collective-permute-start | bytes 1253384 | tf_op jit(solution)/shard_map/ppermute | solution.py:51
  37.5 23.2 %collective-permute-start.2 = (bf16[272,768]{1,0:T(8,128)(2,1)S(1)}, bf16[272,768]{1,0:T(8,128)(2,1)S(1)}, u32[]{:S(2)}, u32[]{:S(2)}) collective-permute-start(bf16[272,768]{1,0:T(8,128)(2,1)S(1)} %copy-done.14), channel_id=1, source_target_pairs={{0,3},{1,2},{2,1},{3,0},{4,7},{5,6},{6,5},{7,4},{8,11},{9,10},{10,... | collective-permute-start | bytes 1253384 | tf_op jit(solution)/shard_map/ppermute | solution.py:51
  45.2 14.4 %collective-permute-start.3 = (bf16[32,256]{1,0:T(8,128)(2,1)S(1)}, bf16[32,256]{1,0:T(8,128)(2,1)S(1)}, u32[]{:S(2)}, u32[]{:S(2)}) collective-permute-start(bf16[32,256]{1,0:T(8,128)(2,1)S(1)} %select_reduce_fusion), channel_id=1, source_target_pairs={{0,4},{1,5},{2,6},{3,7},{4,0},{5,1},{6,2},{7,3},{8,12},{9,13},{10,... | collective-permute-start | bytes 49160 | tf_op jit(solution)/shard_map/ppermute | solution.py:51
  61.9 33.8 %all-to-all-start.2 = ((bf16[4,16,32,256]{3,2,1,0:T(8,128)(2,1)}), bf16[4,16,32,256]{3,2,1,0:T(8,128)(2,1)S(1)}, u32[]{:S(2)}, u32[]{:S(2)}) async-start(bf16[4,16,32,256]{3,2,1,0:T(8,128)(2,1)} %broadcast_in_dim.38), calls=%async_computation.2 | async-start | bytes 2097152 | tf_op jit(solution)/shard_map/all_to_all | solution.py:351
  66.8 28.8 %collective-permute-start.4 = (bf16[2,256,768]{2,1,0:T(8,128)(2,1)S(1)}, bf16[2,256,768]{2,1,0:T(8,128)(2,1)}, u32[]{:S(2)}, u32[]{:S(2)}) collective-permute-start(bf16[2,256,768]{2,1,0:T(8,128)(2,1)S(1)} %halo_kernel.1), channel_id=1, source_target_pairs={{0,128},{1,129},{2,130},{3,131},{4,132},{5,133},{6,134},{7,135},{8... | collective-permute-start | bytes 2359304 | tf_op jit(solution)/shard_map/ppermute | solution.py:353
  95.6 30.1 %collective-permute-start.5 = (bf16[2,256,768]{2,1,0:T(8,128)(2,1)}, bf16[2,256,768]{2,1,0:T(8,128)(2,1)}, u32[]{:S(2)}, u32[]{:S(2)}) collective-permute-start(bf16[2,256,768]{2,1,0:T(8,128)(2,1)} %collective-permute-done.4), channel_id=1, source_target_pairs={{128,320},{129,321},{130,322},{131,323},{132,324},{133,325},{134,3... | collective-permute-start | bytes 2359304 | tf_op jit(solution)/shard_map/ppermute | solution.py:355
  98.3 20.6 %copy-start.17 = (bf16[128,768]{1,0:T(8,128)(2,1)S(1)}, bf16[128,768]{1,0:T(8,128)(2,1)}, u32[]{:S(2)}) copy-start(bf16[128,768]{1,0:T(8,128)(2,1)} %get-tuple-element.59) | copy-start | bytes 589828
  98.3 42.5 %all-to-all-start.3 = ((bf16[16,32,256]{2,1,0:T(8,128)(2,1)}), bf16[16,32,256]{2,1,0:T(8,128)(2,1)S(1)}, u32[]{:S(2)}, u32[]{:S(2)}) async-start(bf16[16,32,256]{2,1,0:T(8,128)(2,1)} %broadcast_in_dim.39), calls=%async_computation.3 | async-start | bytes 524288 | tf_op jit(solution)/shard_map/all_to_all | solution.py:357
  111.2 17.7 %collective-permute-start.6 = (bf16[128,768]{1,0:T(8,128)(2,1)S(1)}, bf16[128,768]{1,0:T(8,128)(2,1)S(1)}, u32[]{:S(2)}, u32[]{:S(2)}) collective-permute-start(bf16[128,768]{1,0:T(8,128)(2,1)S(1)} %copy-done.19), channel_id=1, source_target_pairs={{0,1},{1,0},{2,3},{3,2},{4,5},{5,4},{6,7},{7,6},{8,9},{9,8},{10,11... | collective-permute-start | bytes 589832 | tf_op jit(solution)/shard_map/ppermute | solution.py:51
  113.1 15.8 %collective-permute-start.7 = (bf16[128,768]{1,0:T(8,128)(2,1)S(1)}, bf16[128,768]{1,0:T(8,128)(2,1)S(1)}, u32[]{:S(2)}, u32[]{:S(2)}) collective-permute-start(bf16[128,768]{1,0:T(8,128)(2,1)S(1)} %copy-done.18), channel_id=1, source_target_pairs={{0,2},{1,3},{2,0},{3,1},{4,6},{5,7},{6,4},{7,5},{8,10},{9,11},{10,... | collective-permute-start | bytes 589832 | tf_op jit(solution)/shard_map/ppermute | solution.py:51
  118.9 11.4 %collective-permute-start.8 = (bf16[128,768]{1,0:T(8,128)(2,1)S(1)}, bf16[128,768]{1,0:T(8,128)(2,1)S(1)}, u32[]{:S(2)}, u32[]{:S(2)}) collective-permute-start(bf16[128,768]{1,0:T(8,128)(2,1)S(1)} %copy-done.17), channel_id=1, source_target_pairs={{0,3},{1,2},{2,1},{3,0},{4,7},{5,6},{6,5},{7,4},{8,11},{9,10},{10,... | collective-permute-start | bytes 589832 | tf_op jit(solution)/shard_map/ppermute | solution.py:51
  128.9 26.0 %copy-start.9 = (bf16[128,768]{1,0:T(8,128)(2,1)}, bf16[128,768]{1,0:T(8,128)(2,1)S(1)}, u32[]{:S(2)}) copy-start(bf16[128,768]{1,0:T(8,128)(2,1)S(1)} %collective-permute-done.6.q1) | copy-start | bytes 589828
  128.9 52.5 %copy-start.10 = (bf16[128,768]{1,0:T(8,128)(2,1)}, bf16[128,768]{1,0:T(8,128)(2,1)S(1)}, u32[]{:S(2)}) copy-start(bf16[128,768]{1,0:T(8,128)(2,1)S(1)} %collective-permute-done.7.q2) | copy-start | bytes 589828
  130.3 51.2 %copy-start.11 = (bf16[128,768]{1,0:T(8,128)(2,1)}, bf16[128,768]{1,0:T(8,128)(2,1)S(1)}, u32[]{:S(2)}) copy-start(bf16[128,768]{1,0:T(8,128)(2,1)S(1)} %collective-permute-done.8.q3) | copy-start | bytes 589828
  140.8 47.3 %collective-permute-start.9 = (bf16[2,256,768]{2,1,0:T(8,128)(2,1)}, bf16[2,256,768]{2,1,0:T(8,128)(2,1)S(1)}, u32[]{:S(2)}, u32[]{:S(2)}) collective-permute-start(bf16[2,256,768]{2,1,0:T(8,128)(2,1)} %collective-permute-done.5), channel_id=1, source_target_pairs={{320,4},{321,5},{322,6},{323,7},{324,8},{325,9},{326,10},{327,11},... | collective-permute-start | bytes 2359304 | tf_op jit(solution)/shard_map/ppermute | solution.py:363
  145.1 31.8 %collective-permute-start.12 = (bf16[512,256]{1,0:T(8,128)(2,1)S(1)}, bf16[512,256]{1,0:T(8,128)(2,1)S(1)}, u32[]{:S(2)}, u32[]{:S(2)}) collective-permute-start(bf16[512,256]{1,0:T(8,128)(2,1)S(1)} %bitcast.6), channel_id=1, source_target_pairs={{0,24},{1,25},{2,26},{3,27},{4,28},{5,29},{6,30},{7,31},{8,16},{9,... | collective-permute-start | bytes 786440 | tf_op jit(solution)/shard_map/ppermute | solution.py:51
  149.3 27.6 %collective-permute-start.11 = (bf16[512,256]{1,0:T(8,128)(2,1)S(1)}, bf16[512,256]{1,0:T(8,128)(2,1)S(1)}, u32[]{:S(2)}, u32[]{:S(2)}) collective-permute-start(bf16[512,256]{1,0:T(8,128)(2,1)S(1)} %bitcast.7), channel_id=1, source_target_pairs={{0,16},{1,17},{2,18},{3,19},{4,20},{5,21},{6,22},{7,23},{8,24},{9,... | collective-permute-start | bytes 786440 | tf_op jit(solution)/shard_map/ppermute | solution.py:51
  152.8 28.7 %collective-permute-start.10 = (bf16[512,256]{1,0:T(8,128)(2,1)S(1)}, bf16[512,256]{1,0:T(8,128)(2,1)S(1)}, u32[]{:S(2)}, u32[]{:S(2)}) collective-permute-start(bf16[512,256]{1,0:T(8,128)(2,1)S(1)} %bitcast.8), channel_id=1, source_target_pairs={{0,8},{1,9},{2,10},{3,11},{4,12},{5,13},{6,14},{7,15},{8,0},{9,1},... | collective-permute-start | bytes 786440 | tf_op jit(solution)/shard_map/ppermute | solution.py:51
  154.9 40.8 %all-to-all-start.4 = ((bf16[16,32,256]{2,1,0:T(8,128)(2,1)}), bf16[16,32,256]{2,1,0:T(8,128)(2,1)S(1)}, u32[]{:S(2)}, u32[]{:S(2)}) async-start(bf16[16,32,256]{2,1,0:T(8,128)(2,1)} %far_kernel.1), calls=%async_computation.4 | async-start | bytes 524288 | tf_op jit(solution)/shard_map/all_to_all | solution.py:371
  (13 other events, 82.4 us)

commit v5 on v4

--- a/solution.py
+++ b/solution.py
@@ -357,10 +357,10 @@
     spread = lax.all_to_all(spread, GRP, 0, 0).reshape(-1, 2 * DIM)
     part, halo = tie((part, halo))
     far = call(far_kernel, (WINDOWS, PART, 2 * DIM), 10**10, [part, quarters])
+    halo, far, spread, asked = tie((halo, far, spread, asked))
+
+    halo = lax.ppermute(halo, AXES, leg(2))
     asked = [asked[0]] + [send(asked[d], flip("y", d)) for d in range(1, YS)]
-    halo, far, spread, asked = tie((halo, far, spread, asked))
-
-    halo = lax.ppermute(halo, AXES, leg(2))
     scratch = [
         pltpu.VMEM((YS, ROWS, WIDE), bf16),
         pltpu.VMEM((YS, BLOCK, WIDE), bf16),

time: 216 us -> 220 us (1.019)
  the two profiles are of different devices: /device:TPU:70 before, /device:TPU:1 now
where the time goes in v5:
time: 220 us; the launch traced here: 219 us
  starting transfers between devices  102 us (46%)
  waiting for transfers between devices  52.4 us (24%)
  blocking collectives  31.4 us (14%)
  Pallas kernels  22.6 us (10%)
  local copies, waits for them, and re-layouts  5.68 us (3%)
  between operations  3.08 us (1%)
    ppermute x10, starting transfers between devices, send(): return lax.ppermute(value, AXES, route(move))  36.1 us
    ppermute x1, waiting for transfers between devices, on_device(): halo = lax.ppermute(halo, AXES, leg(1))  26.4 us
    pallas_call x6, Pallas kernels, call(): pl.pallas_call(kernel, out_shape=outs, in_specs=[SMEM if o.ndim == 1 else...  22.6 us
    ppermute x1, starting transfers between devices, on_device(): halo = lax.ppermute(halo, AXES, leg(1))  17.7 us
    all_to_all x1, blocking collectives, on_device(): back = lax.all_to_all(out, 'y', 0, 0)  16.3 us
    all_to_all x1, blocking collectives, on_device(): parts = lax.all_to_all(f1, ('x', 'y'), 0, 0)  15.1 us
    all_to_all x1, starting transfers between devices, on_device(): part = lax.all_to_all(s1, GRP, 0, 0)  14.7 us
    ppermute x10, waiting for transfers between devices, send(): return lax.ppermute(value, AXES, route(move))  13.4 us
  transfers between devices with their start and end apart: 17, of which 6 were waited for; matrix products, arithmetic and copies ran while one was open for 1% of the time, Pallas kernels for 8%

profile of v5, /device:TPU:1, one launch (start us, length us, event | category | flops | bytes accessed | tf_op | source)
XLA Modules:
  0.0 218.8 jit_solution(402073936546660959)
XLA Ops:
  0.6 4.4 %pack_kernel.1 = (bf16[16,32,384]{2,1,0:T(8,128)(2,1)}, bf16[16,32,256]{2,1,0:T(8,128)(2,1)}, bf16[272,768]{1,0:T(8,128)(2,1)}, bf16[272,768]{1,0:T(8,128)(2,1)}...) custom-call(s32[2]{0:T(128)} %pad_add_fusion.info, ...), custom_call_target="tpu_custom_call" | custom-call | flops 1000000 | bytes 2359816 | tf_op jit(solution)/shard_map/pack_kernel/pallas_call | solution.py:304
  5.0 15.1 %all_to_all.30 = bf16[16,32,256]{2,1,0:T(8,128)(2,1)S(1)} all-to-all(bf16[16,32,256]{2,1,0:T(8,128)(2,1)} %get-tuple-element.41), channel_id=1, replica_groups=mesh['zp'=4,'zq'=2,'core'=2,'x'=4,'zh'=2,'y'=4] {'x','y'}, dimensions={0} | all-to-all | bytes 524288 | tf_op jit(solution)/shard_map/all_to_all | solution.py:341
  20.1 14.7 %all-to-all-start.1 = ((bf16[16,32,384]{2,1,0:T(8,128)(2,1)}), bf16[16,32,384]{2,1,0:T(8,128)(2,1)S(1)}, u32[]{:S(2)}, u32[]{:S(2)}) async-start(bf16[16,32,384]{2,1,0:T(8,128)(2,1)} %get-tuple-element.43), calls=%async_computation.1 | async-start | bytes 786432 | tf_op jit(solution)/shard_map/all_to_all | solution.py:343
  37.1 3.5 %collective-permute-start.1 = (bf16[272,768]{1,0:T(8,128)(2,1)S(1)}, bf16[272,768]{1,0:T(8,128)(2,1)S(1)}, u32[]{:S(2)}, u32[]{:S(2)}) collective-permute-start(bf16[272,768]{1,0:T(8,128)(2,1)S(1)} %copy-done.15), channel_id=1, source_target_pairs={{0,2},{1,3},{2,0},{3,1},{4,6},{5,7},{6,4},{7,5},{8,10},{9,11},{10,... | collective-permute-start | bytes 1253384 | tf_op jit(solution)/shard_map/ppermute | solution.py:51
  40.6 3.9 %collective-permute-start.2 = (bf16[272,768]{1,0:T(8,128)(2,1)S(1)}, bf16[272,768]{1,0:T(8,128)(2,1)S(1)}, u32[]{:S(2)}, u32[]{:S(2)}) collective-permute-start(bf16[272,768]{1,0:T(8,128)(2,1)S(1)} %copy-done.14), channel_id=1, source_target_pairs={{0,3},{1,2},{2,1},{3,0},{4,7},{5,6},{6,5},{7,4},{8,11},{9,10},{10,... | collective-permute-start | bytes 1253384 | tf_op jit(solution)/shard_map/ppermute | solution.py:51
  47.9 7.9 %collective-permute-start.3 = (bf16[32,256]{1,0:T(8,128)(2,1)S(1)}, bf16[32,256]{1,0:T(8,128)(2,1)S(1)}, u32[]{:S(2)}, u32[]{:S(2)}) collective-permute-start(bf16[32,256]{1,0:T(8,128)(2,1)S(1)} %select_reduce_fusion), channel_id=1, source_target_pairs={{0,4},{1,5},{2,6},{3,7},{4,0},{5,1},{6,2},{7,3},{8,12},{9,13},{10,... | collective-permute-start | bytes 49160 | tf_op jit(solution)/shard_map/ppermute | solution.py:51
  55.9 5.2 %collective-permute-done.3 = bf16[32,256]{1,0:T(8,128)(2,1)S(1)} collective-permute-done((bf16[32,256]{1,0:T(8,128)(2,1)S(1)}, bf16[32,256]{1,0:T(8,128)(2,1)S(1)}, u32[]{:S(2)}, u32[]{:S(2)}) %collective-permute-start.3) | collective-permute-done | bytes 16416 | tf_op jit(solution)/shard_map/ppermute | solution.py:51
  64.4 5.1 %all-to-all-start.2 = ((bf16[4,16,32,256]{3,2,1,0:T(8,128)(2,1)}), bf16[4,16,32,256]{3,2,1,0:T(8,128)(2,1)S(1)}, u32[]{:S(2)}, u32[]{:S(2)}) async-start(bf16[4,16,32,256]{3,2,1,0:T(8,128)(2,1)} %broadcast_in_dim.38), calls=%async_computation.2 | async-start | bytes 2097152 | tf_op jit(solution)/shard_map/all_to_all | solution.py:351
  70.8 8.1 %collective-permute-start.4 = (bf16[2,256,768]{2,1,0:T(8,128)(2,1)S(1)}, bf16[2,256,768]{2,1,0:T(8,128)(2,1)}, u32[]{:S(2)}, u32[]{:S(2)}) collective-permute-start(bf16[2,256,768]{2,1,0:T(8,128)(2,1)S(1)} %halo_kernel.1), channel_id=1, source_target_pairs={{0,128},{1,129},{2,130},{3,131},{4,132},{5,133},{6,134},{7,135},{8... | collective-permute-start | bytes 2359304 | tf_op jit(solution)/shard_map/ppermute | solution.py:353
  78.9 9.0 %collective-permute-done.4 = bf16[2,256,768]{2,1,0:T(8,128)(2,1)} collective-permute-done((bf16[2,256,768]{2,1,0:T(8,128)(2,1)S(1)}, bf16[2,256,768]{2,1,0:T(8,128)(2,1)}, u32[]{:S(2)}, u32[]{:S(2)}) %collective-permute-start.4) | collective-permute-done | bytes 786464 | tf_op jit(solution)/shard_map/ppermute | solution.py:353
  87.9 3.6 %all-to-all-done.2.keys_values = bf16[4,16,32,256]{3,2,1,0:T(8,128)(2,1)S(1)} async-done(((bf16[4,16,32,256]{3,2,1,0:T(8,128)(2,1)}), bf16[4,16,32,256]{3,2,1,0:T(8,128)(2,1)S(1)}, u32[]{:S(2)}, u32[]{:S(2)}) %all-to-all-start.2) | async-done | bytes 1048608 | tf_op jit(solution)/shard_map/all_to_all | solution.py:351
  91.5 17.7 %collective-permute-start.5 = (bf16[2,256,768]{2,1,0:T(8,128)(2,1)}, bf16[2,256,768]{2,1,0:T(8,128)(2,1)}, u32[]{:S(2)}, u32[]{:S(2)}) collective-permute-start(bf16[2,256,768]{2,1,0:T(8,128)(2,1)} %collective-permute-done.4), channel_id=1, source_target_pairs={{128,320},{129,321},{130,322},{131,323},{132,324},{133,325},{134,3... | collective-permute-start | bytes 2359304 | tf_op jit(solution)/shard_map/ppermute | solution.py:355
  110.0 4.7 %all-to-all-start.3 = ((bf16[16,32,256]{2,1,0:T(8,128)(2,1)}), bf16[16,32,256]{2,1,0:T(8,128)(2,1)S(1)}, u32[]{:S(2)}, u32[]{:S(2)}) async-start(bf16[16,32,256]{2,1,0:T(8,128)(2,1)} %broadcast_in_dim.39), calls=%async_computation.3 | async-start | bytes 524288 | tf_op jit(solution)/shard_map/all_to_all | solution.py:357
  114.7 26.4 %collective-permute-done.5 = bf16[2,256,768]{2,1,0:T(8,128)(2,1)} collective-permute-done((bf16[2,256,768]{2,1,0:T(8,128)(2,1)}, bf16[2,256,768]{2,1,0:T(8,128)(2,1)}, u32[]{:S(2)}, u32[]{:S(2)}) %collective-permute-start.5) | collective-permute-done | bytes 786464 | tf_op jit(solution)/shard_map/ppermute | solution.py:355
  141.1 3.2 %far_kernel.1 = bf16[16,32,256]{2,1,0:T(8,128)(2,1)} custom-call(bf16[16,32,384]{2,1,0:T(8,128)(2,1)S(1)} %all-to-all-done.1.part, bf16[4,16,32,256]{3,2,1,0:T(8,128)(2,1)S(1)} %all-to-all-done.2.keys_values), custom_call_target="tpu_custom_call" | custom-call | flops 10000000000 | bytes 1441792 | tf_op jit(solution)/shard_map/far_kernel/pallas_call | solution.py:304
  144.3 4.7 %collective-permute-start.6 = (bf16[2,256,768]{2,1,0:T(8,128)(2,1)}, bf16[2,256,768]{2,1,0:T(8,128)(2,1)S(1)}, u32[]{:S(2)}, u32[]{:S(2)}) collective-permute-start(bf16[2,256,768]{2,1,0:T(8,128)(2,1)} %collective-permute-done.5), channel_id=1, source_target_pairs={{320,4},{321,5},{322,6},{323,7},{324,8},{325,9},{326,10},{327,11},... | collective-permute-start | bytes 2359304 | tf_op jit(solution)/shard_map/ppermute | solution.py:362
  151.0 5.1 %collective-permute-start.8 = (bf16[128,768]{1,0:T(8,128)(2,1)S(1)}, bf16[128,768]{1,0:T(8,128)(2,1)S(1)}, u32[]{:S(2)}, u32[]{:S(2)}) collective-permute-start(bf16[128,768]{1,0:T(8,128)(2,1)S(1)} %copy-done.18), channel_id=1, source_target_pairs={{0,2},{1,3},{2,0},{3,1},{4,6},{5,7},{6,4},{7,5},{8,10},{9,11},{10,... | collective-permute-start | bytes 589832 | tf_op jit(solution)/shard_map/ppermute | solution.py:51
  158.7 2.9 %collective-permute-start.11 = (bf16[512,256]{1,0:T(8,128)(2,1)S(1)}, bf16[512,256]{1,0:T(8,128)(2,1)S(1)}, u32[]{:S(2)}, u32[]{:S(2)}) collective-permute-start(bf16[512,256]{1,0:T(8,128)(2,1)S(1)} %bitcast.7), channel_id=1, source_target_pairs={{0,16},{1,17},{2,18},{3,19},{4,20},{5,21},{6,22},{7,23},{8,24},{9,... | collective-permute-start | bytes 786440 | tf_op jit(solution)/shard_map/ppermute | solution.py:51
  161.6 3.4 %collective-permute-start.10 = (bf16[512,256]{1,0:T(8,128)(2,1)S(1)}, bf16[512,256]{1,0:T(8,128)(2,1)S(1)}, u32[]{:S(2)}, u32[]{:S(2)}) collective-permute-start(bf16[512,256]{1,0:T(8,128)(2,1)S(1)} %bitcast.8), channel_id=1, source_target_pairs={{0,8},{1,9},{2,10},{3,11},{4,12},{5,13},{6,14},{7,15},{8,0},{9,1},... | collective-permute-start | bytes 786440 | tf_op jit(solution)/shard_map/ppermute | solution.py:51
  165.1 10.9 %all-to-all-start.4 = ((bf16[16,32,256]{2,1,0:T(8,128)(2,1)}), bf16[16,32,256]{2,1,0:T(8,128)(2,1)S(1)}, u32[]{:S(2)}, u32[]{:S(2)}) async-start(bf16[16,32,256]{2,1,0:T(8,128)(2,1)} %far_kernel.1), calls=%async_computation.4 | async-start | bytes 524288 | tf_op jit(solution)/shard_map/all_to_all | solution.py:371
  179.5 6.1 %collective-permute-done.9.q3 = bf16[128,768]{1,0:T(8,128)(2,1)S(1)} collective-permute-done((bf16[128,768]{1,0:T(8,128)(2,1)S(1)}, bf16[128,768]{1,0:T(8,128)(2,1)S(1)}, u32[]{:S(2)}, u32[]{:S(2)}) %collective-permute-start.9) | collective-permute-done | bytes 196640 | tf_op jit(solution)/shard_map/ppermute | solution.py:51
  187.3 5.9 %early_kernel.1.early = bf16[2,128,896]{2,1,0:T(8,128)(2,1)} custom-call(s32[2]{0:T(128)} %pad_add_fusion.info, f32[4,512]{1,0:T(4,128)} %reshape.25.fixed_ok, bf16[272,768]{1,0:T(8,128)(2,1)} %get-tuple-element.46.r0.p0, bf16[272,768]{1,0:T(8,128)(2,1)} %copy-done.1, bf16[272,768]{1,0:T(8,128)(2,1)} %copy-done.2, bf16[272,768]{1,0:T(8,128)(2,1)} %copy-done.3, ...), custom_call_target="tpu_custom_call" | custom-call | flops 300000000 | bytes 3514376 | tf_op jit(solution)/shard_map/early_kernel/pallas_call | solution.py:304
  194.1 6.7 %late_kernel.1 = bf16[4,128,896]{2,1,0:T(8,128)(2,1)} custom-call(s32[2]{0:T(128)} %pad_add_fusion.info, f32[4,512]{1,0:T(4,128)} %reshape.25.fixed_ok, bf16[2,256,768]{2,1,0:T(8,128)(2,1)} %copy-done.13, bf16[2,128,896]{2,1,0:T(8,128)(2,1)} %early_kernel.1.early, bf16[272,768]{1,0:T(8,128)(2,1)} %get-tuple-element.46.r0.p0, bf16[272,768]{1,0:T(8,128)(2,1)} %copy-done.1, ...), custom_call_target="tpu_custom_call" | custom-call | flops 10000000000 | bytes 4759560 | tf_op jit(solution)/shard_map/late_kernel/pallas_call | solution.py:304
  200.8 16.3 %all_to_all.31.back = bf16[4,128,896]{2,1,0:T(8,128)(2,1)S(1)} all-to-all(bf16[4,128,896]{2,1,0:T(8,128)(2,1)} %late_kernel.1), channel_id=1, replica_groups=mesh['zp'=4,'zq'=2,'core'=2,'x'=4,'zh'=2,'y'=4] {'y'}, dimensions={0} | all-to-all | bytes 1835008 | tf_op jit(solution)/shard_map/all_to_all | solution.py:378
  (70 shorter events, 21.0 us)
Async XLA Ops:
  5.0 29.9 %copy-start.16 = (bf16[272,768]{1,0:T(8,128)(2,1)S(1)}, bf16[272,768]{1,0:T(8,128)(2,1)}, u32[]{:S(2)}) copy-start(bf16[272,768]{1,0:T(8,128)(2,1)} %get-tuple-element.38) | copy-start | bytes 1253380
  5.0 32.0 %copy-start.15 = (bf16[272,768]{1,0:T(8,128)(2,1)S(1)}, bf16[272,768]{1,0:T(8,128)(2,1)}, u32[]{:S(2)}) copy-start(bf16[272,768]{1,0:T(8,128)(2,1)} %get-tuple-element.39) | copy-start | bytes 1253380
  20.1 20.5 %copy-start.14 = (bf16[272,768]{1,0:T(8,128)(2,1)S(1)}, bf16[272,768]{1,0:T(8,128)(2,1)}, u32[]{:S(2)}) copy-start(bf16[272,768]{1,0:T(8,128)(2,1)} %get-tuple-element.40) | copy-start | bytes 1253380
  20.1 43.1 %all-to-all-start.1 = ((bf16[16,32,384]{2,1,0:T(8,128)(2,1)}), bf16[16,32,384]{2,1,0:T(8,128)(2,1)S(1)}, u32[]{:S(2)}, u32[]{:S(2)}) async-start(bf16[16,32,384]{2,1,0:T(8,128)(2,1)} %get-tuple-element.43), calls=%async_computation.1 | async-start | bytes 786432 | tf_op jit(solution)/shard_map/all_to_all | solution.py:343
  34.9 26.2 %collective-permute-start = (bf16[272,768]{1,0:T(8,128)(2,1)S(1)}, bf16[272,768]{1,0:T(8,128)(2,1)S(1)}, u32[]{:S(2)}, u32[]{:S(2)}) collective-permute-start(bf16[272,768]{1,0:T(8,128)(2,1)S(1)} %copy-done.16), channel_id=1, source_target_pairs={{0,1},{1,0},{2,3},{3,2},{4,5},{5,4},{6,7},{7,6},{8,9},{9,8},{10,11... | collective-permute-start | bytes 1253384 | tf_op jit(solution)/shard_map/ppermute | solution.py:51
  37.1 24.1 %collective-permute-start.1 = (bf16[272,768]{1,0:T(8,128)(2,1)S(1)}, bf16[272,768]{1,0:T(8,128)(2,1)S(1)}, u32[]{:S(2)}, u32[]{:S(2)}) collective-permute-start(bf16[272,768]{1,0:T(8,128)(2,1)S(1)} %copy-done.15), channel_id=1, source_target_pairs={{0,2},{1,3},{2,0},{3,1},{4,6},{5,7},{6,4},{7,5},{8,10},{9,11},{10,... | collective-permute-start | bytes 1253384 | tf_op jit(solution)/shard_map/ppermute | solution.py:51
  40.6 22.6 %collective-permute-start.2 = (bf16[272,768]{1,0:T(8,128)(2,1)S(1)}, bf16[272,768]{1,0:T(8,128)(2,1)S(1)}, u32[]{:S(2)}, u32[]{:S(2)}) collective-permute-start(bf16[272,768]{1,0:T(8,128)(2,1)S(1)} %copy-done.14), channel_id=1, source_target_pairs={{0,3},{1,2},{2,1},{3,0},{4,7},{5,6},{6,5},{7,4},{8,11},{9,10},{10,... | collective-permute-start | bytes 1253384 | tf_op jit(solution)/shard_map/ppermute | solution.py:51
  47.9 13.2 %collective-permute-start.3 = (bf16[32,256]{1,0:T(8,128)(2,1)S(1)}, bf16[32,256]{1,0:T(8,128)(2,1)S(1)}, u32[]{:S(2)}, u32[]{:S(2)}) collective-permute-start(bf16[32,256]{1,0:T(8,128)(2,1)S(1)} %select_reduce_fusion), channel_id=1, source_target_pairs={{0,4},{1,5},{2,6},{3,7},{4,0},{5,1},{6,2},{7,3},{8,12},{9,13},{10,... | collective-permute-start | bytes 49160 | tf_op jit(solution)/shard_map/ppermute | solution.py:51
  64.4 27.1 %all-to-all-start.2 = ((bf16[4,16,32,256]{3,2,1,0:T(8,128)(2,1)}), bf16[4,16,32,256]{3,2,1,0:T(8,128)(2,1)S(1)}, u32[]{:S(2)}, u32[]{:S(2)}) async-start(bf16[4,16,32,256]{3,2,1,0:T(8,128)(2,1)} %broadcast_in_dim.38), calls=%async_computation.2 | async-start | bytes 2097152 | tf_op jit(solution)/shard_map/all_to_all | solution.py:351
  70.8 17.1 %collective-permute-start.4 = (bf16[2,256,768]{2,1,0:T(8,128)(2,1)S(1)}, bf16[2,256,768]{2,1,0:T(8,128)(2,1)}, u32[]{:S(2)}, u32[]{:S(2)}) collective-permute-start(bf16[2,256,768]{2,1,0:T(8,128)(2,1)S(1)} %halo_kernel.1), channel_id=1, source_target_pairs={{0,128},{1,129},{2,130},{3,131},{4,132},{5,133},{6,134},{7,135},{8... | collective-permute-start | bytes 2359304 | tf_op jit(solution)/shard_map/ppermute | solution.py:353
  91.5 49.6 %collective-permute-start.5 = (bf16[2,256,768]{2,1,0:T(8,128)(2,1)}, bf16[2,256,768]{2,1,0:T(8,128)(2,1)}, u32[]{:S(2)}, u32[]{:S(2)}) collective-permute-start(bf16[2,256,768]{2,1,0:T(8,128)(2,1)} %collective-permute-done.4), channel_id=1, source_target_pairs={{128,320},{129,321},{130,322},{131,323},{132,324},{133,325},{134,3... | collective-permute-start | bytes 2359304 | tf_op jit(solution)/shard_map/ppermute | solution.py:355
  110.0 34.3 %all-to-all-start.3 = ((bf16[16,32,256]{2,1,0:T(8,128)(2,1)}), bf16[16,32,256]{2,1,0:T(8,128)(2,1)S(1)}, u32[]{:S(2)}, u32[]{:S(2)}) async-start(bf16[16,32,256]{2,1,0:T(8,128)(2,1)} %broadcast_in_dim.39), calls=%async_computation.3 | async-start | bytes 524288 | tf_op jit(solution)/shard_map/all_to_all | solution.py:357
  114.7 34.4 %copy-start.19 = (bf16[128,768]{1,0:T(8,128)(2,1)S(1)}, bf16[128,768]{1,0:T(8,128)(2,1)}, u32[]{:S(2)}) copy-start(bf16[128,768]{1,0:T(8,128)(2,1)} %get-tuple-element.62) | copy-start | bytes 589828
  114.7 36.3 %copy-start.18 = (bf16[128,768]{1,0:T(8,128)(2,1)S(1)}, bf16[128,768]{1,0:T(8,128)(2,1)}, u32[]{:S(2)}) copy-start(bf16[128,768]{1,0:T(8,128)(2,1)} %get-tuple-element.63) | copy-start | bytes 589828
  144.3 20.9 %copy-start.5 = (bf16[16,32,256]{2,1,0:T(8,128)(2,1)}, bf16[16,32,256]{2,1,0:T(8,128)(2,1)S(1)}, u32[]{:S(2)}) copy-start(bf16[16,32,256]{2,1,0:T(8,128)(2,1)S(1)} %all-to-all-done.3) | copy-start | bytes 786436
  144.3 49.0 %collective-permute-start.6 = (bf16[2,256,768]{2,1,0:T(8,128)(2,1)}, bf16[2,256,768]{2,1,0:T(8,128)(2,1)S(1)}, u32[]{:S(2)}, u32[]{:S(2)}) collective-permute-start(bf16[2,256,768]{2,1,0:T(8,128)(2,1)} %collective-permute-done.5), channel_id=1, source_target_pairs={{320,4},{321,5},{322,6},{323,7},{324,8},{325,9},{326,10},{327,11},... | collective-permute-start | bytes 2359304 | tf_op jit(solution)/shard_map/ppermute | solution.py:362
  149.0 12.6 %collective-permute-start.7 = (bf16[128,768]{1,0:T(8,128)(2,1)S(1)}, bf16[128,768]{1,0:T(8,128)(2,1)S(1)}, u32[]{:S(2)}, u32[]{:S(2)}) collective-permute-start(bf16[128,768]{1,0:T(8,128)(2,1)S(1)} %copy-done.19), channel_id=1, source_target_pairs={{0,1},{1,0},{2,3},{3,2},{4,5},{5,4},{6,7},{7,6},{8,9},{9,8},{10,11... | collective-permute-start | bytes 589832 | tf_op jit(solution)/shard_map/ppermute | solution.py:51
  151.0 25.1 %collective-permute-start.8 = (bf16[128,768]{1,0:T(8,128)(2,1)S(1)}, bf16[128,768]{1,0:T(8,128)(2,1)S(1)}, u32[]{:S(2)}, u32[]{:S(2)}) collective-permute-start(bf16[128,768]{1,0:T(8,128)(2,1)S(1)} %copy-done.18), channel_id=1, source_target_pairs={{0,2},{1,3},{2,0},{3,1},{4,6},{5,7},{6,4},{7,5},{8,10},{9,11},{10,... | collective-permute-start | bytes 589832 | tf_op jit(solution)/shard_map/ppermute | solution.py:51
  156.1 29.6 %collective-permute-start.12 = (bf16[512,256]{1,0:T(8,128)(2,1)S(1)}, bf16[512,256]{1,0:T(8,128)(2,1)S(1)}, u32[]{:S(2)}, u32[]{:S(2)}) collective-permute-start(bf16[512,256]{1,0:T(8,128)(2,1)S(1)} %bitcast.6), channel_id=1, source_target_pairs={{0,24},{1,25},{2,26},{3,27},{4,28},{5,29},{6,30},{7,31},{8,16},{9,... | collective-permute-start | bytes 786440 | tf_op jit(solution)/shard_map/ppermute | solution.py:51
  158.7 26.9 %collective-permute-start.11 = (bf16[512,256]{1,0:T(8,128)(2,1)S(1)}, bf16[512,256]{1,0:T(8,128)(2,1)S(1)}, u32[]{:S(2)}, u32[]{:S(2)}) collective-permute-start(bf16[512,256]{1,0:T(8,128)(2,1)S(1)} %bitcast.7), channel_id=1, source_target_pairs={{0,16},{1,17},{2,18},{3,19},{4,20},{5,21},{6,22},{7,23},{8,24},{9,... | collective-permute-start | bytes 786440 | tf_op jit(solution)/shard_map/ppermute | solution.py:51
  161.6 24.1 %collective-permute-start.10 = (bf16[512,256]{1,0:T(8,128)(2,1)S(1)}, bf16[512,256]{1,0:T(8,128)(2,1)S(1)}, u32[]{:S(2)}, u32[]{:S(2)}) collective-permute-start(bf16[512,256]{1,0:T(8,128)(2,1)S(1)} %bitcast.8), channel_id=1, source_target_pairs={{0,8},{1,9},{2,10},{3,11},{4,12},{5,13},{6,14},{7,15},{8,0},{9,1},... | collective-permute-start | bytes 786440 | tf_op jit(solution)/shard_map/ppermute | solution.py:51
  165.1 11.0 %copy-start.17 = (bf16[128,768]{1,0:T(8,128)(2,1)S(1)}, bf16[128,768]{1,0:T(8,128)(2,1)}, u32[]{:S(2)}) copy-start(bf16[128,768]{1,0:T(8,128)(2,1)} %get-tuple-element.64) | copy-start | bytes 589828
  165.1 35.7 %all-to-all-start.4 = ((bf16[16,32,256]{2,1,0:T(8,128)(2,1)}), bf16[16,32,256]{2,1,0:T(8,128)(2,1)S(1)}, u32[]{:S(2)}, u32[]{:S(2)}) async-start(bf16[16,32,256]{2,1,0:T(8,128)(2,1)} %far_kernel.1), calls=%async_computation.4 | async-start | bytes 524288 | tf_op jit(solution)/shard_map/all_to_all | solution.py:371
  176.1 9.6 %collective-permute-start.9 = (bf16[128,768]{1,0:T(8,128)(2,1)S(1)}, bf16[128,768]{1,0:T(8,128)(2,1)S(1)}, u32[]{:S(2)}, u32[]{:S(2)}) collective-permute-start(bf16[128,768]{1,0:T(8,128)(2,1)S(1)} %copy-done.17), channel_id=1, source_target_pairs={{0,3},{1,2},{2,1},{3,0},{4,7},{5,6},{6,5},{7,4},{8,11},{9,10},{10,... | collective-permute-start | bytes 589832 | tf_op jit(solution)/shard_map/ppermute | solution.py:51
  (13 other events, 53.3 us)
